TPU v7x, 32 devices: a whole 2x2x4 slice. The times are simulated.
32 devices in a mesh: dp: 8 (over z, x), tensor: 4 (over y, core).
Axes of the slice: x: 2, y: 2, z: 4, core: 2. Of those that a mesh axis runs over, the one named last changes fastest.
Arguments:
- tokens: bfloat16 [12288, 768], P('dp'), may hold values from -6 to 6
- grad_out: bfloat16 [12288, 768], P('dp'), may hold values from -8 to 8
- token_weight: float32 [12288], P('dp'), may hold values from 0.5 to 2
- lengths: int32 [24], P('dp'), may hold values from 1 to 512, 6144 in all
- step: int32 [1], replicated, may hold values from 2 to 20
- qkv_weight: bfloat16 [3, 768, 768], P(None, 'dp', 'tensor'), may hold values from -0.21875 to 0.21875
- out_weight: bfloat16 [768, 768], P('tensor', 'dp'), may hold values from -1.75 to 1.75
- up_weight: bfloat16 [768, 3072], P('dp', 'tensor'), may hold values from -0.21875 to 0.21875
- down_weight: bfloat16 [3072, 768], P('tensor', 'dp'), may hold values from -0.109375 to 0.109375
- norm_params: bfloat16 [4, 768], P(None, 'dp'), may hold values from 0.5 to 1.5
- first_qkv: float32 [3, 768, 768], P(None, 'dp', 'tensor'), may hold values from -32 to 32
- first_out: float32 [768, 768], P('tensor', 'dp'), may hold values from -4 to 4
- first_up: float32 [768, 3072], P('dp', 'tensor'), may hold values from -20 to 20
- first_down: float32 [3072, 768], P('tensor', 'dp'), may hold values from -40 to 40
- first_norm: float32 [4, 768], P(None, 'dp'), may hold values from -56 to 56
- second_qkv: float32 [3, 768, 768], P(None, 'dp', 'tensor'), may hold values from 143.21678 to 572.8671
- second_out: float32 [768, 768], P('tensor', 'dp'), may hold values from 2.2413425 to 8.951049
- second_up: float32 [768, 3072], P('dp', 'tensor'), may hold values from 57.01632 to 227.9424
- second_down: float32 [3072, 768], P('tensor', 'dp'), may hold values from 191.6928 to 768
- second_norm: float32 [4, 768], P(None, 'dp'), may hold values from 391.3728 to 1566.72
Outputs:
- output: bfloat16 [12288, 768], P('dp')
- grad_input: float32 [12288, 768], P('dp')
- new_qkv: float32 [3, 768, 768], P(None, 'dp', 'tensor')
- moment_qkv: float32 [3, 768, 768], P(None, 'dp', 'tensor')
- square_qkv: float32 [3, 768, 768], P(None, 'dp', 'tensor')
- copy_qkv: bfloat16 [3, 768, 768], P(None, 'dp', 'tensor')
- new_out: float32 [768, 768], P('tensor', 'dp')
- moment_out: float32 [768, 768], P('tensor', 'dp')
- square_out: float32 [768, 768], P('tensor', 'dp')
- copy_out: bfloat16 [768, 768], P('tensor', 'dp')
- new_up: float32 [768, 3072], P('dp', 'tensor')
- moment_up: float32 [768, 3072], P('dp', 'tensor')
- square_up: float32 [768, 3072], P('dp', 'tensor')
- copy_up: bfloat16 [768, 3072], P('dp', 'tensor')
- new_down: float32 [3072, 768], P('tensor', 'dp')
- moment_down: float32 [3072, 768], P('tensor', 'dp')
- square_down: float32 [3072, 768], P('tensor', 'dp')
- copy_down: bfloat16 [3072, 768], P('tensor', 'dp')
- new_norm: float32 [4, 768], P(None, 'dp')
- moment_norm: float32 [4, 768], P(None, 'dp')
- square_norm: float32 [4, 768], P(None, 'dp')
- copy_norm: bfloat16 [4, 768], P(None, 'dp')
Inputs may be any that keep to these rules, and one draw needn't show every extreme that they name: `lengths`: used tokens of each sequence; one sequence uses all 512 slots.
All inputs are finite; a program needn't handle non-finite values. No bound on the sum of `lengths` on one device may be relied on, other than what follows from the above.
Results may differ from a plain program's by a relative error of at most 0.014.
Values may be sent and summed in bfloat16 or wider, within the bound.
No kernel may reach another device: no remote copies, remote signals or barrier semaphores. Data moves between devices by JAX's collectives and lax.ppermute only.
A program may use at most 128 MiB of HBM per device.

v0:
```python
import jax
import jax.numpy as jnp
from jax import lax
from jax.sharding import PartitionSpec as P

HD = 64


NORM_EPS = 1e-05
BETA_ONE = 0.9
BETA_TWO = 0.95
ADAM_EPS = 1e-08
DECAY_RATE = 0.01
PEAK_RATE = 0.15
WARM_STEPS = 2.0
LAST_STEP = 40.0
MASK_VALUE = -1000000000.0


def exact_gelu(values):
    return jax.nn.gelu(values, approximate=False)


def norm_forward(summed, gain, shift):
    center = summed - jnp.mean(summed, axis=-1, keepdims=True)
    inverse = lax.rsqrt(jnp.mean(center * center, axis=-1, keepdims=True) + NORM_EPS)
    normed = center * inverse
    return (normed * gain + shift, normed, inverse)


def norm_backward(upstream, normed, inverse, gain):
    scaled = upstream * gain
    inner = (
        scaled
        - jnp.mean(scaled, axis=-1, keepdims=True)
        - normed * jnp.mean(scaled * normed, axis=-1, keepdims=True)
    )
    return (inner * inverse, jnp.sum(upstream * normed, axis=0), jnp.sum(upstream, axis=0))


def adamw_update(gradient, weight_low, first, second, rate, fix_one, fix_two, decay):
    weight = weight_low.astype(jnp.float32)
    first_new = BETA_ONE * first + (1.0 - BETA_ONE) * gradient
    second_new = BETA_TWO * second + (1.0 - BETA_TWO) * gradient * gradient
    direction = first_new / fix_one / (jnp.sqrt(second_new / fix_two) + ADAM_EPS)
    weight_new = weight - rate * (direction + decay * weight)
    return (weight_new, first_new, second_new, weight_new.astype(jnp.bfloat16))


def on_device(
    tokens,
    grad_out,
    token_weight,
    lengths,
    step,
    qkv_weight,
    out_weight,
    up_weight,
    down_weight,
    norm_params,
    first_qkv,
    first_out,
    first_up,
    first_down,
    first_norm,
    second_qkv,
    second_out,
    second_up,
    second_down,
    second_norm,
):
    qkv_full, out_full, up_full, down_full, norm_full = (
        lax.all_gather(qkv_weight, "dp", axis=1, tiled=True),
        lax.all_gather(out_weight, "dp", axis=1, tiled=True),
        lax.all_gather(up_weight, "dp", axis=0, tiled=True),
        lax.all_gather(down_weight, "dp", axis=1, tiled=True),
        lax.all_gather(norm_params, "dp", axis=1, tiled=True),
    )
    norm_float = norm_full.astype(jnp.float32)
    seq_count = lengths.shape[0]
    tok_count = tokens.shape[0]
    seq_len = tok_count // seq_count
    local_width = qkv_full.shape[2]
    local_heads = local_width // HD
    score_scale = HD ** (-0.5)
    tok_float = tokens.astype(jnp.float32)
    projected = jnp.einsum(
        "td,cde->cte", tokens, qkv_full, preferred_element_type=jnp.float32
    ).astype(jnp.bfloat16)
    split_heads = projected.reshape(3, seq_count, seq_len, local_heads, HD)
    queries, key_rows, value_rows = (split_heads[0], split_heads[1], split_heads[2])
    key_valid = jnp.arange(seq_len, dtype=jnp.int32)[None, :] < lengths[:, None]
    key_mask = key_valid[:, None, None, :]

    def attention_scores():
        raw_scores = jnp.einsum(
            "sqhe,skhe->shqk", queries, key_rows, preferred_element_type=jnp.float32
        )
        return jnp.where(key_mask, raw_scores * score_scale, MASK_VALUE)

    first_scores = attention_scores()
    log_total = jax.nn.logsumexp(first_scores, axis=-1, keepdims=True)
    probs_low = jnp.exp(first_scores - log_total).astype(jnp.bfloat16)
    context = jnp.einsum(
        "shqk,skhe->sqhe", probs_low, value_rows, preferred_element_type=jnp.float32
    )
    context_low = context.reshape(tok_count, local_width).astype(jnp.bfloat16)
    attn_part = jnp.dot(context_low, out_full, preferred_element_type=jnp.float32)
    attn_total = lax.psum(attn_part, "tensor")
    hidden_one, normed_one, inverse_one = norm_forward(
        tok_float + attn_total, norm_float[0], norm_float[1]
    )
    hidden_mine = hidden_one.astype(jnp.bfloat16)
    up_value = jnp.dot(hidden_mine, up_full, preferred_element_type=jnp.float32)
    gelu_value, gelu_pull = jax.vjp(exact_gelu, up_value)
    inner_low = gelu_value.astype(jnp.bfloat16)
    ffn_part = jnp.dot(inner_low, down_full, preferred_element_type=jnp.float32)
    ffn_total = lax.psum(ffn_part, "tensor")
    result, normed_two, inverse_two = norm_forward(
        hidden_one + ffn_total, norm_float[2], norm_float[3]
    )
    tok_valid = key_valid.reshape(tok_count).astype(jnp.float32)
    upstream = grad_out.astype(jnp.float32) * token_weight[:, None] * tok_valid[:, None]
    grad_two, gain_two, shift_two = norm_backward(upstream, normed_two, inverse_two, norm_float[2])
    ffn_mine = grad_two.astype(jnp.bfloat16)
    grad_down = jnp.einsum("tf,td->fd", inner_low, ffn_mine, preferred_element_type=jnp.float32)
    grad_inner = jnp.dot(ffn_mine, down_full.T, preferred_element_type=jnp.float32)
    up_low = gelu_pull(grad_inner)[0].astype(jnp.bfloat16)
    grad_up = jnp.einsum("td,tf->df", hidden_mine, up_low, preferred_element_type=jnp.float32)
    hidden_part = jnp.dot(up_low, up_full.T, preferred_element_type=jnp.float32)
    hidden_grad = grad_two + lax.psum(hidden_part, "tensor")
    grad_one, gain_one, shift_one = norm_backward(
        hidden_grad, normed_one, inverse_one, norm_float[0]
    )
    attn_mine = grad_one.astype(jnp.bfloat16)
    grad_outw = jnp.einsum("te,td->ed", context_low, attn_mine, preferred_element_type=jnp.float32)
    context_grad = jnp.dot(attn_mine, out_full.T, preferred_element_type=jnp.float32).astype(
        jnp.bfloat16
    )
    context_grad = context_grad.reshape(seq_count, seq_len, local_heads, HD)
    probs = jnp.exp(attention_scores() - log_total)
    probs_again = probs.astype(jnp.bfloat16)
    probs_grad = jnp.einsum(
        "sqhe,skhe->shqk", context_grad, value_rows, preferred_element_type=jnp.float32
    )
    value_grad = jnp.einsum(
        "shqk,sqhe->skhe", probs_again, context_grad, preferred_element_type=jnp.float32
    )
    score_grad = (
        probs * (probs_grad - jnp.sum(probs_grad * probs, axis=-1, keepdims=True)) * score_scale
    ).astype(jnp.bfloat16)
    query_grad = jnp.einsum(
        "shqk,skhe->sqhe", score_grad, key_rows, preferred_element_type=jnp.float32
    )
    key_grad = jnp.einsum(
        "shqk,sqhe->skhe", score_grad, queries, preferred_element_type=jnp.float32
    )
    proj_grad = (
        jnp.stack([query_grad, key_grad, value_grad])
        .astype(jnp.bfloat16)
        .reshape(3, tok_count, local_width)
    )
    grad_qkv = jnp.einsum("td,cte->cde", tokens, proj_grad, preferred_element_type=jnp.float32)
    input_part = jnp.einsum("cte,cde->td", proj_grad, qkv_full, preferred_element_type=jnp.float32)
    norm_partial = jnp.stack([gain_one, shift_one, gain_two, shift_two])
    result_low = result.astype(jnp.bfloat16)
    input_grad = grad_one + lax.psum(input_part, "tensor")
    shard_qkv, shard_out, shard_up, shard_down, shard_norm = (
        lax.psum_scatter(grad_qkv, "dp", scatter_dimension=1, tiled=True),
        lax.psum_scatter(grad_outw, "dp", scatter_dimension=1, tiled=True),
        lax.psum_scatter(grad_up, "dp", scatter_dimension=0, tiled=True),
        lax.psum_scatter(grad_down, "dp", scatter_dimension=1, tiled=True),
        lax.psum_scatter(norm_partial, "dp", scatter_dimension=1, tiled=True),
    )
    step_float = step[0].astype(jnp.float32)
    rate = PEAK_RATE * jnp.minimum(
        step_float / WARM_STEPS, (LAST_STEP - step_float) / (LAST_STEP - WARM_STEPS)
    )
    fix_one = 1.0 - BETA_ONE**step_float
    fix_two = 1.0 - BETA_TWO**step_float
    upd_qkv = adamw_update(
        shard_qkv, qkv_weight, first_qkv, second_qkv, rate, fix_one, fix_two, DECAY_RATE
    )
    upd_out = adamw_update(
        shard_out, out_weight, first_out, second_out, rate, fix_one, fix_two, DECAY_RATE
    )
    upd_up = adamw_update(
        shard_up, up_weight, first_up, second_up, rate, fix_one, fix_two, DECAY_RATE
    )
    upd_down = adamw_update(
        shard_down, down_weight, first_down, second_down, rate, fix_one, fix_two, DECAY_RATE
    )
    upd_norm = adamw_update(
        shard_norm, norm_params, first_norm, second_norm, rate, fix_one, fix_two, 0.0
    )
    return (
        result_low,
        input_grad,
        upd_qkv[0],
        upd_qkv[1],
        upd_qkv[2],
        upd_qkv[3],
        upd_out[0],
        upd_out[1],
        upd_out[2],
        upd_out[3],
        upd_up[0],
        upd_up[1],
        upd_up[2],
        upd_up[3],
        upd_down[0],
        upd_down[1],
        upd_down[2],
        upd_down[3],
        upd_norm[0],
        upd_norm[1],
        upd_norm[2],
        upd_norm[3],
    )


def solution(mesh):
    return jax.shard_map(
        on_device,
        mesh=mesh,
        in_specs=(
            P("dp", None),
            P("dp", None),
            P("dp"),
            P("dp"),
            P(),
            P(None, "dp", "tensor"),
            P("tensor", "dp"),
            P("dp", "tensor"),
            P("tensor", "dp"),
            P(None, "dp"),
            P(None, "dp", "tensor"),
            P("tensor", "dp"),
            P("dp", "tensor"),
            P("tensor", "dp"),
            P(None, "dp"),
            P(None, "dp", "tensor"),
            P("tensor", "dp"),
            P("dp", "tensor"),
            P("tensor", "dp"),
            P(None, "dp"),
        ),
        out_specs=(
            P("dp", None),
            P("dp", None),
            P(None, "dp", "tensor"),
            P(None, "dp", "tensor"),
            P(None, "dp", "tensor"),
            P(None, "dp", "tensor"),
            P("tensor", "dp"),
            P("tensor", "dp"),
            P("tensor", "dp"),
            P("tensor", "dp"),
            P("dp", "tensor"),
            P("dp", "tensor"),
            P("dp", "tensor"),
            P("dp", "tensor"),
            P("tensor", "dp"),
            P("tensor", "dp"),
            P("tensor", "dp"),
            P("tensor", "dp"),
            P(None, "dp"),
            P(None, "dp"),
            P(None, "dp"),
            P(None, "dp"),
        ),
        check_vma=False,
    )
```

profile of v0, /device:TPU:0, one launch (start us, length us, event | category | flops | bytes accessed | tf_op | source)
XLA Modules:
  0.0 819.0 jit_solution(9086663741849592017)
XLA Ops:
  9.8 38.8 %all_gather.15 = bf16[3,768,192]{2,0,1:T(4,128)(2,1)S(1)} all-gather(bf16[3,96,192]{2,0,1:T(4,128)(2,1)S(1)} %copy.117), channel_id=1, replica_groups=mesh['dp'=8,'tensor'=4] {'dp'}, dimensions={1}, use_global_device_ids=true | all-gather | bytes 995328 | tf_op jit(solution)/shard_map/all_gather | solution.py:73
  48.6 4.4 fusion.39
  54.1 2.4 fusion.2
  56.5 2.2 exponential_reduce_fusion
  60.6 5.3 fusion.58
  66.7 31.2 %all_gather.16 = bf16[192,768]{0,1:T(8,128)(2,1)S(1)} all-gather(bf16[192,96]{0,1:T(8,128)(2,1)S(1)} %copy.124), channel_id=1, replica_groups=mesh['dp'=8,'tensor'=4] {'dp'}, dimensions={1}, use_global_device_ids=true | all-gather | bytes 331776 | tf_op jit(solution)/shard_map/all_gather | solution.py:74
  97.9 3.0 fusion.127
  102.2 19.1 %all-gather = bf16[8,96,4]{1,2,0:T(4,128)(2,1)S(1)} all-gather(bf16[1,96,4]{1,2,0:T(4,128)(2,1)S(1)} %bitcast.84), channel_id=1, replica_groups=mesh['dp'=8,'tensor'=4] {'dp'}, dimensions={0}, use_global_device_ids=true | all-gather | bytes 6912 | tf_op jit(solution)/shard_map/all_gather | solution.py:77
  121.4 72.8 %all-reduce.5.cloned.1.call-done = f32[1536,768]{1,0:T(8,128)} async-done(((f32[1536,768]{1,0:T(8,128)}), f32[1536,768]{1,0:T(8,128)}) %all-reduce.5.cloned.1.call-update) | async-done | bytes 4718608 | tf_op jit(solution)/shard_map/psum | solution.py:109
  194.2 2.9 fusion.125
  200.4 14.3 %multiply_convert_fusion.1 = (bf16[1536,768]{1,0:T(8,128)(2,1)}, f32[1536,768]{1,0:T(8,128)}, f32[1536,768]{1,0:T(8,128)}) fusion(bf16[1536,768]{1,0:T(8,128)(2,1)S(1)} %fusion.38, bf16[768,768]{1,0:T(8,128)(2,1)} %all-gather.4.cloned.1.call-done), kind=kOutput, calls=%fused_computation.26 | convolution fusion | flops 1888616448 | bytes 15335424 | tf_op jit(solution)/shard_map/dot_general | solution.py:114
  214.7 6.3 fusion.128
  221.2 94.1 %all-reduce.7.cloned.1.call-done = f32[1536,768]{1,0:T(8,128)} async-done(((f32[1536,768]{1,0:T(8,128)}), f32[1536,768]{1,0:T(8,128)}) %all-reduce.7.cloned.1.call-update) | async-done | bytes 4718608 | tf_op jit(solution)/shard_map/psum | solution.py:118
  315.3 4.7 fusion.122
  321.6 2.9 multiply_reduce_fusion.1
  324.6 4.4 subtract_multiply_fusion.1
  329.1 3.3 add_convert_fusion
  333.9 4.3 fusion.129
  339.6 92.9 %all-reduce.9.cloned.1.call-done = f32[1536,768]{1,0:T(8,128)} async-done(((f32[1536,768]{1,0:T(8,128)}), f32[1536,768]{1,0:T(8,128)}) %all-reduce.9.cloned.1.call-update) | async-done | bytes 4718608 | tf_op jit(solution)/shard_map/psum | solution.py:131
  432.5 7.1 multiply_reduce_fusion.2
  439.6 3.3 subtract_multiply_fusion
  443.0 2.2 copy-done.1
  445.2 1.8 convolution_convert_fusion.1
  446.9 2.2 reshape.173
  449.1 7.2 fusion.59
  456.3 5.1 fusion.71
  461.4 1.9 convolution_bitcast_fusion.1
  466.1 18.4 %fusion.52 = bf16[3,512,3,64]{1,3,2,0:T(8,128)(2,1)} fusion(f32[3,3,512,512]{2,3,1,0:T(8,128)} %fusion.71, f32[3,3,512,512]{2,3,1,0:T(8,128)} %copy-done.2, f32[3,3,512]{2,1,0:T(4,128)S(1)} %copy-done.26, pred[3,512]{1,0:T(4,128)(4,1)S(1)} %get-tuple-element.155, bf16[3,512,3,64]{1,0,3,2:T(4,128)(2,1)} %copy-done.6), kind=kOutput, calls=%fused_computation.69 | convolution fusion | flops 328242176 | bytes 20073984 | tf_op jit(solution)/shard_map/shqk,sqhe->skhe/dot_general | solution.py:155
  484.5 18.3 %fusion.55 = bf16[3,512,3,64]{1,3,2,0:T(8,128)(2,1)} fusion(f32[3,3,512,512]{2,3,1,0:T(8,128)} %fusion.71, f32[3,3,512,512]{2,3,1,0:T(8,128)} %copy-done.2, f32[3,3,512]{2,1,0:T(4,128)S(1)} %copy-done.26, pred[3,512]{1,0:T(4,128)(4,1)S(1)} %get-tuple-element.155, bf16[3,512,3,64]{1,0,3,2:T(4,128)(2,1)} %copy-done.5), kind=kOutput, calls=%fused_computation.70 | convolution fusion | flops 328242176 | bytes 20073984 | tf_op jit(solution)/shard_map/shqk,skhe->sqhe/dot_general | solution.py:152
  504.2 2.3 stack.29
  506.4 2.5 copy.133
  508.9 2.5 stack.28
  511.4 2.5 copy.130
  513.9 2.5 stack.27
  520.0 5.6 convolution_bitcast_fusion
  525.8 6.5 fusion.62
  532.4 5.1 fusion.130
  537.6 5.0 fusion.43
  542.6 3.1 copy.149
  545.8 2.8 reshape.182
  553.4 39.2 %reduce-scatter.18.cloned.1.call-done = f32[96,192]{1,0:T(8,128)} async-done(((f32[768,192]{1,0:T(8,128)}), f32[96,192]{1,0:T(8,128)}) %reduce-scatter.18.cloned.1.call-update) | async-done | bytes 73744
  595.2 24.8 %all-reduce.11.cloned.1.call-done = f32[1536,768]{1,0:T(8,128)} async-done(((f32[1536,768]{1,0:T(8,128)}), f32[1536,768]{1,0:T(8,128)}) %all-reduce.11.cloned.1.call-update) | async-done | bytes 4718608 | tf_op jit(solution)/shard_map/psum | solution.py:167
  620.0 6.6 add.161
  626.6 38.0 %reduce-scatter.14.cloned.1.call-done = f32[768,96]{0,1:T(8,128)} async-done(((f32[768,768]{0,1:T(8,128)}), f32[768,96]{0,1:T(8,128)}) %reduce-scatter.14.cloned.1.call-update) | async-done | bytes 294928 | tf_op jit(solution)/shard_map/reduce_scatter | solution.py:172
  664.6 2.1 fusion.114
  666.7 70.0 %reduce-scatter.12.cloned.1.call-done = f32[96,768]{1,0:T(8,128)} async-done(((f32[768,768]{1,0:T(8,128)}), f32[96,768]{1,0:T(8,128)}) %reduce-scatter.12.cloned.1.call-update) | async-done | bytes 294928 | tf_op jit(solution)/shard_map/reduce_scatter | solution.py:171
  736.7 2.1 fusion.116
  738.7 67.9 %reduce-scatter.16.cloned.1.call-done = f32[96,576]{1,0:T(8,128)} async-done(((f32[768,576]{1,0:T(8,128)}), f32[96,576]{1,0:T(8,128)}) %reduce-scatter.16.cloned.1.call-update) | async-done | bytes 221200
  (156 shorter events, 34.4 us)
Async XLA Ops:
  8.0 186.1 %all-reduce.5.cloned.1.call-start = ((), (), s32[]{:S(2)}) async-start(), calls=%async_computation.5 | async-start | bytes 9437184 | tf_op jit(solution)/shard_map/psum | solution.py:109
  48.6 4.4 copy-start.12
  53.6 2.8 copy-start.6
  54.1 2.4 copy-start.5
  56.5 3.6 copy-start.2
  60.1 5.8 copy-start.25
  60.6 5.3 copy-start.7
  60.6 6.0 copy-start.21
  97.9 4.3 copy-start.28
  97.9 96.3 %copy-start.10 = (bf16[1536,768]{1,0:T(8,128)(2,1)S(1)}, bf16[1536,768]{1,0:T(8,128)(2,1)}, u32[]{:S(2)}) copy-start(bf16[1536,768]{1,0:T(8,128)(2,1)} %param.20) | copy-start | bytes 7077892
  100.9 99.4 %all-gather.4.cloned.1.call-start = ((), (), s32[]{:S(2)}) async-start(), calls=%async_computation.6 | async-start | bytes 1327104 | tf_op jit(solution)/shard_map/all_gather | solution.py:75
  101.5 113.1 %all-gather.6.cloned.1.call-start = ((), (), s32[]{:S(2)}) async-start(), calls=%async_computation.7 | async-start | bytes 1327104 | tf_op jit(solution)/shard_map/all_gather | solution.py:76
  102.1 213.2 %all-reduce.7.cloned.1.call-start = ((), (), s32[]{:S(2)}) async-start(), calls=%async_computation.8 | async-start | bytes 9437184 | tf_op jit(solution)/shard_map/psum | solution.py:118
  197.0 2.2 copy-start
  220.9 211.6 %all-reduce.9.cloned.1.call-start = ((), (), s32[]{:S(2)}) async-start(), calls=%async_computation.9 | async-start | bytes 9437184 | tf_op jit(solution)/shard_map/psum | solution.py:131
  319.9 1.7 copy-start.4
  321.6 7.4 slice-start.2
  321.6 7.4 slice-start.4
  324.5 4.5 copy-start.33
  324.6 4.5 slice-start.3
  324.6 4.5 slice-start.5
  329.0 3.4 copy-start.3
  329.1 4.8 copy-start.32
  338.2 213.6 %reduce-scatter.20.cloned.1.call-start = ((), (), s32[]{:S(2)}) async-start(), calls=%async_computation.15 | async-start | bytes 442368
  443.0 2.2 copy-start.1
  445.2 4.0 copy-start.26
  446.9 14.5 %slice-start = ((s8[4718592]{0:T(1024)(128)(4,1)}), s8[524288]{0:T(1024)(128)(4,1)S(1)}, s32[]{:S(2)}) async-start(s8[4718592]{0:T(1024)(128)(4,1)} %bitcast.73), calls=%async_computation.16 | async-start | bytes 1048576
  449.1 7.2 copy-start.8
  449.1 7.2 copy-start.9
  449.1 12.3 %slice-start.1 = ((s8[4718592]{0:T(1024)(128)(4,1)}), s8[4194304]{0:T(1024)(128)(4,1)S(1)}, s32[]{:S(2)}) async-start(s8[4718592]{0:T(1024)(128)(4,1)} %bitcast.73), calls=%async_computation.17 | async-start | bytes 8388608
  461.4 2.6 copy-start.27
  465.8 126.8 %reduce-scatter.18.cloned.1.call-start = ((), (), s32[]{:S(2)}) async-start(), calls=%async_computation.14 | async-start | bytes 884736
  484.5 18.3 %copy-start.16 = (bf16[3,512,3,64]{1,3,2,0:T(8,128)(2,1)S(1)}, bf16[3,512,3,64]{1,3,2,0:T(8,128)(2,1)}, u32[]{:S(2)}) copy-start(bf16[3,512,3,64]{1,3,2,0:T(8,128)(2,1)} %fusion.59) | copy-start | bytes 1769476
  516.4 103.6 %all-reduce.11.cloned.1.call-start = ((), (), s32[]{:S(2)}) async-start(), calls=%async_computation.10 | async-start | bytes 9437184 | tf_op jit(solution)/shard_map/psum | solution.py:167
  525.7 138.9 %reduce-scatter.14.cloned.1.call-start = ((), (), s32[]{:S(2)}) async-start(), calls=%async_computation.12 | async-start | bytes 2654208 | tf_op jit(solution)/shard_map/reduce_scatter | solution.py:172
  532.3 204.3 %reduce-scatter.12.cloned.1.call-start = ((), (), s32[]{:S(2)}) async-start(), calls=%async_computation.11 | async-start | bytes 2654208 | tf_op jit(solution)/shard_map/reduce_scatter | solution.py:171
  537.5 269.1 %reduce-scatter.16.cloned.1.call-start = ((), (), s32[]{:S(2)}) async-start(), calls=%async_computation.13 | async-start | bytes 2211840
  545.7 2.9 copy-start.15
  545.8 7.0 copy-start.29
  545.8 7.0 copy-start.30
  545.8 7.0 copy-start.31
  545.8 47.7 %copy-start.23 = (f32[192,96]{1,0:T(8,128)S(1)}, f32[192,96]{1,0:T(8,128)}, u32[]{:S(2)}) copy-start(f32[192,96]{1,0:T(8,128)} %param.36) | copy-start | bytes 221188
  595.2 69.4 %copy-start.13 = (bf16[768,96]{0,1:T(8,128)(2,1)S(1)}, bf16[768,96]{0,1:T(8,128)(2,1)}, u32[]{:S(2)}) copy-start(bf16[768,96]{0,1:T(8,128)(2,1)} %param.28) | copy-start | bytes 442372
  595.2 69.4 %copy-start.17 = (f32[768,96]{0,1:T(8,128)S(1)}, f32[768,96]{0,1:T(8,128)}, u32[]{:S(2)}) copy-start(f32[768,96]{0,1:T(8,128)} %param.38) | copy-start | bytes 884740
  595.2 69.4 %copy-start.18 = (f32[768,96]{0,1:T(8,128)S(1)}, f32[768,96]{0,1:T(8,128)}, u32[]{:S(2)}) copy-start(f32[768,96]{0,1:T(8,128)} %param.33) | copy-start | bytes 884740
  595.2 141.5 %copy-start.14 = (bf16[96,768]{1,0:T(8,128)(2,1)S(1)}, bf16[96,768]{1,0:T(8,128)(2,1)}, u32[]{:S(2)}) copy-start(bf16[96,768]{1,0:T(8,128)(2,1)} %param.27) | copy-start | bytes 442372
  595.2 141.5 %copy-start.19 = (f32[96,768]{1,0:T(8,128)S(1)}, f32[96,768]{1,0:T(8,128)}, u32[]{:S(2)}) copy-start(f32[96,768]{1,0:T(8,128)} %param.37) | copy-start | bytes 884740
  595.2 141.4 %copy-start.20 = (f32[96,768]{1,0:T(8,128)S(1)}, f32[96,768]{1,0:T(8,128)}, u32[]{:S(2)}) copy-start(f32[96,768]{1,0:T(8,128)} %param.32) | copy-start | bytes 884740
  (3 other events, 4.4 us)
Sparse Core Ops, SparseCore 0:
  101.1 93.0 all-reduce.4
  221.1 94.1 all-reduce.6
  338.3 94.1 all-reduce.8
  525.8 94.1 all-reduce.10
Sparse Core Ops, SparseCore 1:
  103.6 40.5 all-gather.3
  146.2 40.0 all-gather.5
  465.8 61.7 reduce-scatter.19
  530.9 61.6 reduce-scatter.17
  596.5 68.1 reduce-scatter.13
  668.6 68.1 reduce-scatter.11
  740.4 66.2 reduce-scatter.15
where the time goes:
time: 826 us; the launch traced here: 819 us
  waiting for transfers between devices  501 us (61%)
  matrix products  118 us (14%)
  blocking collectives  89.1 us (11%)
  local copies, waits for them, and re-layouts  48.1 us (6%)
  other arithmetic  44.7 us (5%)
  between operations  16.9 us (2%)
    unnamed x14, waiting for transfers between devices  108 us
    psum x1, waiting for transfers between devices, on_device(): ffn_total = lax.psum(ffn_part, 'tensor')  94.1 us
    psum x1, waiting for transfers between devices, on_device(): hidden_grad = grad_two + lax.psum(hidden_part, 'tensor')  92.9 us
    psum x1, waiting for transfers between devices, on_device(): attn_total = lax.psum(attn_part, 'tensor')  72.8 us
    reduce_scatter x1, waiting for transfers between devices, on_device(): lax.psum_scatter(grad_up, 'dp', scatter_dimension=0, tiled=True)  70 us
    all_gather x1, blocking collectives, on_device(): lax.all_gather(qkv_weight, 'dp', axis=1, tiled=True)  38.8 us
    reduce_scatter x1, waiting for transfers between devices, on_device(): lax.psum_scatter(grad_down, 'dp', scatter_dimension=1, tiled=True)  38 us
    all_gather x1, blocking collectives, on_device(): lax.all_gather(out_weight, 'dp', axis=1, tiled=True)  31.2 us
  transfers between devices with their start and end apart: 11, of which 8 were waited for; matrix products, arithmetic and copies ran while one was open for 14% of the time, Pallas kernels for 0%

commit v1 on v0

v1 whole, which is shorter than its diff:
```python
import jax
import jax.numpy as jnp
from jax import lax
from jax.sharding import PartitionSpec as P

HD = 64
NORM_EPS = 1e-05
BETA_ONE = 0.9
BETA_TWO = 0.95
ADAM_EPS = 1e-08
DECAY_RATE = 0.01
PEAK_RATE = 0.15
WARM_STEPS = 2.0
LAST_STEP = 40.0
MASK_VALUE = -1000000000.0
BF = jnp.bfloat16
F32 = jnp.float32
CHUNK = 256


def dot_nn(a, b):
    return lax.dot_general(a, b, (((1,), (0,)), ((), ())), preferred_element_type=F32)


def dot_nt(a, b):
    return lax.dot_general(a, b, (((1,), (1,)), ((), ())), preferred_element_type=F32)


def dot_tn(a, b):
    return lax.dot_general(a, b, (((0,), (0,)), ((), ())), preferred_element_type=F32)


def norm_stats(summed):
    center = summed - jnp.mean(summed, axis=-1, keepdims=True)
    inverse = lax.rsqrt(jnp.mean(center * center, axis=-1, keepdims=True) + NORM_EPS)
    return center * inverse, inverse


def norm_pull(upstream, normed, inverse, gain):
    scaled = upstream * gain
    return inverse * (
        scaled
        - jnp.mean(scaled, axis=-1, keepdims=True)
        - normed * jnp.mean(scaled * normed, axis=-1, keepdims=True)
    )


def adamw_update(gradient, weight_low, first, second, rate, fix_one, fix_two, decay):
    weight = weight_low.astype(F32)
    first_new = BETA_ONE * first + (1.0 - BETA_ONE) * gradient
    second_new = BETA_TWO * second + (1.0 - BETA_TWO) * gradient * gradient
    direction = first_new / fix_one / (jnp.sqrt(second_new / fix_two) + ADAM_EPS)
    weight_new = weight - rate * (direction + decay * weight)
    return (weight_new, first_new, second_new, weight_new.astype(BF))


def swap(x, axis, size, bit):
    return lax.ppermute(x, axis, [(i, i ^ bit) for i in range(size)])


def solution(mesh):
    dp_size = mesh.shape["dp"]
    t_size = mesh.shape["tensor"]

    def core_swap(x):
        return swap(x, "tensor", t_size, 1)

    def far_swap(x):
        return swap(x, "tensor", t_size, 2)

    def gather_dp(x):
        rows = x.shape[0]
        if dp_size != 8 or rows % 16:
            return lax.all_gather(x, "dp", axis=0, tiled=True)
        me = lax.axis_index("dp")
        deep = [x] + [swap(x, "dp", 8, k) for k in (2, 4, 6)]
        wide = swap(jnp.stack(deep), "dp", 8, 1)
        whole = jnp.stack([deep[0], wide[0], deep[1], wide[1], deep[2], wide[2], deep[3], wide[3]])
        order = jnp.bitwise_xor(jnp.arange(8, dtype=jnp.int32), me)
        return jnp.take(whole, order, axis=0).reshape(8 * rows, x.shape[1])

    def scatter_dp(x):
        if dp_size != 8 or (x.shape[0] // 8) % 16:
            return lax.psum_scatter(x, "dp", scatter_dimension=0, tiled=True)
        me = lax.axis_index("dp")
        blocks = x.reshape(4, 2, x.shape[0] // 8, x.shape[1])
        side, level = me % 2, me // 2
        there = lax.dynamic_index_in_dim(blocks, 1 - side, 1, keepdims=False).astype(BF)
        here = lax.dynamic_index_in_dim(blocks, side, 1, keepdims=False)
        here = here + swap(there, "dp", 8, 1).astype(F32)
        total = lax.dynamic_index_in_dim(here, level, 0, keepdims=False)
        for k in (1, 2, 3):
            piece = lax.dynamic_index_in_dim(here, jnp.bitwise_xor(level, k), 0, keepdims=False)
            total = total + swap(piece.astype(BF), "dp", 8, 2 * k).astype(F32)
        return total

    def on_device(
        tokens, grad_out, token_weight, lengths, step, qkv_weight, out_weight, up_weight, down_weight,
        norm_params, first_qkv, first_out, first_up, first_down, first_norm, second_qkv, second_out,
        second_up, second_down, second_norm,
    ):
        t_index = lax.axis_index("tensor")
        low, high = t_index % 2, t_index // 2
        seq_count = lengths.shape[0]
        tok_count, width = tokens.shape
        seq_len = tok_count // seq_count
        half = seq_len // 2
        rows_d = qkv_weight.shape[1]
        local = qkv_weight.shape[2]
        heads = local // HD
        score_scale = HD ** (-0.5)

        pack_q = jnp.concatenate(
            [qkv_weight[0], qkv_weight[1], qkv_weight[2], norm_params.T, jnp.zeros((rows_d, 60), BF)], axis=1
        )
        pack_u = jnp.concatenate([up_weight, out_weight.T], axis=1)
        q_mine = gather_dp(pack_q)
        u_mine = gather_dp(pack_u)
        d_mine = gather_dp(down_weight.T)
        norm_float = q_mine[:, 3 * local : 3 * local + 4].T.astype(F32)
        q_w = [q_mine, core_swap(q_mine)]
        u_w = [u_mine, core_swap(u_mine)]
        d_w = [d_mine, core_swap(d_mine)]
        o_here = jnp.concatenate([w[:, up_weight.shape[1] :] for w in u_w], axis=1)
        o_there = far_swap(o_here)
        o_low = jnp.where(high == 0, o_here, o_there)
        o_high = jnp.where(high == 0, o_there, o_here)
        u_w = [w[:, : up_weight.shape[1]] for w in u_w]

        def pick(x):
            whole = lax.dynamic_slice_in_dim(x, low * seq_len, seq_len, 0)
            part = lax.dynamic_slice_in_dim(x, 2 * seq_len + low * half, half, 0)
            return whole, part

        tok_a, tok_c = pick(tokens)
        tok_kv = tokens[2 * seq_len :]
        len_a = lax.dynamic_index_in_dim(lengths, low, 0, keepdims=False)
        len_c = lengths[2]
        mask_a = (jnp.arange(seq_len, dtype=jnp.int32) < len_a)[None, None, :]
        mask_c = (jnp.arange(seq_len, dtype=jnp.int32) < len_c)[None, None, :]
        valid_a = mask_a[0, 0].astype(F32)
        valid_c = lax.dynamic_slice_in_dim(mask_c[0, 0].astype(F32), low * half, half, 0)

        def attend(xq, xkv, mask):
            saved, outs = [], []
            for w in q_w:
                q = dot_nn(xq, w[:, :local]).astype(BF).reshape(-1, heads, HD)
                k = dot_nn(xkv, w[:, local : 2 * local]).astype(BF).reshape(-1, heads, HD)
                v = dot_nn(xkv, w[:, 2 * local : 3 * local]).astype(BF).reshape(-1, heads, HD)
                s = jnp.einsum("qhe,khe->hqk", q, k, preferred_element_type=F32) * score_scale
                s = jnp.where(mask, s, MASK_VALUE)
                lse = jax.nn.logsumexp(s, axis=-1, keepdims=True)
                p = jnp.exp(s - lse)
                ctx = jnp.einsum("hqk,khe->qhe", p.astype(BF), v, preferred_element_type=F32)
                outs.append(ctx.astype(BF).reshape(-1, local))
                saved.append((q, k, v, lse))
            return jnp.concatenate(outs, axis=1), saved

        ctx_a, saved_a = attend(tok_a, tok_a, mask_a)
        ctx_c, saved_c = attend(tok_c, tok_kv, mask_c)
        chunks = [(tok_a[:half], ctx_a[:half]), (tok_a[half:], ctx_a[half:]), (tok_c, ctx_c)]

        def forward(tok, ctx):
            ctx_there = far_swap(ctx)
            ctx_low = jnp.where(high == 0, ctx, ctx_there)
            ctx_high = jnp.where(high == 0, ctx_there, ctx)
            attn = dot_nt(ctx_low, o_low) + dot_nt(ctx_high, o_high)
            normed, inverse = norm_stats(tok.astype(F32) + attn)
            hidden = normed * norm_float[0] + norm_float[1]
            hidden_low = hidden.astype(BF)
            inner, slope, part = [], [], 0.0
            for u, d in zip(u_w, d_w):
                upv = dot_nn(hidden_low, u)
                cdf = 0.5 * (1.0 + lax.erf(upv * (0.5**0.5)))
                pdf = jnp.exp(-0.5 * upv * upv) * 0.3989422804014327
                inner.append((upv * cdf).astype(BF))
                slope.append(cdf + upv * pdf)
                part = part + dot_nt(inner[-1], d)
            return normed, inverse, hidden, hidden_low, inner, slope, part.astype(BF)

        fwd = [forward(*c) for c in chunks]
        go_a, go_c = pick(grad_out)
        tw_a, tw_c = pick(token_weight)
        scale = jnp.concatenate([tw_a * valid_a, tw_c * valid_c])
        go = jnp.concatenate([go_a, go_c])

        def middle(i, f):
            normed, inverse, hidden, hidden_low, inner, slope, part = f
            ffn = part.astype(F32) + far_swap(part).astype(F32)
            normed2, inverse2 = norm_stats(hidden + ffn)
            out = (normed2 * norm_float[2] + norm_float[3]).astype(BF)
            up = go[i * half : (i + 1) * half].astype(F32) * scale[i * half : (i + 1) * half, None]
            grad_two = norm_pull(up, normed2, inverse2, norm_float[2])
            sums = jnp.stack([jnp.sum(up * normed2, axis=0), jnp.sum(up, axis=0)])
            ffn_low = grad_two.astype(BF)
            up_low, back = [], 0.0
            for u, d, s in zip(u_w, d_w, slope):
                up_low.append((dot_nn(ffn_low, d) * s).astype(BF))
                back = back + dot_nt(up_low[-1], u)
            return out, grad_two, ffn_low, up_low, back.astype(BF), sums

        mid = [middle(i, f) for i, f in enumerate(fwd)]
        out_mine = jnp.concatenate([m[0] for m in mid])

        def whole_rows(mine, there):
            first = [mine[:seq_len], there[:seq_len], mine[seq_len:], there[seq_len:]]
            second = [there[:seq_len], mine[:seq_len], there[seq_len:], mine[seq_len:]]
            return jnp.where(low == 0, jnp.concatenate(first), jnp.concatenate(second))

        result = whole_rows(out_mine, core_swap(out_mine))

        hidden_low = jnp.concatenate([f[3] for f in fwd])
        ffn_low = jnp.concatenate([m[2] for m in mid])
        grads_u, grads_d = [], []
        for t in range(2):
            grads_u.append(dot_tn(hidden_low, jnp.concatenate([m[3][t] for m in mid])))
            grads_d.append(dot_tn(ffn_low, jnp.concatenate([f[4][t] for f in fwd])))

        def reduce_all(mine, there):
            return scatter_dp(mine + core_swap(there.astype(BF)).astype(F32))

        shard_up = reduce_all(grads_u[0], grads_u[1])
        shard_down = reduce_all(grads_d[0], grads_d[1]).T

        def first_norm_back(f, m):
            hidden_grad = m[1] + (m[4].astype(F32) + far_swap(m[4]).astype(F32))
            grad_one = norm_pull(hidden_grad, f[0], f[1], norm_float[0])
            sums = jnp.stack([jnp.sum(hidden_grad * f[0], axis=0), jnp.sum(hidden_grad, axis=0)])
            return grad_one, grad_one.astype(BF), sums

        back = [first_norm_back(f, m) for f, m in zip(fwd, mid)]

        def attend_back(attn_low, saved, mask):
            grads = []
            for t, (q, k, v, lse) in enumerate(saved):
                ctx_grad = dot_nn(attn_low, o_here[:, t * local : (t + 1) * local]).astype(BF).reshape(-1, heads, HD)
                s = jnp.einsum("qhe,khe->hqk", q, k, preferred_element_type=F32) * score_scale
                p = jnp.exp(jnp.where(mask, s, MASK_VALUE) - lse)
                dp = jnp.einsum("qhe,khe->hqk", ctx_grad, v, preferred_element_type=F32)
                dv = jnp.einsum("hqk,qhe->khe", p.astype(BF), ctx_grad, preferred_element_type=F32)
                ds = (p * (dp - jnp.sum(dp * p, axis=-1, keepdims=True)) * score_scale).astype(BF)
                dq = jnp.einsum("hqk,khe->qhe", ds, k, preferred_element_type=F32)
                dk = jnp.einsum("hqk,qhe->khe", ds, q, preferred_element_type=F32)
                grads.append(tuple(g.reshape(-1, local) for g in (dq, dk, dv)))
            return grads

        low_a = jnp.concatenate([back[0][1], back[1][1]])
        pg_a = [jnp.concatenate(g, axis=1).astype(BF) for g in attend_back(low_a, saved_a, mask_a)]
        pg_c = []
        for (dq, dk, dv) in attend_back(back[2][1], saved_c, mask_c):
            kv = jnp.concatenate([dk, dv], axis=1)
            mine = lax.dynamic_slice_in_dim(kv, low * half, half, 0)
            there = lax.dynamic_slice_in_dim(kv, (1 - low) * half, half, 0).astype(BF)
            pg_c.append((dq, mine, there))
        got = [core_swap(pg_c[1 - t][2]) for t in range(2)]
        pg_c = [jnp.concatenate([pg_c[t][0], pg_c[t][1] + got[t].astype(F32)], axis=1).astype(BF) for t in range(2)]
        pgs = [[pg_a[t][:half] for t in range(2)], [pg_a[t][half:] for t in range(2)], pg_c]
        gi = []
        for i in range(3):
            part = sum(dot_nt(pgs[i][t], q_w[t][:, : 3 * local]) for t in range(2)).astype(BF)
            gi.append(back[i][0] + (part.astype(F32) + far_swap(part).astype(F32)))
        gi = jnp.concatenate(gi)
        input_grad = whole_rows(gi, core_swap(gi))

        tok_mine = jnp.concatenate([tok_a, tok_c])
        low_mine = jnp.concatenate([b[1] for b in back])
        ctx_mine = jnp.concatenate([ctx_a, ctx_c])
        sum_one = back[0][2] + back[1][2] + back[2][2]
        sum_two = mid[0][5] + mid[1][5] + mid[2][5]
        norm_cols = jnp.concatenate([sum_one, sum_two]).astype(BF).astype(F32).T
        packs = []
        for t in range(2):
            gq = dot_tn(tok_mine, jnp.concatenate([pgs[0][t], pgs[1][t], pgs[2][t]]))
            go_t = dot_tn(low_mine, ctx_mine[:, t * local : (t + 1) * local])
            packs.append(jnp.concatenate([gq, go_t, norm_cols], axis=1))
        shard = reduce_all(packs[0], packs[1])
        shard_qkv = jnp.stack([shard[:, c * local : (c + 1) * local] for c in range(3)])
        shard_out = shard[:, 3 * local : 4 * local].T
        shard_norm = shard[:, 4 * local : 4 * local + 4].T

        step_float = step[0].astype(F32)
        rate = PEAK_RATE * jnp.minimum(step_float / WARM_STEPS, (LAST_STEP - step_float) / (LAST_STEP - WARM_STEPS))
        fix_one = 1.0 - BETA_ONE**step_float
        fix_two = 1.0 - BETA_TWO**step_float
        res = (result, input_grad)
        for g, w, m, v, decay in (
            (shard_qkv, qkv_weight, first_qkv, second_qkv, DECAY_RATE),
            (shard_out, out_weight, first_out, second_out, DECAY_RATE),
            (shard_up, up_weight, first_up, second_up, DECAY_RATE),
            (shard_down, down_weight, first_down, second_down, DECAY_RATE),
            (shard_norm, norm_params, first_norm, second_norm, 0.0),
        ):
            res = res + adamw_update(g, w, m, v, rate, fix_one, fix_two, decay)
        return res

    rows = P("dp", None)
    qkv, col, row, norm = P(None, "dp", "tensor"), P("tensor", "dp"), P("dp", "tensor"), P(None, "dp")
    params = (qkv, col, row, col, norm)
    return jax.shard_map(
        on_device,
        mesh=mesh,
        in_specs=(rows, rows, P("dp"), P("dp"), P()) + params * 3,
        out_specs=(rows, rows) + (qkv,) * 4 + (col,) * 4 + (row,) * 4 + (col,) * 4 + (norm,) * 4,
        check_vma=False,
    )
```

time: 826 us -> 452 us (0.55)
  waiting for transfers between devices: 501 us -> 90.3 us
  blocking collectives: 89.1 us -> 0 us
  matrix products: 118 us -> 173 us
  starting transfers between devices: 1.1 us -> 47.4 us
  local copies, waits for them, and re-layouts: 48.1 us -> 72.1 us
  other arithmetic: 44.7 us -> 61.9 us
  between operations: 16.9 us -> 4.22 us
    psum x4 -> x0, waiting for transfers between devices: 285 us -> none  [the longest x1 94.1 us: on_device(): ffn_total = lax.psum(ffn_part, 'tensor')]
    unnamed x14 -> x0, waiting for transfers between devices: 108 us -> none
    reduce_scatter x2 -> x0, waiting for transfers between devices: 108 us -> none  [the longest x1 70 us: on_device(): lax.psum_scatter(grad_up, 'dp', scatter_dimension=0, tiled=True)]
    ppermute x0 -> x47, waiting for transfers between devices: none -> 90.3 us  [swap(): return lax.ppermute(x, axis, [(i, i ^ bit) for i in range(size)])]
    all_gather x3 -> x0, blocking collectives: 89.1 us -> none  [the longest x1 38.8 us: on_device(): lax.all_gather(qkv_weight, 'dp', axis=1, tiled=True)]
    dot_general x17 -> x84, matrix products: 116 us -> 173 us  [the longest x24 44.4 us: dot_nt(): lax.dot_general(a, b, (((1,), (1,)), ((), ())), preferred_element_type=F32)]
    ppermute x0 -> x47, starting transfers between devices: none -> 47.4 us  [swap(): return lax.ppermute(x, axis, [(i, i ^ bit) for i in range(size)])]
    unnamed x99 -> x342, local copies, waits for them, and re-layouts: 28.3 us -> 44.9 us
  transfers between devices with their start and end apart: 11 -> 47, of which waited for: 8 -> 14; matrix products, arithmetic and copies ran while one was open for 14% -> 61% of each run, Pallas kernels for 0% -> 0%
where the time goes in v1:
time: 452 us; the launch traced here: 449 us
  matrix products  173 us (38%)
  waiting for transfers between devices  90.3 us (20%)
  local copies, waits for them, and re-layouts  72.1 us (16%)
  other arithmetic  61.9 us (14%)
  starting transfers between devices  47.4 us (10%)
    ppermute x47, waiting for transfers between devices, swap(): return lax.ppermute(x, axis, [(i, i ^ bit) for i in range(size)])  90.3 us
    ppermute x47, starting transfers between devices, swap(): return lax.ppermute(x, axis, [(i, i ^ bit) for i in range(size)])  47.4 us
    unnamed x342, local copies, waits for them, and re-layouts  44.9 us
    dot_general x24, matrix products, dot_nt(): lax.dot_general(a, b, (((1,), (1,)), ((), ())), preferred_element_type=F32)  44.4 us
    dot_general x28, matrix products, dot_nn(): lax.dot_general(a, b, (((1,), (0,)), ((), ())), preferred_element_type=F32)  37.8 us
    dot_general x4, matrix products, attend_back(): dk = jnp.einsum('hqk,qhe->khe', ds, q, preferred_element_type=F32)  26.7 us
    dot_general x4, matrix products, attend_back(): dq = jnp.einsum('hqk,khe->qhe', ds, k, preferred_element_type=F32)  25.1 us
    dot_general x8, matrix products, dot_tn(): lax.dot_general(a, b, (((0,), (0,)), ((), ())), preferred_element_type=F32)  13.4 us
  transfers between devices with their start and end apart: 47, of which 14 were waited for; matrix products, arithmetic and copies ran while one was open for 61% of the time, Pallas kernels for 0%

profile of v1, /device:TPU:0, one launch (start us, length us, event | category | flops | bytes accessed | tf_op | source)
XLA Modules:
  0.0 449.1 jit_solution(15966968418879146629)
XLA Ops:
  2.6 5.1 %collective-permute-start.2 = (bf16[96,640]{1,0:T(8,128)(2,1)S(1)}, bf16[96,640]{1,0:T(8,128)(2,1)S(1)}, u32[]{:S(2)}, u32[]{:S(2)}) collective-permute-start(bf16[96,640]{1,0:T(8,128)(2,1)S(1)} %concatenate.110), channel_id=1, source_target_pairs={{0,24},{4,28},{8,16},{12,20},{16,8},{20,12},{24,0},{28,4},{1,25},{... | collective-permute-start | bytes 368648 | tf_op jit(solution)/shard_map/ppermute | solution.py:58
  8.4 2.3 collective-permute-start.13
  35.8 2.9 collective-permute-start.6
  42.4 6.0 %collective-permute-done.6 = bf16[96,960]{1,0:T(8,128)(2,1)S(1)} collective-permute-done((bf16[96,960]{1,0:T(8,128)(2,1)}, bf16[96,960]{1,0:T(8,128)(2,1)S(1)}, u32[]{:S(2)}, u32[]{:S(2)}) %collective-permute-start.6) | collective-permute-done | bytes 184352 | tf_op jit(solution)/shard_map/ppermute | solution.py:58
  62.0 2.1 convolution_convert_fusion.19
  68.4 2.3 fusion.373
  92.1 3.2 gather_fusion.1
  124.3 2.8 convolution_convert_fusion.7
  129.4 9.9 %collective-permute-done.11 = bf16[768,384]{1,0:T(8,128)(2,1)S(1)} collective-permute-done((bf16[768,384]{1,0:T(8,128)(2,1)S(1)}, bf16[768,384]{1,0:T(8,128)(2,1)S(1)}, u32[]{:S(2)}, u32[]{:S(2)}) %collective-permute-start.11) | collective-permute-done | bytes 589856 | tf_op jit(solution)/shard_map/ppermute | solution.py:58
  141.7 5.2 %collective-permute-done.5 = bf16[256,384]{0,1:T(8,128)(2,1)S(1)} collective-permute-done((bf16[256,384]{0,1:T(8,128)(2,1)S(1)}, bf16[256,384]{0,1:T(8,128)(2,1)S(1)}, u32[]{:S(2)}, u32[]{:S(2)}) %collective-permute-start.5) | collective-permute-done | bytes 196640 | tf_op jit(solution)/shard_map/ppermute | solution.py:58
  155.5 14.5 %fusion.374 = f32[256,768]{1,0:T(8,128)S(1)} fusion(bf16[256,768]{1,0:T(8,128)(2,1)S(1)} %get-tuple-element.297, bf16[768,768]{1,0:T(8,128)(2,1)} %bitcast_select_fusion.1), kind=kOutput, calls=%fused_computation.636 | convolution fusion | flops 301989888 | bytes 2359296 | tf_op jit(solution)/shard_map/dot_general | solution.py:26
  176.1 6.4 %collective-permute-done.17 = bf16[256,768]{1,0:T(8,128)(2,1)S(1)} collective-permute-done((bf16[256,768]{1,0:T(8,128)(2,1)S(1)}, bf16[256,768]{1,0:T(8,128)(2,1)S(1)}, u32[]{:S(2)}, u32[]{:S(2)}) %collective-permute-start.17) | collective-permute-done | bytes 393248 | tf_op jit(solution)/shard_map/ppermute | solution.py:58
  191.2 6.4 %collective-permute-done.19 = bf16[256,768]{1,0:T(8,128)(2,1)S(1)} collective-permute-done((bf16[256,768]{1,0:T(8,128)(2,1)S(1)}, bf16[256,768]{1,0:T(8,128)(2,1)S(1)}, u32[]{:S(2)}, u32[]{:S(2)}) %collective-permute-start.19) | collective-permute-done | bytes 393248 | tf_op jit(solution)/shard_map/ppermute | solution.py:58
  207.3 2.1 fusion.55
  209.4 2.2 convolution_convert_fusion
  217.8 2.1 convolution_convert_fusion.1
  227.1 5.4 %collective-permute-done.27 = bf16[256,768]{1,0:T(8,128)(2,1)S(1)} collective-permute-done((bf16[256,768]{1,0:T(8,128)(2,1)S(1)}, bf16[256,768]{1,0:T(8,128)(2,1)S(1)}, u32[]{:S(2)}, u32[]{:S(2)}) %collective-permute-start.27) | collective-permute-done | bytes 393248 | tf_op jit(solution)/shard_map/ppermute | solution.py:58
  234.0 2.9 collective-permute-done.24
  238.3 2.2 fusion.360
  248.1 6.6 %fusion.102 = bf16[3,64,256]{2,1,0:T(8,128)(2,1)} fusion(bf16[512,3,64]{0,2,1:T(8,128)(2,1)} %bitcast.384, f32[3,256,512]{2,1,0:T(8,128)} %fusion.380, f32[3,256,512]{2,1,0:T(8,128)S(1)} %copy-done.4, f32[3,256]{1,0:T(4,128)S(1)} %copy-done.126), kind=kOutput, calls=%fused_computation.155 | convolution fusion | flops 53134592 | bytes 3443712 | tf_op jit(solution)/shard_map/hqk,khe->qhe/dot_general | solution.py:242
  254.7 6.8 %fusion.44 = f32[3,64,512]{2,1,0:T(8,128)} fusion(bf16[256,3,64]{0,2,1:T(8,128)(2,1)} %bitcast.392, f32[3,256,512]{2,1,0:T(8,128)} %fusion.380, f32[3,256,512]{2,1,0:T(8,128)S(1)} %copy-done.4, f32[3,256]{1,0:T(4,128)S(1)} %copy-done.126), kind=kOutput, calls=%fused_computation.52 | convolution fusion | flops 53085440 | bytes 3640320 | tf_op jit(solution)/shard_map/hqk,qhe->khe/dot_general | solution.py:243
  261.6 2.2 fusion.272
  268.4 2.3 fusion.378
  270.7 5.4 %fusion.90 = bf16[3,64,512]{2,1,0:T(8,128)(2,1)} fusion(bf16[512,3,64]{0,2,1:T(8,128)(2,1)} %bitcast.388, f32[3,512,512]{1,2,0:T(8,128)} %fusion.378, f32[3,512,512]{1,2,0:T(8,128)S(1)} %copy-done.6, f32[3,512]{1,0:T(4,128)S(1)} %copy-done.140, pred[512]{0:T(512)(128)(4,1)} %iota_compare_fusion.1), kind=kOutput, calls=%fused_computation.135 | convolution fusion | flops 109414400 | bytes 6691328 | tf_op jit(solution)/shard_map/hqk,khe->qhe/dot_general | solution.py:242
  276.1 7.4 %fusion.93 = bf16[3,64,512]{2,1,0:T(8,128)(2,1)} fusion(bf16[512,3,64]{0,2,1:T(8,128)(2,1)} %bitcast.386, f32[3,512,512]{1,2,0:T(8,128)} %fusion.378, f32[3,512,512]{1,2,0:T(8,128)} %copy-done.5, f32[3,512]{1,0:T(4,128)} %copy-done.139, pred[512]{0:T(512)(128)(4,1)} %iota_compare_fusion.1), kind=kOutput, calls=%fused_computation.136 | convolution fusion | flops 109414400 | bytes 6691328 | tf_op jit(solution)/shard_map/hqk,qhe->khe/dot_general | solution.py:243
  283.5 2.6 convolution_convert_fusion.5
  286.1 2.3 fusion.377
  288.3 5.6 %fusion.96 = bf16[3,64,512]{2,1,0:T(8,128)(2,1)} fusion(bf16[512,3,64]{0,2,1:T(8,128)(2,1)} %bitcast.360, f32[3,512,512]{1,2,0:T(8,128)} %fusion.377, f32[3,512,512]{1,2,0:T(8,128)S(1)} %copy-done.1, f32[3,512]{1,0:T(4,128)S(1)} %copy-done.138, pred[512]{0:T(512)(128)(4,1)} %iota_compare_fusion.1), kind=kOutput, calls=%fused_computation.137 | convolution fusion | flops 109414400 | bytes 6691328 | tf_op jit(solution)/shard_map/hqk,khe->qhe/dot_general | solution.py:242
  293.9 5.5 %fusion.99 = bf16[3,64,512]{2,1,0:T(8,128)(2,1)} fusion(bf16[512,3,64]{0,2,1:T(8,128)(2,1)} %bitcast.358, f32[3,512,512]{1,2,0:T(8,128)} %fusion.377, f32[3,512,512]{1,2,0:T(8,128)S(1)} %copy-done.1, f32[3,512]{1,0:T(4,128)S(1)} %copy-done.138, pred[512]{0:T(512)(128)(4,1)} %iota_compare_fusion.1), kind=kOutput, calls=%fused_computation.138 | convolution fusion | flops 109414400 | bytes 6691328 | tf_op jit(solution)/shard_map/hqk,qhe->khe/dot_general | solution.py:243
  300.6 2.6 fusion.187
  303.2 2.6 fusion.189
  306.6 7.0 %fusion.35 = f32[3,64,512]{2,1,0:T(8,128)S(1)} fusion(bf16[256,3,64]{0,2,1:T(8,128)(2,1)S(1)} %bitcast.390, f32[3,256,512]{2,1,0:T(8,128)} %fusion.379, f32[3,256,512]{2,1,0:T(8,128)} %copy-done.2, f32[3,256]{1,0:T(4,128)S(1)} %copy-done.124), kind=kOutput, calls=%fused_computation.49 | convolution fusion | flops 53085440 | bytes 3640320 | tf_op jit(solution)/shard_map/hqk,qhe->khe/dot_general | solution.py:243
  320.3 7.6 %fusion.105 = bf16[3,64,256]{2,1,0:T(8,128)(2,1)} fusion(bf16[512,3,64]{0,2,1:T(8,128)(2,1)S(1)} %bitcast.382, f32[3,256,512]{2,1,0:T(8,128)} %fusion.379, f32[3,256,512]{2,1,0:T(8,128)} %copy-done.2, f32[3,256]{1,0:T(4,128)S(1)} %copy-done.124), kind=kOutput, calls=%fused_computation.156 | convolution fusion | flops 53134592 | bytes 3443712 | tf_op jit(solution)/shard_map/hqk,khe->qhe/dot_general | solution.py:242
  337.5 10.4 %collective-permute-done.25 = bf16[256,768]{1,0:T(8,128)(2,1)S(1)} collective-permute-done((bf16[256,768]{1,0:T(8,128)(2,1)S(1)}, bf16[256,768]{1,0:T(8,128)(2,1)S(1)}, u32[]{:S(2)}, u32[]{:S(2)}) %collective-permute-start.25) | collective-permute-done | bytes 393248 | tf_op jit(solution)/shard_map/ppermute | solution.py:58
  349.9 8.8 %collective-permute-done.30 = bf16[256,768]{1,0:T(8,128)(2,1)S(1)} collective-permute-done((bf16[256,768]{1,0:T(8,128)(2,1)S(1)}, bf16[256,768]{1,0:T(8,128)(2,1)S(1)}, u32[]{:S(2)}, u32[]{:S(2)}) %collective-permute-start.30) | collective-permute-done | bytes 393248 | tf_op jit(solution)/shard_map/ppermute | solution.py:58
  361.2 2.6 convert_add_fusion.1
  365.1 2.4 convert_add_fusion
  373.6 6.6 %collective-permute-done.38 = bf16[4,96,768]{2,1,0:T(8,128)(2,1)S(1)} collective-permute-done((bf16[4,96,768]{2,1,0:T(8,128)(2,1)S(1)}, bf16[4,96,768]{2,1,0:T(8,128)(2,1)S(1)}, u32[]{:S(2)}, u32[]{:S(2)}) %collective-permute-start.38) | collective-permute-done | bytes 589856 | tf_op jit(solution)/shard_map/ppermute | solution.py:58
  385.1 2.2 copy.208
  388.7 3.2 collective-permute-done.43
  402.4 2.4 fusion.354
  404.8 3.6 collective-permute-done.33
  413.7 11.0 %collective-permute-done.45 = bf16[96,768]{1,0:T(8,128)(2,1)} collective-permute-done((bf16[96,768]{1,0:T(8,128)(2,1)}, bf16[96,768]{1,0:T(8,128)(2,1)}, u32[]{:S(2)}, u32[]{:S(2)}) %collective-permute-start.45) | collective-permute-done | bytes 147488 | tf_op jit(solution)/shard_map/ppermute | solution.py:58
  424.7 2.3 fusion.351
  427.1 4.2 collective-permute-done.35
  436.6 2.8 slice_dynamic-update-slice_fusion
  441.6 2.1 slice_dynamic-update-slice_fusion.2
  443.8 5.1 %broadcast_select_fusion = f32[1536,768]{1,0:T(8,128)} fusion(f32[1536,768]{1,0:T(8,128)} %get-tuple-element.238, f32[1536,768]{1,0:T(8,128)S(1)} %constant_dynamic-update-slice_fusion.21, pred[]{:T(512)S(6)} %eq.9), kind=kLoop, calls=%fused_computation.25 | loop fusion | flops 1179648 | bytes 14155777 | tf_op jit(solution)/shard_map/jit(_where)/select_n | solution.py:208
  (617 shorter events, 222.5 us)
Async XLA Ops:
  2.6 21.6 %collective-permute-start.2 = (bf16[96,640]{1,0:T(8,128)(2,1)S(1)}, bf16[96,640]{1,0:T(8,128)(2,1)S(1)}, u32[]{:S(2)}, u32[]{:S(2)}) collective-permute-start(bf16[96,640]{1,0:T(8,128)(2,1)S(1)} %concatenate.110), channel_id=1, source_target_pairs={{0,24},{4,28},{8,16},{12,20},{16,8},{20,12},{24,0},{28,4},{1,25},{... | collective-permute-start | bytes 368648 | tf_op jit(solution)/shard_map/ppermute | solution.py:58
  7.7 16.6 %collective-permute-start.1 = (bf16[96,640]{1,0:T(8,128)(2,1)S(1)}, bf16[96,640]{1,0:T(8,128)(2,1)}, u32[]{:S(2)}, u32[]{:S(2)}) collective-permute-start(bf16[96,640]{1,0:T(8,128)(2,1)S(1)} %concatenate.110), channel_id=1, source_target_pairs={{0,16},{4,20},{8,24},{12,28},{16,0},{20,4},{24,8},{28,12},{1,17},{... | collective-permute-start | bytes 368648 | tf_op jit(solution)/shard_map/ppermute | solution.py:58
  7.7 18.0 %collective-permute-start = (bf16[96,640]{1,0:T(8,128)(2,1)S(1)}, bf16[96,640]{1,0:T(8,128)(2,1)}, u32[]{:S(2)}, u32[]{:S(2)}) collective-permute-start(bf16[96,640]{1,0:T(8,128)(2,1)S(1)} %concatenate.110), channel_id=1, source_target_pairs={{0,8},{4,12},{8,0},{12,4},{16,24},{20,28},{24,16},{28,20},{1,9},{5... | collective-permute-start | bytes 368648 | tf_op jit(solution)/shard_map/ppermute | solution.py:58
  8.4 27.4 %collective-permute-start.13 = (bf16[96,768]{1,0:T(8,128)(2,1)}, bf16[96,768]{1,0:T(8,128)(2,1)S(1)}, u32[]{:S(2)}, u32[]{:S(2)}) collective-permute-start(bf16[96,768]{1,0:T(8,128)(2,1)} %bitcast.328), channel_id=1, source_target_pairs={{0,16},{4,20},{8,24},{12,28},{16,0},{20,4},{24,8},{28,12},{1,17},{... | collective-permute-start | bytes 442376 | tf_op jit(solution)/shard_map/ppermute | solution.py:58
  10.7 28.0 %collective-permute-start.12 = (bf16[96,768]{1,0:T(8,128)(2,1)}, bf16[96,768]{1,0:T(8,128)(2,1)}, u32[]{:S(2)}, u32[]{:S(2)}) collective-permute-start(bf16[96,768]{1,0:T(8,128)(2,1)} %bitcast.329), channel_id=1, source_target_pairs={{0,8},{4,12},{8,0},{12,4},{16,24},{20,28},{24,16},{28,20},{1,9},{5... | collective-permute-start | bytes 442376 | tf_op jit(solution)/shard_map/ppermute | solution.py:58
  24.2 15.8 %collective-permute-start.14 = (bf16[96,768]{1,0:T(8,128)(2,1)S(1)}, bf16[96,768]{1,0:T(8,128)(2,1)S(1)}, u32[]{:S(2)}, u32[]{:S(2)}) collective-permute-start(bf16[96,768]{1,0:T(8,128)(2,1)S(1)} %bitcast.330), channel_id=1, source_target_pairs={{0,24},{4,28},{8,16},{12,20},{16,8},{20,12},{24,0},{28,4},{1,25},{... | collective-permute-start | bytes 442376 | tf_op jit(solution)/shard_map/ppermute | solution.py:58
  24.9 17.5 %collective-permute-start.7 = (bf16[96,960]{1,0:T(8,128)(2,1)}, bf16[96,960]{1,0:T(8,128)(2,1)S(1)}, u32[]{:S(2)}, u32[]{:S(2)}) collective-permute-start(bf16[96,960]{1,0:T(8,128)(2,1)} %get-tuple-element.263), channel_id=1, source_target_pairs={{0,16},{4,20},{8,24},{12,28},{16,0},{20,4},{24,8},{28,12},{1,17},{... | collective-permute-start | bytes 552968 | tf_op jit(solution)/shard_map/ppermute | solution.py:58
  27.7 22.8 %collective-permute-start.3 = (bf16[4,96,640]{2,1,0:T(8,128)(2,1)}, bf16[4,96,640]{2,1,0:T(8,128)(2,1)S(1)}, u32[]{:S(2)}, u32[]{:S(2)}) collective-permute-start(bf16[4,96,640]{2,1,0:T(8,128)(2,1)} %pad_maximum_fusion.17), channel_id=1, source_target_pairs={{0,4},{4,0},{8,12},{12,8},{16,20},{20,16},{24,28},{28,24},{1,5},{5... | collective-permute-start | bytes 1474568 | tf_op jit(solution)/shard_map/ppermute | solution.py:58
  35.8 12.7 %collective-permute-start.6 = (bf16[96,960]{1,0:T(8,128)(2,1)}, bf16[96,960]{1,0:T(8,128)(2,1)S(1)}, u32[]{:S(2)}, u32[]{:S(2)}) collective-permute-start(bf16[96,960]{1,0:T(8,128)(2,1)} %get-tuple-element.263), channel_id=1, source_target_pairs={{0,8},{4,12},{8,0},{12,4},{16,24},{20,28},{24,16},{28,20},{1,9},{5... | collective-permute-start | bytes 552968 | tf_op jit(solution)/shard_map/ppermute | solution.py:58
  38.7 9.7 %collective-permute-start.8 = (bf16[96,960]{1,0:T(8,128)(2,1)}, bf16[96,960]{1,0:T(8,128)(2,1)S(1)}, u32[]{:S(2)}, u32[]{:S(2)}) collective-permute-start(bf16[96,960]{1,0:T(8,128)(2,1)} %get-tuple-element.263), channel_id=1, source_target_pairs={{0,24},{4,28},{8,16},{12,20},{16,8},{20,12},{24,0},{28,4},{1,25},{... | collective-permute-start | bytes 552968 | tf_op jit(solution)/shard_map/ppermute | solution.py:58
  41.9 28.8 %collective-permute-start.15 = (bf16[4,96,768]{2,1,0:T(8,128)(2,1)}, bf16[4,96,768]{2,1,0:T(8,128)(2,1)}, u32[]{:S(2)}, u32[]{:S(2)}) collective-permute-start(bf16[4,96,768]{2,1,0:T(8,128)(2,1)} %pad_maximum_fusion.12), channel_id=1, source_target_pairs={{0,4},{4,0},{8,12},{12,8},{16,20},{20,16},{24,28},{28,24},{1,5},{5... | collective-permute-start | bytes 1769480 | tf_op jit(solution)/shard_map/ppermute | solution.py:58
  49.5 34.2 %collective-permute-start.9 = (bf16[4,96,960]{2,1,0:T(8,128)(2,1)}, bf16[4,96,960]{2,1,0:T(8,128)(2,1)}, u32[]{:S(2)}, u32[]{:S(2)}) collective-permute-start(bf16[4,96,960]{2,1,0:T(8,128)(2,1)} %pad_maximum_fusion.7), channel_id=1, source_target_pairs={{0,4},{4,0},{8,12},{12,8},{16,20},{20,16},{24,28},{28,24},{1,5},{5... | collective-permute-start | bytes 2211848 | tf_op jit(solution)/shard_map/ppermute | solution.py:58
  64.1 34.9 %collective-permute-start.4 = (bf16[768,640]{0,1:T(8,128)(2,1)}, bf16[768,640]{0,1:T(8,128)(2,1)}, u32[]{:S(2)}, u32[]{:S(2)}) collective-permute-start(bf16[768,640]{0,1:T(8,128)(2,1)} %broadcast_select_fusion.2), channel_id=1, source_target_pairs={{0,1},{1,0},{2,3},{3,2},{4,5},{5,4},{6,7},{7,6},{8,9},{9,8},{10,11... | collective-permute-start | bytes 2949128 | tf_op jit(solution)/shard_map/ppermute | solution.py:58
  66.0 195.6 %copy-start.2 = (f32[3,256,512]{2,1,0:T(8,128)}, f32[3,256,512]{2,1,0:T(8,128)S(1)}, u32[]{:S(2)}) copy-start(f32[3,256,512]{2,1,0:T(8,128)S(1)} %get-tuple-element.285) | copy-start | bytes 4718596
  83.1 69.5 %collective-permute-start.16 = (bf16[768,768]{1,0:T(8,128)(2,1)}, bf16[768,768]{1,0:T(8,128)(2,1)}, u32[]{:S(2)}, u32[]{:S(2)}) collective-permute-start(bf16[768,768]{1,0:T(8,128)(2,1)} %bitcast_select_fusion.1), channel_id=1, source_target_pairs={{0,1},{1,0},{2,3},{3,2},{4,5},{5,4},{6,7},{7,6},{8,9},{9,8},{10,11... | collective-permute-start | bytes 3538952 | tf_op jit(solution)/shard_map/ppermute | solution.py:58
  98.9 19.2 %collective-permute-start.10 = (bf16[768,960]{0,1:T(8,128)(2,1)}, bf16[768,960]{0,1:T(8,128)(2,1)S(1)}, u32[]{:S(2)}, u32[]{:S(2)}) collective-permute-start(bf16[768,960]{0,1:T(8,128)(2,1)} %copy.198), channel_id=1, source_target_pairs={{0,1},{1,0},{2,3},{3,2},{4,5},{5,4},{6,7},{7,6},{8,9},{9,8},{10,11... | collective-permute-start | bytes 4423688 | tf_op jit(solution)/shard_map/ppermute | solution.py:58
  106.8 32.8 %collective-permute-start.20 = (bf16[256,384]{0,1:T(8,128)(2,1)}, bf16[256,384]{0,1:T(8,128)(2,1)}, u32[]{:S(2)}, u32[]{:S(2)}) collective-permute-start(bf16[256,384]{0,1:T(8,128)(2,1)} %pad_maximum_fusion.27), channel_id=1, source_target_pairs={{0,2},{1,3},{2,0},{3,1},{4,6},{5,7},{6,4},{7,5},{8,10},{9,11},{10,... | collective-permute-start | bytes 589832 | tf_op jit(solution)/shard_map/ppermute | solution.py:58
  123.0 16.2 %collective-permute-start.11 = (bf16[768,384]{1,0:T(8,128)(2,1)S(1)}, bf16[768,384]{1,0:T(8,128)(2,1)S(1)}, u32[]{:S(2)}, u32[]{:S(2)}) collective-permute-start(bf16[768,384]{1,0:T(8,128)(2,1)S(1)} %pad_maximum_fusion.11), channel_id=1, source_target_pairs={{0,2},{1,3},{2,0},{3,1},{4,6},{5,7},{6,4},{7,5},{8,10},{9,11},{10,... | collective-permute-start | bytes 1769480 | tf_op jit(solution)/shard_map/ppermute | solution.py:58
  127.2 46.7 %collective-permute-start.18 = (bf16[256,384]{0,1:T(8,128)(2,1)S(1)}, bf16[256,384]{0,1:T(8,128)(2,1)S(1)}, u32[]{:S(2)}, u32[]{:S(2)}) collective-permute-start(bf16[256,384]{0,1:T(8,128)(2,1)S(1)} %get-tuple-element.260), channel_id=1, source_target_pairs={{0,2},{1,3},{2,0},{3,1},{4,6},{5,7},{6,4},{7,5},{8,10},{9,11},{10,... | collective-permute-start | bytes 589832 | tf_op jit(solution)/shard_map/ppermute | solution.py:58
  128.8 18.2 %collective-permute-start.5 = (bf16[256,384]{0,1:T(8,128)(2,1)S(1)}, bf16[256,384]{0,1:T(8,128)(2,1)S(1)}, u32[]{:S(2)}, u32[]{:S(2)}) collective-permute-start(bf16[256,384]{0,1:T(8,128)(2,1)S(1)} %get-tuple-element.261), channel_id=1, source_target_pairs={{0,2},{1,3},{2,0},{3,1},{4,6},{5,7},{6,4},{7,5},{8,10},{9,11},{10,... | collective-permute-start | bytes 589832 | tf_op jit(solution)/shard_map/ppermute | solution.py:58
  154.4 21.7 %collective-permute-start.21 = (bf16[256,768]{1,0:T(8,128)(2,1)S(1)}, bf16[256,768]{1,0:T(8,128)(2,1)S(1)}, u32[]{:S(2)}, u32[]{:S(2)}) collective-permute-start(bf16[256,768]{1,0:T(8,128)(2,1)S(1)} %fusion.51), channel_id=1, source_target_pairs={{0,2},{1,3},{2,0},{3,1},{4,6},{5,7},{6,4},{7,5},{8,10},{9,11},{10,... | collective-permute-start | bytes 1179656 | tf_op jit(solution)/shard_map/ppermute | solution.py:58
  172.3 10.2 %collective-permute-start.17 = (bf16[256,768]{1,0:T(8,128)(2,1)S(1)}, bf16[256,768]{1,0:T(8,128)(2,1)S(1)}, u32[]{:S(2)}, u32[]{:S(2)}) collective-permute-start(bf16[256,768]{1,0:T(8,128)(2,1)S(1)} %fusion.49), channel_id=1, source_target_pairs={{0,2},{1,3},{2,0},{3,1},{4,6},{5,7},{6,4},{7,5},{8,10},{9,11},{10,... | collective-permute-start | bytes 1179656 | tf_op jit(solution)/shard_map/ppermute | solution.py:58
  188.4 9.3 %collective-permute-start.19 = (bf16[256,768]{1,0:T(8,128)(2,1)S(1)}, bf16[256,768]{1,0:T(8,128)(2,1)S(1)}, u32[]{:S(2)}, u32[]{:S(2)}) collective-permute-start(bf16[256,768]{1,0:T(8,128)(2,1)S(1)} %fusion.50), channel_id=1, source_target_pairs={{0,2},{1,3},{2,0},{3,1},{4,6},{5,7},{6,4},{7,5},{8,10},{9,11},{10,... | collective-permute-start | bytes 1179656 | tf_op jit(solution)/shard_map/ppermute | solution.py:58
  205.0 20.7 %collective-permute-start.23 = (bf16[256,768]{1,0:T(8,128)(2,1)S(1)}, bf16[256,768]{1,0:T(8,128)(2,1)S(1)}, u32[]{:S(2)}, u32[]{:S(2)}) collective-permute-start(bf16[256,768]{1,0:T(8,128)(2,1)S(1)} %fusion.54), channel_id=1, source_target_pairs={{0,2},{1,3},{2,0},{3,1},{4,6},{5,7},{6,4},{7,5},{8,10},{9,11},{10,... | collective-permute-start | bytes 1179656 | tf_op jit(solution)/shard_map/ppermute | solution.py:58
  220.4 12.1 %collective-permute-start.27 = (bf16[256,768]{1,0:T(8,128)(2,1)S(1)}, bf16[256,768]{1,0:T(8,128)(2,1)S(1)}, u32[]{:S(2)}, u32[]{:S(2)}) collective-permute-start(bf16[256,768]{1,0:T(8,128)(2,1)S(1)} %fusion.62), channel_id=1, source_target_pairs={{0,2},{1,3},{2,0},{3,1},{4,6},{5,7},{6,4},{7,5},{8,10},{9,11},{10,... | collective-permute-start | bytes 1179656 | tf_op jit(solution)/shard_map/ppermute | solution.py:58
  221.9 15.0 %collective-permute-start.24 = (bf16[256,768]{1,0:T(8,128)(2,1)S(1)}, bf16[256,768]{1,0:T(8,128)(2,1)S(1)}, u32[]{:S(2)}, u32[]{:S(2)}) collective-permute-start(bf16[256,768]{1,0:T(8,128)(2,1)S(1)} %fusion.57), channel_id=1, source_target_pairs={{0,2},{1,3},{2,0},{3,1},{4,6},{5,7},{6,4},{7,5},{8,10},{9,11},{10,... | collective-permute-start | bytes 1179656 | tf_op jit(solution)/shard_map/ppermute | solution.py:58
  223.6 137.0 %collective-permute-start.37 = (bf16[768,768]{1,0:T(8,128)(2,1)}, bf16[768,768]{1,0:T(8,128)(2,1)}, u32[]{:S(2)}, u32[]{:S(2)}) collective-permute-start(bf16[768,768]{1,0:T(8,128)(2,1)} %convolution_convert_fusion.1), channel_id=1, source_target_pairs={{0,1},{1,0},{2,3},{3,2},{4,5},{5,4},{6,7},{7,6},{8,9},{9,8},{10,11... | collective-permute-start | bytes 3538952 | tf_op jit(solution)/shard_map/ppermute | solution.py:58
  223.6 141.5 %collective-permute-start.42 = (bf16[768,768]{1,0:T(8,128)(2,1)}, bf16[768,768]{1,0:T(8,128)(2,1)}, u32[]{:S(2)}, u32[]{:S(2)}) collective-permute-start(bf16[768,768]{1,0:T(8,128)(2,1)} %convolution_convert_fusion), channel_id=1, source_target_pairs={{0,1},{1,0},{2,3},{3,2},{4,5},{5,4},{6,7},{7,6},{8,9},{9,8},{10,11... | collective-permute-start | bytes 3538952 | tf_op jit(solution)/shard_map/ppermute | solution.py:58
  306.6 21.3 %collective-permute-start.28 = (bf16[256,384]{0,1:T(8,128)(2,1)}, bf16[256,384]{0,1:T(8,128)(2,1)}, u32[]{:S(2)}, u32[]{:S(2)}) collective-permute-start(bf16[256,384]{0,1:T(8,128)(2,1)} %fusion.225), channel_id=1, source_target_pairs={{0,1},{1,0},{2,3},{3,2},{4,5},{5,4},{6,7},{7,6},{8,9},{9,8},{10,11... | collective-permute-start | bytes 589832 | tf_op jit(solution)/shard_map/ppermute | solution.py:58
  314.5 17.7 %collective-permute-start.29 = (bf16[256,384]{0,1:T(8,128)(2,1)}, bf16[256,384]{0,1:T(8,128)(2,1)}, u32[]{:S(2)}, u32[]{:S(2)}) collective-permute-start(bf16[256,384]{0,1:T(8,128)(2,1)} %fusion.227), channel_id=1, source_target_pairs={{0,1},{1,0},{2,3},{3,2},{4,5},{5,4},{6,7},{7,6},{8,9},{9,8},{10,11... | collective-permute-start | bytes 589832 | tf_op jit(solution)/shard_map/ppermute | solution.py:58
  316.1 53.4 %collective-permute-start.22 = (bf16[768,768]{1,0:T(8,128)(2,1)}, bf16[768,768]{1,0:T(8,128)(2,1)}, u32[]{:S(2)}, u32[]{:S(2)}) collective-permute-start(bf16[768,768]{1,0:T(8,128)(2,1)} %pad_maximum_fusion.2), channel_id=1, source_target_pairs={{0,1},{1,0},{2,3},{3,2},{4,5},{5,4},{6,7},{7,6},{8,9},{9,8},{10,11... | collective-permute-start | bytes 3538952 | tf_op jit(solution)/shard_map/ppermute | solution.py:58
  327.9 20.5 %collective-permute-start.26 = (bf16[256,768]{1,0:T(8,128)(2,1)S(1)}, bf16[256,768]{1,0:T(8,128)(2,1)S(1)}, u32[]{:S(2)}, u32[]{:S(2)}) collective-permute-start(bf16[256,768]{1,0:T(8,128)(2,1)S(1)} %fusion.59), channel_id=1, source_target_pairs={{0,2},{1,3},{2,0},{3,1},{4,6},{5,7},{6,4},{7,5},{8,10},{9,11},{10,... | collective-permute-start | bytes 1179656 | tf_op jit(solution)/shard_map/ppermute | solution.py:58
  332.1 15.8 %collective-permute-start.25 = (bf16[256,768]{1,0:T(8,128)(2,1)S(1)}, bf16[256,768]{1,0:T(8,128)(2,1)S(1)}, u32[]{:S(2)}, u32[]{:S(2)}) collective-permute-start(bf16[256,768]{1,0:T(8,128)(2,1)S(1)} %fusion.58), channel_id=1, source_target_pairs={{0,2},{1,3},{2,0},{3,1},{4,6},{5,7},{6,4},{7,5},{8,10},{9,11},{10,... | collective-permute-start | bytes 1179656 | tf_op jit(solution)/shard_map/ppermute | solution.py:58
  347.9 10.7 %collective-permute-start.30 = (bf16[256,768]{1,0:T(8,128)(2,1)S(1)}, bf16[256,768]{1,0:T(8,128)(2,1)S(1)}, u32[]{:S(2)}, u32[]{:S(2)}) collective-permute-start(bf16[256,768]{1,0:T(8,128)(2,1)S(1)} %fusion.63), channel_id=1, source_target_pairs={{0,2},{1,3},{2,0},{3,1},{4,6},{5,7},{6,4},{7,5},{8,10},{9,11},{10,... | collective-permute-start | bytes 1179656 | tf_op jit(solution)/shard_map/ppermute | solution.py:58
  348.5 35.6 %collective-permute-start.32 = (bf16[768,772]{0,1:T(8,128)(2,1)S(1)}, bf16[768,772]{0,1:T(8,128)(2,1)S(1)}, u32[]{:S(2)}, u32[]{:S(2)}) collective-permute-start(bf16[768,772]{0,1:T(8,128)(2,1)S(1)} %pad_maximum_fusion.1), channel_id=1, source_target_pairs={{0,1},{1,0},{2,3},{3,2},{4,5},{5,4},{6,7},{7,6},{8,9},{9,8},{10,11... | collective-permute-start | bytes 3557384 | tf_op jit(solution)/shard_map/ppermute | solution.py:58
  360.5 76.1 %collective-permute-start.31 = (f32[768,768]{1,0:T(8,128)}, f32[768,768]{1,0:T(8,128)}, u32[]{:S(2)}, u32[]{:S(2)}) collective-permute-start(f32[768,768]{1,0:T(8,128)} %pad_maximum_fusion), channel_id=1, source_target_pairs={{0,1},{1,0},{2,3},{3,2},{4,5},{5,4},{6,7},{7,6},{8,9},{9,8},{10,11... | collective-permute-start | bytes 7077896 | tf_op jit(solution)/shard_map/ppermute | solution.py:58
  364.0 16.3 %collective-permute-start.38 = (bf16[4,96,768]{2,1,0:T(8,128)(2,1)S(1)}, bf16[4,96,768]{2,1,0:T(8,128)(2,1)S(1)}, u32[]{:S(2)}, u32[]{:S(2)}) collective-permute-start(bf16[4,96,768]{2,1,0:T(8,128)(2,1)S(1)} %fusion.191), channel_id=1, source_target_pairs={{0,4},{4,0},{8,12},{12,8},{16,20},{20,16},{24,28},{28,24},{1,5},{5... | collective-permute-start | bytes 1769480 | tf_op jit(solution)/shard_map/ppermute | solution.py:58
  368.4 23.5 %collective-permute-start.43 = (bf16[4,96,768]{2,1,0:T(8,128)(2,1)}, bf16[4,96,768]{2,1,0:T(8,128)(2,1)}, u32[]{:S(2)}, u32[]{:S(2)}) collective-permute-start(bf16[4,96,768]{2,1,0:T(8,128)(2,1)} %fusion.192), channel_id=1, source_target_pairs={{0,4},{4,0},{8,12},{12,8},{16,20},{20,16},{24,28},{28,24},{1,5},{5... | collective-permute-start | bytes 1769480 | tf_op jit(solution)/shard_map/ppermute | solution.py:58
  381.3 17.5 %collective-permute-start.39 = (bf16[96,768]{1,0:T(8,128)(2,1)}, bf16[96,768]{1,0:T(8,128)(2,1)}, u32[]{:S(2)}, u32[]{:S(2)}) collective-permute-start(bf16[96,768]{1,0:T(8,128)(2,1)} %get-tuple-element.247), channel_id=1, source_target_pairs={{0,8},{4,12},{8,0},{12,4},{16,24},{20,28},{24,16},{28,20},{1,9},{5... | collective-permute-start | bytes 442376 | tf_op jit(solution)/shard_map/ppermute | solution.py:58
  382.5 17.1 %collective-permute-start.41 = (bf16[96,768]{1,0:T(8,128)(2,1)}, bf16[96,768]{1,0:T(8,128)(2,1)}, u32[]{:S(2)}, u32[]{:S(2)}) collective-permute-start(bf16[96,768]{1,0:T(8,128)(2,1)} %get-tuple-element.248), channel_id=1, source_target_pairs={{0,24},{4,28},{8,16},{12,20},{16,8},{20,12},{24,0},{28,4},{1,25},{... | collective-permute-start | bytes 442376 | tf_op jit(solution)/shard_map/ppermute | solution.py:58
  384.0 17.1 %collective-permute-start.40 = (bf16[96,768]{1,0:T(8,128)(2,1)}, bf16[96,768]{1,0:T(8,128)(2,1)}, u32[]{:S(2)}, u32[]{:S(2)}) collective-permute-start(bf16[96,768]{1,0:T(8,128)(2,1)} %get-tuple-element.249), channel_id=1, source_target_pairs={{0,16},{4,20},{8,24},{12,28},{16,0},{20,4},{24,8},{28,12},{1,17},{... | collective-permute-start | bytes 442376 | tf_op jit(solution)/shard_map/ppermute | solution.py:58
  391.9 16.5 %collective-permute-start.33 = (bf16[4,96,772]{2,1,0:T(8,128)(2,1)S(1)}, bf16[4,96,772]{2,1,0:T(8,128)(2,1)}, u32[]{:S(2)}, u32[]{:S(2)}) collective-permute-start(bf16[4,96,772]{2,1,0:T(8,128)(2,1)S(1)} %fusion.181), channel_id=1, source_target_pairs={{0,4},{4,0},{8,12},{12,8},{16,20},{20,16},{24,28},{28,24},{1,5},{5... | collective-permute-start | bytes 1778696 | tf_op jit(solution)/shard_map/ppermute | solution.py:58
  398.9 12.6 %collective-permute-start.44 = (bf16[96,768]{1,0:T(8,128)(2,1)}, bf16[96,768]{1,0:T(8,128)(2,1)}, u32[]{:S(2)}, u32[]{:S(2)}) collective-permute-start(bf16[96,768]{1,0:T(8,128)(2,1)} %get-tuple-element.244), channel_id=1, source_target_pairs={{0,8},{4,12},{8,0},{12,4},{16,24},{20,28},{24,16},{28,20},{1,9},{5... | collective-permute-start | bytes 442376 | tf_op jit(solution)/shard_map/ppermute | solution.py:58
  399.7 13.2 %collective-permute-start.46 = (bf16[96,768]{1,0:T(8,128)(2,1)}, bf16[96,768]{1,0:T(8,128)(2,1)}, u32[]{:S(2)}, u32[]{:S(2)}) collective-permute-start(bf16[96,768]{1,0:T(8,128)(2,1)} %get-tuple-element.245), channel_id=1, source_target_pairs={{0,24},{4,28},{8,16},{12,20},{16,8},{20,12},{24,0},{28,4},{1,25},{... | collective-permute-start | bytes 442376 | tf_op jit(solution)/shard_map/ppermute | solution.py:58
  401.2 23.6 %collective-permute-start.45 = (bf16[96,768]{1,0:T(8,128)(2,1)}, bf16[96,768]{1,0:T(8,128)(2,1)}, u32[]{:S(2)}, u32[]{:S(2)}) collective-permute-start(bf16[96,768]{1,0:T(8,128)(2,1)} %get-tuple-element.246), channel_id=1, source_target_pairs={{0,16},{4,20},{8,24},{12,28},{16,0},{20,4},{24,8},{28,12},{1,17},{... | collective-permute-start | bytes 442376 | tf_op jit(solution)/shard_map/ppermute | solution.py:58
  410.1 16.9 %collective-permute-start.34 = (bf16[96,772]{0,1:T(8,128)(2,1)S(1)}, bf16[96,772]{0,1:T(8,128)(2,1)S(1)}, u32[]{:S(2)}, u32[]{:S(2)}) collective-permute-start(bf16[96,772]{0,1:T(8,128)(2,1)S(1)} %get-tuple-element.241), channel_id=1, source_target_pairs={{0,8},{4,12},{8,0},{12,4},{16,24},{20,28},{24,16},{28,20},{1,9},{5... | collective-permute-start | bytes 444680 | tf_op jit(solution)/shard_map/ppermute | solution.py:58
  411.4 15.6 %collective-permute-start.36 = (bf16[96,772]{0,1:T(8,128)(2,1)S(1)}, bf16[96,772]{0,1:T(8,128)(2,1)S(1)}, u32[]{:S(2)}, u32[]{:S(2)}) collective-permute-start(bf16[96,772]{0,1:T(8,128)(2,1)S(1)} %get-tuple-element.242), channel_id=1, source_target_pairs={{0,24},{4,28},{8,16},{12,20},{16,8},{20,12},{24,0},{28,4},{1,25},{... | collective-permute-start | bytes 444680 | tf_op jit(solution)/shard_map/ppermute | solution.py:58
  412.9 18.4 %collective-permute-start.35 = (bf16[96,772]{0,1:T(8,128)(2,1)S(1)}, bf16[96,772]{0,1:T(8,128)(2,1)S(1)}, u32[]{:S(2)}, u32[]{:S(2)}) collective-permute-start(bf16[96,772]{0,1:T(8,128)(2,1)S(1)} %get-tuple-element.243), channel_id=1, source_target_pairs={{0,16},{4,20},{8,24},{12,28},{16,0},{20,4},{24,8},{28,12},{1,17},{... | collective-permute-start | bytes 444680 | tf_op jit(solution)/shard_map/ppermute | solution.py:58
  (150 other events, 940.2 us)

commit v2 on v1

v2 whole, which is shorter than its diff:
```python
import jax
import jax.numpy as jnp
from jax import lax
from jax.experimental import pallas as pl
from jax.experimental.pallas import tpu as pltpu
from jax.sharding import PartitionSpec as P

HD = 64
NORM_EPS = 1e-05
MASK_VALUE = -1000000000.0
BETA_ONE = 0.9
BETA_TWO = 0.95
ADAM_EPS = 1e-08
DECAY_RATE = 0.01
PEAK_RATE = 0.15
WARM_STEPS = 2.0
LAST_STEP = 40.0
BF = jnp.bfloat16
F32 = jnp.float32
VM = pltpu.VMEM
CHUNK = 256


def dot_nn(a, b):
    return lax.dot_general(a, b, (((1,), (0,)), ((), ())), preferred_element_type=F32)


def dot_nt(a, b):
    return lax.dot_general(a, b, (((1,), (1,)), ((), ())), preferred_element_type=F32)


def dot_tn(a, b):
    return lax.dot_general(a, b, (((0,), (0,)), ((), ())), preferred_element_type=F32)


def sds(shape, dtype=BF):
    return jax.ShapeDtypeStruct(shape, dtype)


class Order:
    def __init__(self):
        self.last = None

    def call(self, body, outs, ins, info, name, scratch=(), limit=20, raw_in=False, raw_out=False, deps=(), warm=(), free=False):
        ins = list(ins)
        n = len(ins) + 1
        specs = [pl.BlockSpec(memory_space=pltpu.SMEM)]
        specs += [pl.BlockSpec(memory_space=pltpu.HBM if raw_in else VM)] * len(ins)
        extra = list(warm) + list(deps) + ([] if self.last is None or free else [self.last])
        specs += [pl.BlockSpec(memory_space=VM)] * len(warm)
        specs += [pl.BlockSpec(memory_space=pl.ANY)] * (len(extra) - len(warm))

        def run(*refs):
            body(*refs[:n], *refs[n + len(extra) :])

        single = not isinstance(outs, (list, tuple))
        shapes = outs if single else list(outs)
        spec = pl.BlockSpec(memory_space=pltpu.HBM if raw_out else VM)
        res = pl.pallas_call(
            run,
            out_shape=shapes,
            in_specs=specs,
            out_specs=spec if single else [spec] * len(shapes),
            scratch_shapes=list(scratch),
            compiler_params=pltpu.CompilerParams(vmem_limit_bytes=limit * 1024 * 1024),
            cost_estimate=pl.CostEstimate(flops=1, bytes_accessed=1, transcendentals=0),
            name=name,
        )(info, *ins, *extra)
        if not free:
            self.last = res if single else res[-1]
        return res


def low_of(info):
    return lax.rem(info[0], 2)


def rows_of(kind):
    return 2 * CHUNK if kind == "a" else CHUNK


def first_row(info, kind, other=False):
    low = 1 - low_of(info) if other else low_of(info)
    return pl.multiple_of(2 * low * CHUNK if kind == "a" else (4 + low) * CHUNK, CHUNK)


def used_of(info, kind):
    return info[2 + low_of(info)] if kind == "a" else info[4]


def by_chunk(rows, step):
    if rows == CHUNK:
        step(0)
    else:

        @pl.loop(0, rows // CHUNK)
        def _(r):
            step(pl.multiple_of(r * CHUNK, CHUNK))


def norm_stats(summed):
    center = summed - jnp.mean(summed, axis=-1, keepdims=True)
    inverse = lax.rsqrt(jnp.mean(center * center, axis=-1, keepdims=True) + NORM_EPS)
    return center * inverse, inverse


def norm_pull(upstream, normed, inverse, gain):
    scaled = upstream * gain
    return inverse * (
        scaled
        - jnp.mean(scaled, axis=-1, keepdims=True)
        - normed * jnp.mean(scaled * normed, axis=-1, keepdims=True)
    )


def gelu_parts(u):
    cdf = 0.5 * (1.0 + lax.erf(u * (0.5**0.5)))
    pdf = jnp.exp(-0.5 * u * u) * 0.3989422804014327
    return u * cdf, cdf + u * pdf


def adamw_update(gradient, weight_low, first, second, rate, fix_one, fix_two, decay):
    weight = weight_low.astype(F32)
    first_new = BETA_ONE * first + (1.0 - BETA_ONE) * gradient
    second_new = BETA_TWO * second + (1.0 - BETA_TWO) * gradient * gradient
    direction = first_new / fix_one / (jnp.sqrt(second_new / fix_two) + ADAM_EPS)
    weight_new = weight - rate * (direction + decay * weight)
    return (weight_new, first_new, second_new, weight_new.astype(BF))


def pack(order, info, qkv, out):
    rows, local = qkv.shape[1], qkv.shape[2]

    def body(sc, *refs):
        given, (pq, po), (q, o, sems) = refs[:2], refs[2:4], refs[4:]
        copies = [pltpu.make_async_copy(a, b, sems.at[k]) for k, (a, b) in enumerate(zip(given, (q, o)))]
        for c in copies:
            c.start()
        for c in copies:
            c.wait()
        for c in range(3):
            pq[:, c * local : (c + 1) * local] = q[c]
        turned = jnp.transpose(o[...].astype(F32)).astype(BF)
        pq[:, 3 * local :] = turned
        po[...] = turned

    ins = [qkv, out]
    scratch = [VM(x.shape, x.dtype) for x in ins] + [pltpu.SemaphoreType.DMA((2,))]
    return order.call(body, [sds((rows, 4 * local)), sds((rows, local))], ins, info, "pack", scratch=scratch, raw_in=True)


def pack_more(order, info, up, out_there, norm, **kw):
    rows, units, local = up.shape[0], up.shape[1], out_there.shape[1]
    pad = -(units + local) % 128

    def body(sc, u, o, n, p):
        p[:, :units] = u[...]
        p[:, units : units + local] = o[...]
        cols = jnp.concatenate([n[...].astype(F32), jnp.zeros((124, rows), F32)], axis=0)
        p[:, units + local :] = jnp.transpose(cols)[:, :pad].astype(BF)

    return order.call(body, sds((rows, units + local + pad)), [up, out_there, norm], info, "pack_more", **kw)


def stack(order, info, blocks, name, **kw):
    height, width = blocks[0].shape
    count = len(blocks)

    def body(sc, *refs):
        for k in range(count):
            refs[count][k * height : (k + 1) * height, :] = refs[k][...]

    return order.call(body, sds((count * height, width)), blocks, info, name, **kw)


def place(order, info, blocks, marks, name, **kw):
    count = len(marks)
    height, width = sum(b.shape[0] for b in blocks) // count, blocks[0].shape[1]
    n = len(blocks)

    def body(sc, *refs):
        k = 0
        for ref in refs[:n]:
            for r in range(0, ref.shape[0], height):
                at = pl.ds(pl.multiple_of(jnp.bitwise_xor(sc[1], marks[k]) * height, 16), height)
                refs[n][at, :] = ref[r : r + height, :]
                k += 1

    return order.call(body, sds((count * height, width)), blocks, info, name, **kw)


def settle(order, info, u_own, u_oth, q_own, q_oth, units, local, **kw):
    width = u_own.shape[0]
    top = (units + local) // 128 * 128
    row = units + local - top

    def body(sc, a, b, c, d, norms, here, low, high):
        norms[...] = jnp.transpose(a[:, top:].astype(F32))[row : row + 8, :]
        first = sc[0] < 2
        for k, (x, y) in enumerate(((c, a), (d, b))):
            lanes = slice(k * local, (k + 1) * local)
            x, y = x[:, 3 * local :], y[:, units : units + local]
            here[:, lanes] = x
            low[:, lanes] = jnp.where(first, x, y)
            high[:, lanes] = jnp.where(first, y, x)

    outs = [sds((8, width), F32)] + [sds((width, 2 * local))] * 3
    return order.call(body, outs, [u_own, u_oth, q_own, q_oth], info, "settle", **kw)


def attend(order, info, kind, tokens, w_own, w_oth, local, name, **kw):
    heads = local // HD
    both = 2 * local
    kv_rows = 2 * CHUNK
    rows = rows_of(kind)

    def body(sc, x_ref, w0, w1, q_ref, k_ref, v_ref, lse_ref, ctx_ref, part_ref):
        keys = lax.broadcasted_iota(jnp.int32, (1, kv_rows), 1)
        bias = jnp.where(keys < used_of(sc, kind), 0.0, MASK_VALUE)
        for t, w in enumerate((w0, w1)):
            if kind == "c":
                q_ref[t] = (dot_nn(x_ref[pl.ds(first_row(sc, kind), rows), :], w[:, :local]) * 0.125).astype(BF)
                p = dot_nn(x_ref[2 * kv_rows :, :], w[:, local : 3 * local])
                k_ref[t] = p[:, :local].astype(BF)
                v_ref[t] = p[:, local:].astype(BF)
            else:
                p = dot_nn(x_ref[pl.ds(first_row(sc, kind), rows), :], w[:, : 3 * local])
                q_ref[t] = (p[:, :local] * 0.125).astype(BF)
                k_ref[t] = p[:, local : 2 * local].astype(BF)
                v_ref[t] = p[:, 2 * local :].astype(BF)

        @pl.loop(0, 2 * (rows // CHUNK))
        def _(i):
            t = lax.rem(i, 2)
            at = pl.ds(pl.multiple_of(lax.div(i, 2) * CHUNK, CHUNK), CHUNK)
            for h in range(heads):
                lanes = slice(h * HD, (h + 1) * HD)
                s = dot_nt(q_ref[t, at, lanes], k_ref[t, :, lanes]) + bias
                top = jnp.max(s, axis=-1, keepdims=True)
                e = jnp.exp(s - top)
                total = jnp.sum(e, axis=-1, keepdims=True)
                part_ref[t, at, lanes] = dot_nn((e * (1.0 / total)).astype(BF), v_ref[t, :, lanes]).astype(BF)
                lse_ref[t, at, h : h + 1] = top + jnp.log(total)

        for t in range(2):
            ctx_ref[:, t * local : (t + 1) * local] = part_ref[t]

    outs = [sds((2, n, local)) for n in (rows, kv_rows, kv_rows)] + [sds((2, rows, 128), F32), sds((rows, both))]
    return order.call(body, outs, [tokens, w_own, w_oth], info, name, scratch=[VM((2, rows, local), BF)], **kw)


def lift(order, info, kind, tokens, ctx, there, o_low, o_high, u0, u1, norms, units, name, **kw):
    rows, width = rows_of(kind), tokens.shape[1]
    both = 2 * units

    def body(sc, tok, c0, c1, ol, oh, u0, u1, nr, normed_ref, inv_ref, slope_ref, own_ref, send_ref):
        first = sc[0] < 2
        top = first_row(sc, kind)

        def step(r):
            at = pl.ds(r, CHUNK)
            a, b = c0[at, :], c1[at, :]
            attn = dot_nt(jnp.where(first, a, b), ol[...]) + dot_nt(jnp.where(first, b, a), oh[...])
            normed, inverse = norm_stats(tok[pl.ds(pl.multiple_of(top + r, CHUNK), CHUNK), :].astype(F32) + attn)
            normed_ref[at, :] = normed
            inv_ref[at, :] = jnp.broadcast_to(inverse, (CHUNK, 128))
            send_ref[at, :width] = (normed * nr[0:1, :] + nr[1:2, :]).astype(BF)
            for t, u in enumerate((u0, u1)):
                for c in range(0, units, 256):
                    g, s = gelu_parts(dot_nn(send_ref[at, :width], u[:, c : c + 256]))
                    slope_ref[at, t * units + c : t * units + c + 256] = s
                    if t == 0:
                        own_ref[at, c : c + 256] = g.astype(BF)
                    else:
                        send_ref[at, width + c : width + c + 256] = g.astype(BF)

        by_chunk(rows, step)

    outs = [sds((rows, width), F32), sds((rows, 128), F32), sds((rows, both), F32), sds((rows, units)), sds((rows, width + units))]
    return order.call(body, outs, [tokens, ctx, there, o_low, o_high, u0, u1, norms], info, name, **kw)


def drop(order, info, own, sent, d0, d1, name, **kw):
    rows, width = own.shape[0], d0.shape[0]

    def body(sc, own_ref, sent_ref, d0, d1, *parts):
        for k, part_ref in enumerate(parts):
            at = slice(k * CHUNK, (k + 1) * CHUNK)
            part_ref[...] = (dot_nt(own_ref[at, :], d0[...]) + dot_nt(sent_ref[at, width:], d1[...])).astype(BF)

    return order.call(body, [sds((CHUNK, width))] * (rows // CHUNK), [own, sent, d0, d1], info, name, **kw)


def row_scale(info, weights, kind, r):
    length = used_of(info, kind)
    first = r if kind == "a" else low_of(info) * CHUNK
    top = lax.div(first_row(info, kind) + r, 128)
    slot = lax.broadcasted_iota(jnp.int32, (128, 128), 0)
    lane = lax.broadcasted_iota(jnp.int32, (128, 128), 1)
    cols = []
    for k in range(CHUNK // 128):
        keep = (slot == lane) & (slot + (first + k * 128) < length)
        cols.append(jnp.sum(jnp.where(keep, weights[pl.ds(top + k, 1), :], 0.0), axis=-1, keepdims=True))
    return jnp.concatenate(cols, axis=0)


def turn(order, info, kind, normed, part, there, go, weights, norms, u0, u1, d0, d1, slope, name, below=None, **kw):
    rows, width = normed.shape
    n = len(part)
    skip = 0 if below is None else below.shape[0]
    units = d0.shape[1]
    both = 2 * units

    def body(sc, nm, g, sw, nr, u0, u1, d0, d1, sl, *refs):
        parts, refs = refs[: 2 * n], refs[2 * n :]
        if n > 1:
            p0, p1 = refs[-2:]
            refs = refs[:-2]
            for k in range(n):
                p0[k * CHUNK : (k + 1) * CHUNK, :] = parts[k][...]
                p1[k * CHUNK : (k + 1) * CHUNK, :] = parts[n + k][...]
        else:
            p0, p1 = parts
        out_ref, two_ref, own_ref, send_ref, sums_ref, part_ref = refs[-6:]
        if skip:
            out_ref[rows:, :] = refs[0][...]
        sums_ref[...] = jnp.zeros((8, width), F32)
        top = first_row(sc, kind)

        def step(r):
            at = pl.ds(r, CHUNK)
            ffn = p0[at, :].astype(F32) + p1[at, :].astype(F32)
            n2, inv2 = norm_stats((nm[at, :] * nr[0:1, :] + nr[1:2, :]) + ffn)
            out_ref[at, :] = (n2 * nr[2:3, :] + nr[3:4, :]).astype(BF)
            up = g[pl.ds(pl.multiple_of(top + r, CHUNK), CHUNK), :].astype(F32) * row_scale(sc, sw, kind, r)
            two = norm_pull(up, n2, inv2, nr[2:3, :])
            sums_ref[0:1, :] += jnp.sum(up * n2, axis=0, keepdims=True)
            sums_ref[1:2, :] += jnp.sum(up, axis=0, keepdims=True)
            two_ref[at, :] = two
            send_ref[at, :width] = two.astype(BF)
            acc = None
            for t, (u, d) in enumerate(((u0, d0), (u1, d1))):
                to = (own_ref, send_ref)[t]
                for c in range(0, units, 256):
                    lanes = slice(t * width + c, t * width + c + 256)
                    slope = sl[at, t * units + c : t * units + c + 256]
                    to[at, lanes] = (dot_nn(send_ref[at, :width], d[:, c : c + 256]) * slope).astype(BF)
                    piece = dot_nt(to[at, lanes], u[:, c : c + 256])
                    acc = piece if acc is None else acc + piece
            part_ref[at, :] = acc.astype(BF)

        by_chunk(rows, step)

    outs = [sds((rows + skip, width)), sds((rows, width), F32), sds((rows, units)), sds((rows, width + units))]
    outs += [sds((8, width), F32), sds((rows, width))]
    ins = [normed, go, weights, norms, u0, u1, d0, d1, slope, *part, *there] + ([] if below is None else [below])
    scratch = [VM((rows, width), BF)] * (2 if n > 1 else 0)
    return order.call(body, outs, ins, info, name, scratch=scratch, **kw)


def split_sides(info, whole, away, here):
    side = lax.rem(info[1], 2)
    height = whole.shape[0] // 8
    for z in range(4):
        rows = slice(z * height, (z + 1) * height)
        for out, s in ((away, 1 - side), (here, side)):
            out[rows, :] = whole[pl.ds(pl.multiple_of((2 * z + s) * height, 16), height), :].astype(out.dtype)


def grads(order, info, pairs, width, units, name, split=True, **kw):
    flat = [x for p in pairs for x in (p[0], p[2])]

    def body(sc, *refs):
        ins, outs = refs[: len(flat)], refs[len(flat) :]
        whole = outs[-1]

        @pl.loop(0, width // 256)
        def _(i):
            acc = None
            for k, (_, first, _, column) in enumerate(pairs):
                left = ins[2 * k][:, pl.ds(pl.multiple_of(first + i * 256, 256), 256)]
                piece = dot_tn(left, ins[2 * k + 1][:, column : column + units])
                acc = piece if acc is None else acc + piece
            whole[pl.ds(pl.multiple_of(i * 256, 256), 256), :] = acc

        if split:
            split_sides(sc, whole, outs[1], outs[0])

    if split:
        outs, scratch = [sds((width // 2, units), d) for d in (F32, BF)], [VM((width, units), F32)]
    else:
        outs, scratch = sds((width, units), F32), []
    return order.call(body, outs, flat, info, name, scratch=scratch, **kw)


def attend_back(order, info, kind, two, part, there, normed, inverse, norms, o_here, q, k, v, lse, weights, local, name, **kw):
    heads = local // HD
    rows, kv_rows = q.shape[1], k.shape[1]
    width = norms.shape[1]
    whole = kind == "a"

    def body(sc, two_ref, p0, p1, nm, inv, nr, o_ref, q_ref, k_ref, v_ref, lse_ref, *refs):
        if whole:
            w0, w1, one_ref, low_ref, pg0, pg1, sums_ref, part_ref, cg_ref, kv_ref, lt_ref, dq_ref = refs
        else:
            one_ref, low_ref, sums_ref, dq_ref, mine_ref, there_ref, cg_ref, kv_ref, lt_ref = refs
        low = low_of(sc)
        sums_ref[...] = jnp.zeros((8, width), F32)
        keys = lax.broadcasted_iota(jnp.int32, (kv_rows, 1), 0)
        bias = jnp.where(keys < used_of(sc, kind), 0.0, MASK_VALUE)
        if whole:
            kv_ref[...] = jnp.zeros((2, kv_rows, 2 * local), F32)

        def step(r):
            at = pl.ds(r, CHUNK)
            nrm = nm[at, :]
            grad = two_ref[at, :] + (p0[at, :].astype(F32) + p1[at, :].astype(F32))
            sums_ref[0:1, :] += jnp.sum(grad * nrm, axis=0, keepdims=True)
            sums_ref[1:2, :] += jnp.sum(grad, axis=0, keepdims=True)
            one = norm_pull(grad, nrm, inv[at, :1], nr[0:1, :])
            one_ref[at, :] = one
            low_ref[at, :] = one.astype(BF)
            for t in range(2):
                cg_ref[t] = dot_nn(low_ref[at, :], o_ref[:, t * local : (t + 1) * local]).astype(BF)
                lt_ref[t] = jnp.transpose(lse_ref[t, at, :])[:8, :]

            @pl.loop(0, 2)
            def _(t):
                for h in range(heads):
                    lanes = slice(h * HD, (h + 1) * HD)
                    qh, kh, cg = q_ref[t, at, lanes], k_ref[t, :, lanes], cg_ref[t, :, lanes]
                    p = jnp.exp(dot_nt(kh, qh) + bias - lt_ref[t, h : h + 1, :])
                    dp = dot_nt(v_ref[t, :, lanes], cg)
                    ds = (p * (dp - jnp.sum(dp * p, axis=0, keepdims=True))).astype(BF)
                    dv = dot_nn(p.astype(BF), cg)
                    dk = dot_nn(ds, qh)
                    dq_ref[t, at, lanes] = (dot_tn(ds, kh) * 0.125).astype(BF)
                    late = slice(local + h * HD, local + (h + 1) * HD)
                    if whole:
                        kv_ref[t, :, lanes] += dk
                        kv_ref[t, :, late] += dv
                    else:
                        kv_ref[t, :, lanes] = dk
                        kv_ref[t, :, late] = dv

        by_chunk(rows, step)
        if whole:
            for t, pg in enumerate((pg0, pg1)):
                pg[:, :local] = dq_ref[t]
                pg[:, local : 3 * local] = kv_ref[t].astype(BF)
            pg1[:, 3 * local :] = jnp.zeros((rows, -(3 * local) % 128), BF)

            def last(r):
                at = pl.ds(r, CHUNK)
                acc = dot_nt(pg0[at, :], w0[:, : 3 * local]) + dot_nt(pg1[at, : 3 * local], w1[:, : 3 * local])
                part_ref[at, :] = acc.astype(BF)

            by_chunk(rows, last)
        else:
            for t in range(2):
                mine_ref[t] = kv_ref[t, pl.ds(pl.multiple_of(low * CHUNK, CHUNK), CHUNK), :]
                there_ref[t] = kv_ref[t, pl.ds(pl.multiple_of((1 - low) * CHUNK, CHUNK), CHUNK), :].astype(BF)

    outs = [sds((rows, width), F32), sds((rows, width))]
    scratch = [VM((2, CHUNK, local), BF), VM((2, kv_rows, 2 * local), F32), VM((2, 8, CHUNK), F32)]
    if whole:
        outs += [sds((rows, 3 * local)), sds((rows, 3 * local + -(3 * local) % 128)), sds((8, width), F32), sds((rows, width))]
        scratch += [VM((2, rows, local), BF)]
    else:
        outs += [sds((8, width), F32), sds((2, rows, local)), sds((2, CHUNK, 2 * local), F32), sds((2, CHUNK, 2 * local))]
    ins = [two, part, there, normed, inverse, norms, o_here, q, k, v, lse] + (list(weights) if whole else [])
    return order.call(body, outs, ins, info, name, scratch=scratch, **kw)


def project_back(order, info, dq, mine, there, w_own, w_oth, out_oth, local, name, **kw):
    rows, width = dq.shape[1], w_own.shape[0]

    def body(sc, dq_ref, a, b, w0, w1, o, pg0, send_ref, part_ref, pg1):
        acc = None
        send_ref[:, local:] = o[...]
        for t, (w, pg) in enumerate(((w0, pg0), (w1, pg1))):
            pg[:, :local] = dq_ref[t]
            pg[:, local:] = (a[t] + b[1 - t].astype(F32)).astype(BF)
            piece = dot_nt(pg[...], w[:, : 3 * local])
            acc = piece if acc is None else acc + piece
        part_ref[...] = acc.astype(BF)
        for c in range(3):
            send_ref[c * rows : (c + 1) * rows, :local] = pg1[:, c * local : (c + 1) * local]

    outs = [sds((rows, 3 * local)), sds((3 * rows, local + out_oth.shape[1])), sds((rows, width))]
    scratch = [VM((rows, 3 * local), BF)]
    return order.call(body, outs, [dq, mine, there, w_own, w_oth, out_oth], info, name, scratch=scratch, **kw)


def grads_out(order, info, lows, ctxs, sums, local, **kw):
    width = lows[0].shape[1]
    n, s1, s2 = len(lows), len(sums[0]), len(sums[1])

    def body(sc, *refs):
        ls, cs = refs[:n], refs[n : 2 * n]
        ones, twos = refs[2 * n : 2 * n + s1], refs[2 * n + s1 : 2 * n + s1 + s2]
        *outs, cols_ref = refs[2 * n + s1 + s2 :]
        one = sum(x[0:2, :] for x in ones)
        two = sum(x[0:2, :] for x in twos)
        cols = jnp.concatenate([one, two, jnp.zeros((124, width), F32)], axis=0)
        cols_ref[...] = jnp.transpose(cols).astype(BF)

        @pl.loop(0, width // 256)
        def _(i):
            rr = pl.ds(pl.multiple_of(i * 256, 256), 256)
            for t, o in enumerate(outs):
                acc = None
                for x, y in zip(ls, cs):
                    piece = dot_tn(x[:, rr], y[:, t * local : (t + 1) * local])
                    acc = piece if acc is None else acc + piece
                o[rr, :local] = acc.astype(o.dtype)
                o[rr, local:] = cols_ref[rr, :].astype(o.dtype)

    ins = list(lows) + list(ctxs) + list(sums[0]) + list(sums[1])
    outs = [sds((width, local + 128), d) for d in (F32, BF)]
    return order.call(body, outs, ins, info, "grads_out", scratch=[VM((width, 128), BF)], **kw)


def grads_attn(order, info, tokens, mine, there, out_mine, split=True, **kw):
    width, local = tokens.shape[1], mine[0].shape[1] // 3
    full, cut = 4 * local + 128, 2 * local

    def body(sc, tok, ma, mc, ta, tc, om, *outs):
        whole = outs[-1]
        at = {k: pl.ds(first_row(sc, *k), rows_of(k[0])) for k in (("a", False), ("c", False), ("a", True), ("c", True))}
        pairs = [(at["a", False], ma), (at["c", False], mc), (at["a", True], ta)]

        @pl.loop(0, width // 256)
        def _(i):
            rr = pl.ds(pl.multiple_of(i * 256, 256), 256)
            acc = sum(dot_tn(tok[rows, rr], ref[:, : 3 * local]) for rows, ref in pairs)
            last = tok[at["c", True], rr]
            for c in range(3):
                lanes = slice(c * local, (c + 1) * local)
                whole[rr, lanes] = acc[:, lanes] + dot_tn(last, tc[c * CHUNK : (c + 1) * CHUNK, :local])
            whole[rr, 3 * local :] = om[rr, :] + tc[rr, local:].astype(F32)

        if split:
            here_1, away_1, here_2, away_2 = outs[:-1]
            split_sides(sc, whole.at[:, :cut], away_1, here_1)
            split_sides(sc, whole.at[:, cut:], away_2, here_2)

    ins = [tokens, *mine, *there, out_mine]
    if split:
        outs = [sds((width // 2, w), d) for w in (cut, full - cut) for d in (F32, BF)]
        scratch = [VM((width, full), F32)]
    else:
        outs, scratch = sds((width, full), F32), []
    return order.call(body, outs, ins, info, "grads_attn", scratch=scratch, **kw)


def fold_pair(order, info, mine, there, name, **kw):
    height, width = mine.shape[0] // 4, mine.shape[1]

    def body(sc, a, b, here, away):
        level = lax.shift_right_logical(sc[1], 1)
        for out, ks in ((away, (1, 3)), (here, (0, 2))):
            for i, k in enumerate(ks):
                at = pl.ds(pl.multiple_of(jnp.bitwise_xor(level, k) * height, 16), height)
                out[i * height : (i + 1) * height, :] = (a[at, :] + b[at, :].astype(F32)).astype(out.dtype)

    return order.call(body, [sds((2 * height, width), F32), sds((2 * height, width))], [mine, there], info, name, **kw)


def fold_last(order, info, mine, there, name, **kw):
    height, width = mine.shape[0] // 2, mine.shape[1]

    def body(sc, a, b, here, away):
        away[...] = (a[height:, :] + b[height:, :].astype(F32)).astype(BF)
        here[...] = a[:height, :] + b[:height, :].astype(F32)

    return order.call(body, [sds((height, width), F32), sds((height, width))], [mine, there], info, name, **kw)


def add_rows(order, info, groups, name, **kw):
    def body(sc, *refs):
        at = 0
        for k in range(len(groups)):
            a, b, c = refs[3 * k : 3 * k + 3]
            refs[-1][at : at + a.shape[0], :] = a[...] + (b[...].astype(F32) + c[...].astype(F32))
            at += a.shape[0]

    rows = sum(g[0].shape[0] for g in groups)
    return order.call(body, sds((rows, groups[0][0].shape[1]), F32), [x for g in groups for x in g], info, name, **kw)


def lay_rows(order, info, mine, there, name, **kw):
    pieces = []
    for g, arrays in enumerate((mine, there)):
        i = 0
        for n, x in enumerate(arrays):
            for r in range(0, x.shape[0], CHUNK):
                pieces.append((g, g * len(mine) + n, r, i))
                i += 1
    count, arrays = len(pieces), list(mine) + list(there)
    width = mine[0].shape[1]

    def body(sc, *refs):
        out, sems = refs[len(arrays)], refs[len(arrays) + 1]
        copies = []
        for k, (g, n, r, i) in enumerate(pieces):
            half = low_of(sc) if g == 0 else 1 - low_of(sc)
            row = (2 * half + i) * CHUNK if i < 2 else (4 + half) * CHUNK
            at = pl.ds(pl.multiple_of(row, CHUNK), CHUNK)
            copies.append(pltpu.make_async_copy(refs[n].at[r : r + CHUNK, :], out.at[at, :], sems.at[k]))
            copies[-1].start()
        for c in copies:
            c.wait()

    outs = sds((count * CHUNK, width), mine[0].dtype)
    return order.call(body, outs, arrays, info, name, scratch=[pltpu.SemaphoreType.DMA((count,))], raw_out=True, **kw)


def update(order, rates, groups, items, name, **kw):
    arrays = [x for it in items for x in it[:3]]
    shapes = [sds(it[0].shape, d) for it in items for d in (F32, F32, F32, BF)]
    pieces = [p for g in groups for p in g]

    def body(sc, *refs):
        ins = refs[len(pieces) : len(pieces) + len(arrays)]
        outs = refs[len(pieces) + len(arrays) :]
        rate, fix_one, fix_two = sc[0], sc[1], sc[2]
        for n, it in enumerate(items):
            w, m, v = ins[3 * n : 3 * n + 3]
            for index, group, first, count, turned in it[4]:
                lanes = slice(first, first + count)
                g = refs[2 * group][:, lanes] + refs[2 * group + 1][:, lanes].astype(F32)
                if turned:
                    g = jnp.transpose(g)[: w.shape[0], :]
                res = adamw_update(g, w[index], m[index], v[index], rate, fix_one, fix_two, it[3])
                for r, o in zip(res, outs[4 * n : 4 * n + 4]):
                    o[index] = r

    return order.call(body, shapes, pieces + arrays, rates, name, **kw)


def swap(x, axis, size, bit):
    return lax.ppermute(x, axis, [(i, i ^ bit) for i in range(size)])


def solution(mesh):
    dp_size = mesh.shape["dp"]
    t_size = mesh.shape["tensor"]

    def core_swap(x):
        return swap(x, "tensor", t_size, 1)

    def far_swap(x):
        return swap(x, "tensor", t_size, 2)

    def dp_swap(x, bit):
        return swap(x, "dp", dp_size, bit)

    def on_device(
        tokens, grad_out, token_weight, lengths, step, qkv_weight, out_weight, up_weight, down_weight,
        norm_params, first_qkv, first_out, first_up, first_down, first_norm, second_qkv, second_out,
        second_up, second_down, second_norm,
    ):
        order = Order()
        rows_d, local = qkv_weight.shape[1], qkv_weight.shape[2]
        units = up_weight.shape[1]
        tok_count = tokens.shape[0]
        direct = dp_size == 8 and rows_d % 16 == 0
        places = jnp.stack([lax.axis_index("tensor"), lax.axis_index("dp")]).astype(jnp.int32)
        info = jnp.concatenate([places, lengths])
        weights = token_weight.reshape(tok_count // 128, 128)
        step_float = step[0].astype(F32)
        rate = PEAK_RATE * jnp.minimum(step_float / WARM_STEPS, (LAST_STEP - step_float) / (LAST_STEP - WARM_STEPS))
        fix_one = 1.0 - BETA_ONE**step_float
        fix_two = 1.0 - BETA_TWO**step_float
        rates = jnp.stack([rate, fix_one, fix_two])
        down_t = down_weight.T

        slots = (0, 2, 4, 6, 1, 3, 5, 7)
        if direct:
            pack_q, pack_o = pack(order, info, qkv_weight, out_weight)
            q_x = dp_swap(pack_q, 1)
            q_z = [dp_swap(pack_q, k) for k in (2, 4, 6)]
            pack_u = pack_more(order, info, up_weight, far_swap(pack_o), norm_params, warm=[tokens])
            q_near = stack(order, info, q_z, "stack_q", deps=[q_x])
            q_far = dp_swap(q_near, 1)
            u_four = stack(order, info, [pack_u] + [dp_swap(pack_u, k) for k in (2, 4, 6)], "stack_u")
            u_x = dp_swap(u_four, 1)
            q_own = place(order, info, [pack_q, q_near, q_x, q_far], slots, "place_q")
            q_oth = core_swap(q_own)
            d_one = dp_swap(down_t, 4)
        else:
            pad = jnp.zeros((rows_d, -(units + local) % 128 - 4), BF)
            pack_q = jnp.concatenate([qkv_weight[0], qkv_weight[1], qkv_weight[2], out_weight.T], axis=1)
            pack_u = jnp.concatenate([up_weight, far_swap(out_weight.T), norm_params.T, pad], axis=1)
            q_own, u_own, d_own = (lax.all_gather(x, "dp", axis=0, tiled=True) for x in (pack_q, pack_u, down_t))
            q_oth = core_swap(q_own)

        q_a, k_a, v_a, lse_a, ctx_a = attend(order, info, "a", tokens, q_own, q_oth, local, "attend_a")
        ctx_a_there = far_swap(ctx_a)
        if direct:
            d_two = stack(order, info, [down_t, d_one], "stack_d")
            d_z = dp_swap(d_two, 2)
        q_c, k_c, v_c, lse_c, ctx_c = attend(order, info, "c", tokens, q_own, q_oth, local, "attend_c")
        ctx_c_there = far_swap(ctx_c)
        if direct:
            d_four = stack(order, info, [d_two, d_z], "stack_d4")
            d_x = dp_swap(d_four, 1)
            u_own = place(order, info, [u_four, u_x], slots, "place_u", deps=[ctx_a_there])
        u_oth = core_swap(u_own)
        norms, o_here, o_low, o_high = settle(order, info, u_own, u_oth, q_own, q_oth, units, local)
        args = (o_low, o_high, u_own, u_oth, norms, units)
        normed_a, inv_a, slope_a, inner_a, sent_a = lift(order, info, "a", tokens, ctx_a, ctx_a_there, *args, "lift_a")
        if direct:
            d_own = place(order, info, [d_four, d_x], (0, 4, 2, 6, 1, 5, 3, 7), "place_d", warm=[grad_out, weights], deps=[ctx_c_there])
        d_oth = core_swap(d_own)
        normed_c, inv_c, slope_c, inner_c, sent_c = lift(order, info, "c", tokens, ctx_c, ctx_c_there, *args, "lift_c")
        part_c = drop(order, info, inner_c, sent_c, d_own, d_oth, "drop_c")
        part_c_there = [far_swap(p) for p in part_c]
        part_a = drop(order, info, inner_a, sent_a, d_own, d_oth, "drop_a")
        part_a_there = [far_swap(p) for p in part_a]
        got_hi_a, got_hi_c = core_swap(sent_a), core_swap(sent_c)
        args = (grad_out, weights, norms, u_own, u_oth, d_own, d_oth)
        res_c, two_c, up_c, fu_c, sums_c2, back_c = turn(
            order, info, "c", normed_c, part_c, part_c_there, *args, slope_c, "turn_c", deps=[got_hi_a, got_hi_c])
        result, two_a, up_a, fu_a, sums_a2, back_a = turn(
            order, info, "a", normed_a, part_a, part_a_there, *args, slope_a, "turn_a", below=res_c)
        back_a_there = far_swap(back_a)
        back_c_there = far_swap(back_c)
        got_fu_a, got_fu_c = core_swap(fu_a), core_swap(fu_c)
        width = tokens.shape[1]
        pairs = [(fu_a, 0, inner_a, 0), (fu_c, 0, inner_c, 0), (got_fu_a, 0, got_hi_a, width), (got_fu_c, 0, got_hi_c, width)]
        grad_d = grads(order, info, pairs, width, units, "grads_d", split=direct)
        pairs = [(sent_a, 0, up_a, 0), (sent_c, 0, up_c, 0), (got_hi_a, 0, got_fu_a, width), (got_hi_c, 0, got_fu_c, width)]
        grad_u = grads(order, info, pairs, width, units, "grads_u", split=direct)
        res_there = core_swap(result)

        def second_fold(parts, name, **kw):
            here, away = fold_pair(order, info, *parts, "pair_" + name, **kw)
            return here, dp_swap(away, 2)

        def third_fold(pair, name, **kw):
            here, away = fold_last(order, info, *pair, "last_" + name, **kw)
            return here, dp_swap(away, 4)

        if direct:
            fold_d, fold_u = (grad_d[0], dp_swap(grad_d[1], 1)), (grad_u[0], dp_swap(grad_u[1], 1))
        one_a, low_a, pg_a, pg_a_oth, sums_a1, in_a = attend_back(
            order, info, "a", two_a, back_a, back_a_there, normed_a, inv_a, norms, o_here, q_a, k_a, v_a, lse_a, (q_own, q_oth), local, "back_a")
        in_a_there = far_swap(in_a)
        got_a = core_swap(pg_a_oth)
        one_c, low_c, sums_c1, dq_c, kv_mine, kv_there = attend_back(
            order, info, "c", two_c, back_c, back_c_there, normed_c, inv_c, norms, o_here, q_c, k_c, v_c, lse_c, None, local, "back_c")
        kv_got = core_swap(kv_there)
        if direct:
            fold_d = second_fold(fold_d, "d")
            fold_u = second_fold(fold_u, "u")
        res_full = lay_rows(order, info, [result], [res_there], "lay_out")
        out_mine, out_oth = grads_out(
            order, info, (low_a, low_c), (ctx_a, ctx_c), ((sums_a1, sums_c1), (sums_a2, sums_c2)), local)
        pg_c, sent, in_c = project_back(order, info, dq_c, kv_mine, kv_got, q_own, q_oth, out_oth, local, "project_c")
        in_c_there = far_swap(in_c)
        got_c = core_swap(sent)
        grad_a = grads_attn(order, info, tokens, (pg_a, pg_c), (got_a, got_c), out_mine, split=direct)
        everything = slice(None)
        if direct:
            keep_1, send_1, keep_2, send_2 = grad_a
            fold_1, fold_2 = (keep_1, dp_swap(send_1, 1)), (keep_2, dp_swap(send_2, 1))
            fold_d = third_fold(fold_d, "d")
            fold_u = third_fold(fold_u, "u")
            fold_2 = second_fold(fold_2, "vo")
            n_down = update(order, rates, [fold_d], [
                (down_t, first_down.T, second_down.T, DECAY_RATE, [(everything, 0, 0, units, False)])], "update_d")
            fold_1 = second_fold(fold_1, "qk")
            n_up = update(order, rates, [fold_u], [
                (up_weight, first_up, second_up, DECAY_RATE, [(everything, 0, 0, units, False)])], "update_u")
            fold_2 = third_fold(fold_2, "vo")
            fold_1 = third_fold(fold_1, "qk")
        gi = add_rows(order, info, [(one_a, in_a, in_a_there), (one_c, in_c, in_c_there)], "add_in")
        gi_there = core_swap(gi)
        if direct:
            res = update(order, rates, [fold_1, fold_2], [
                (qkv_weight, first_qkv, second_qkv, DECAY_RATE,
                 [(0, 0, 0, local, False), (1, 0, local, local, False), (2, 1, 0, local, False)]),
                (out_weight, first_out, second_out, DECAY_RATE, [(everything, 1, local, local, True)]),
                (norm_params, first_norm, second_norm, 0.0, [(everything, 1, 2 * local, 128, True)]),
            ], "update_a")
            n_down = [x.T for x in n_down]
            n_qkv, n_out, n_norm = res[:4], res[4:8], res[8:]
        input_grad = lay_rows(order, info, [gi], [gi_there], "lay_grad")
        if not direct:
            su, sd, sa = (lax.psum_scatter(x, "dp", scatter_dimension=0, tiled=True) for x in (grad_u, grad_d, grad_a))
            rest = (rate, fix_one, fix_two)
            n_up = adamw_update(su, up_weight, first_up, second_up, *rest, DECAY_RATE)
            n_down = adamw_update(sd.T, down_weight, first_down, second_down, *rest, DECAY_RATE)
            sq = jnp.stack([sa[:, c * local : (c + 1) * local] for c in range(3)])
            n_qkv = adamw_update(sq, qkv_weight, first_qkv, second_qkv, *rest, DECAY_RATE)
            n_out = adamw_update(sa[:, 3 * local : 4 * local].T, out_weight, first_out, second_out, *rest, DECAY_RATE)
            n_norm = adamw_update(sa[:, 4 * local : 4 * local + 4].T, norm_params, first_norm, second_norm, *rest, 0.0)
        return (res_full, input_grad, *n_qkv, *n_out, *n_up, *n_down, *n_norm)

    rows = P("dp", None)
    qkv, col, row, norm = P(None, "dp", "tensor"), P("tensor", "dp"), P("dp", "tensor"), P(None, "dp")
    params = (qkv, col, row, col, norm)
    return jax.shard_map(
        on_device,
        mesh=mesh,
        in_specs=(rows, rows, P("dp"), P("dp"), P()) + params * 3,
        out_specs=(rows, rows) + (qkv,) * 4 + (col,) * 4 + (row,) * 4 + (col,) * 4 + (norm,) * 4,
        check_vma=False,
    )
```

time: 452 us -> 229 us (0.51)
  matrix products: 173 us -> 0 us
  Pallas kernels: 0 us -> 87.6 us
  other arithmetic: 61.9 us -> 0.81 us
  local copies, waits for them, and re-layouts: 72.1 us -> 11.8 us
  waiting for transfers between devices: 90.3 us -> 81.4 us
    dot_general x84 -> x0, matrix products: 173 us -> none  [the longest x24 44.4 us: dot_nt(): lax.dot_general(a, b, (((1,), (1,)), ((), ())), preferred_element_type=F32)]
    pallas_call x0 -> x39, Pallas kernels: none -> 87.6 us  [call(): pl.pallas_call(run, out_shape=shapes, in_specs=specs, out_specs=spec if s...]
    unnamed x342 -> x86, local copies, waits for them, and re-layouts: 44.9 us -> 11.8 us
    convert_element_type x13 -> x0, other arithmetic: 12.6 us -> none  [the longest x5 6.38 us: adamw_update(): return (weight_new, first_new, second_new, weight_new.astype(BF))]
    select_n x10 -> x0, other arithmetic: 11.1 us -> none  [the longest x2 6.79 us: whole_rows(): return jnp.where(low == 0, jnp.concatenate(first), jnp.concatenate(second))]
    reduce_sum x15 -> x0, other arithmetic: 11.1 us -> none  [the longest x3 4.18 us: first_norm_back(): jnp.sum(hidden_grad * f[0], axis=0)]
    another operation x8 -> x1, other arithmetic: 9.18 us -> 0.08 us  [on_device(): rates = jnp.stack([rate, fix_one, fix_two])]
    ppermute x47 -> x46, waiting for transfers between devices: 90.3 us -> 81.4 us  [swap(): return lax.ppermute(x, axis, [(i, i ^ bit) for i in range(size)])]
  transfers between devices with their start and end apart: 47 -> 46, of which waited for: 14 -> 18; matrix products, arithmetic and copies ran while one was open for 61% -> 0% of each run, Pallas kernels for 0% -> 32%
where the time goes in v2:
time: 229 us; the launch traced here: 228 us
  Pallas kernels  87.6 us (38%)
  waiting for transfers between devices  81.4 us (36%)
  starting transfers between devices  44.3 us (19%)
  local copies, waits for them, and re-layouts  11.8 us (5%)
  between operations  2.42 us (1%)
    pallas_call x39, Pallas kernels, call(): pl.pallas_call(run, out_shape=shapes, in_specs=specs, out_specs=spec if s...  87.6 us
    ppermute x46, waiting for transfers between devices, swap(): return lax.ppermute(x, axis, [(i, i ^ bit) for i in range(size)])  81.4 us
    ppermute x46, starting transfers between devices, swap(): return lax.ppermute(x, axis, [(i, i ^ bit) for i in range(size)])  44.3 us
    unnamed x86, local copies, waits for them, and re-layouts  11.8 us
  transfers between devices with their start and end apart: 46, of which 18 were waited for; matrix products, arithmetic and copies ran while one was open for 0% of the time, Pallas kernels for 32%

profile of v2, /device:TPU:0, one launch (start us, length us, event | category | flops | bytes accessed | tf_op | source)
XLA Modules:
  0.0 228.3 jit_solution(6349959080978954562)
XLA Ops:
  4.1 3.0 %collective-permute-start.3 = (bf16[96,768]{1,0:T(8,128)(2,1)S(1)}, bf16[96,768]{1,0:T(8,128)(2,1)S(1)}, u32[]{:S(2)}, u32[]{:S(2)}) collective-permute-start(bf16[96,768]{1,0:T(8,128)(2,1)S(1)} %get-tuple-element.123.refs_1_), channel_id=1, source_target_pairs={{0,4},{4,0},{8,12},{12,8},{16,20},{20,16},{24,28},{28,24},{1,5},{5... | collective-permute-start | bytes 442376 | tf_op jit(solution)/shard_map/ppermute | solution.py:643
  7.1 1.6 collective-permute-start
  8.7 2.6 %collective-permute-start.1 = (bf16[96,768]{1,0:T(8,128)(2,1)S(1)}, bf16[96,768]{1,0:T(8,128)(2,1)S(1)}, u32[]{:S(2)}, u32[]{:S(2)}) collective-permute-start(bf16[96,768]{1,0:T(8,128)(2,1)S(1)} %get-tuple-element.123.refs_1_), channel_id=1, source_target_pairs={{0,16},{4,20},{8,24},{12,28},{16,0},{20,4},{24,8},{28,12},{1,17},{... | collective-permute-start | bytes 442376 | tf_op jit(solution)/shard_map/ppermute | solution.py:643
  13.0 2.6 %collective-permute-done.4.refs_2_ = bf16[96,192]{1,0:T(8,128)(2,1)S(1)} collective-permute-done((bf16[96,192]{1,0:T(8,128)(2,1)S(1)}, bf16[96,192]{1,0:T(8,128)(2,1)S(1)}, u32[]{:S(2)}, u32[]{:S(2)}) %collective-permute-start.4) | collective-permute-done | bytes 36896 | tf_op jit(solution)/shard_map/ppermute | solution.py:643
  15.6 1.7 copy-done
  19.5 3.0 %collective-permute-done.1.refs_2_ = bf16[96,768]{1,0:T(8,128)(2,1)S(1)} collective-permute-done((bf16[96,768]{1,0:T(8,128)(2,1)S(1)}, bf16[96,768]{1,0:T(8,128)(2,1)S(1)}, u32[]{:S(2)}, u32[]{:S(2)}) %collective-permute-start.1) | collective-permute-done | bytes 147488 | tf_op jit(solution)/shard_map/ppermute | solution.py:643
  23.7 2.1 collective-permute-start.6
  28.3 3.1 %collective-permute-done.6.refs_2_ = bf16[96,1024]{1,0:T(8,128)(2,1)S(1)} collective-permute-done((bf16[96,1024]{1,0:T(8,128)(2,1)S(1)}, bf16[96,1024]{1,0:T(8,128)(2,1)S(1)}, u32[]{:S(2)}, u32[]{:S(2)}) %collective-permute-start.6) | collective-permute-done | bytes 196640 | tf_op jit(solution)/shard_map/ppermute | solution.py:643
  31.4 10.3 %collective-permute-done.7.refs_3_ = bf16[96,1024]{1,0:T(8,128)(2,1)S(1)} collective-permute-done((bf16[96,1024]{1,0:T(8,128)(2,1)S(1)}, bf16[96,1024]{1,0:T(8,128)(2,1)S(1)}, u32[]{:S(2)}, u32[]{:S(2)}) %collective-permute-start.7) | collective-permute-done | bytes 196640 | tf_op jit(solution)/shard_map/ppermute | solution.py:643
  43.1 1.6 collective-permute-start.11
  44.7 4.2 %collective-permute-start.12 = (bf16[96,768]{1,0:T(8,128)(2,1)S(1)}, bf16[96,768]{1,0:T(8,128)(2,1)S(1)}, u32[]{:S(2)}, u32[]{:S(2)}) collective-permute-start(bf16[96,768]{1,0:T(8,128)(2,1)S(1)} %bitcast.10), channel_id=1, source_target_pairs={{0,16},{4,20},{8,24},{12,28},{16,0},{20,4},{24,8},{28,12},{1,17},{... | collective-permute-start | bytes 442376 | tf_op jit(solution)/shard_map/ppermute | solution.py:643
  48.9 8.1 %attend_a.1 = (bf16[2,512,192]{2,1,0:T(8,128)(2,1)S(1)}, bf16[2,512,192]{2,1,0:T(8,128)(2,1)S(1)}, bf16[2,512,192]{2,1,0:T(8,128)(2,1)S(1)}, f32[2,512,128]{2,1,0:T(8,128)S(1)}, bf16[512,384]{1,0:T(8,128)(2,1)S(1)}) custom-call(s32[5]{0:T(128)S(1)} %pad_add_fusion.refs_0_, bf16[1536,768]{1,0:T(8,128)(2,1)S(1)} %copy-done.1, ...), custom_call_target="tpu_custom_call" | custom-call | flops 1 | bytes 1 | tf_op jit(solution)/shard_map/attend_a/pallas_call | solution.py:59
  60.7 4.9 %attend_c.1 = (bf16[2,256,192]{2,1,0:T(8,128)(2,1)S(1)}, bf16[2,512,192]{2,1,0:T(8,128)(2,1)S(1)}, bf16[2,512,192]{2,1,0:T(8,128)(2,1)S(1)}, f32[2,256,128]{2,1,0:T(8,128)S(1)}, bf16[256,384]{1,0:T(8,128)(2,1)S(1)}) custom-call(s32[5]{0:T(128)S(1)} %pad_add_fusion.refs_0_, bf16[1536,768]{1,0:T(8,128)(2,1)S(1)} %copy-done.1, ...), custom_call_target="tpu_custom_call" | custom-call | flops 1 | bytes 1 | tf_op jit(solution)/shard_map/attend_c/pallas_call | solution.py:59
  65.7 3.5 %collective-permute-done.13.refs_2_ = bf16[192,768]{1,0:T(8,128)(2,1)S(1)} collective-permute-done((bf16[192,768]{1,0:T(8,128)(2,1)S(1)}, bf16[192,768]{1,0:T(8,128)(2,1)S(1)}, u32[]{:S(2)}, u32[]{:S(2)}) %collective-permute-start.13) | collective-permute-done | bytes 294944 | tf_op jit(solution)/shard_map/ppermute | solution.py:643
  72.4 1.7 collective-permute-done.14.refs_2_.refs_7_.refs_6_
  75.3 5.4 %lift_a.1 = (f32[512,768]{1,0:T(8,128)S(1)}, f32[512,128]{1,0:T(8,128)S(1)}, f32[512,1536]{1,0:T(8,128)S(1)}, bf16[512,768]{1,0:T(8,128)(2,1)S(1)}, bf16[512,1536]{1,0:T(8,128)(2,1)S(1)}) custom-call(s32[5]{0:T(128)S(1)} %pad_add_fusion.refs_0_, bf16[1536,768]{1,0:T(8,128)(2,1)S(1)} %copy-done.1, bf16[512,384]{1,0:T(8,128)(2,1)S(1)} %get-tuple-element.125.refs_3_.refs_2_, ...), custom_call_target="tpu_custom_call" | custom-call | flops 1 | bytes 1 | tf_op jit(solution)/shard_map/lift_a/pallas_call | solution.py:59
  80.8 5.6 %collective-permute-done.15.refs_2_ = bf16[384,768]{1,0:T(8,128)(2,1)S(1)} collective-permute-done((bf16[384,768]{1,0:T(8,128)(2,1)S(1)}, bf16[384,768]{1,0:T(8,128)(2,1)S(1)}, u32[]{:S(2)}, u32[]{:S(2)}) %collective-permute-start.15) | collective-permute-done | bytes 589856 | tf_op jit(solution)/shard_map/ppermute | solution.py:643
  87.6 2.9 %lift_c.1 = (f32[256,768]{1,0:T(8,128)S(1)}, f32[256,128]{1,0:T(8,128)S(1)}, f32[256,1536]{1,0:T(8,128)S(1)}, bf16[256,768]{1,0:T(8,128)(2,1)S(1)}, bf16[256,1536]{1,0:T(8,128)(2,1)S(1)}) custom-call(s32[5]{0:T(128)S(1)} %pad_add_fusion.refs_0_, bf16[1536,768]{1,0:T(8,128)(2,1)S(1)} %copy-done.1, ...), custom_call_target="tpu_custom_call" | custom-call | flops 1 | bytes 1 | tf_op jit(solution)/shard_map/lift_c/pallas_call | solution.py:59
  93.2 2.0 drop_a.1
  97.3 6.7 %collective-permute-done.20.refs_11_ = bf16[256,768]{1,0:T(8,128)(2,1)S(1)} collective-permute-done((bf16[256,768]{1,0:T(8,128)(2,1)S(1)}, bf16[256,768]{1,0:T(8,128)(2,1)S(1)}, u32[]{:S(2)}, u32[]{:S(2)}) %collective-permute-start.20) | collective-permute-done | bytes 393248 | tf_op jit(solution)/shard_map/ppermute | solution.py:643
  104.0 3.5 %turn_c.1 = (bf16[256,768]{1,0:T(8,128)(2,1)S(1)}, f32[256,768]{1,0:T(8,128)S(1)}, bf16[256,768]{1,0:T(8,128)(2,1)S(1)}, bf16[256,1536]{1,0:T(8,128)(2,1)S(1)}, ...) custom-call(s32[5]{0:T(128)S(1)} %pad_add_fusion.refs_0_, f32[256,768]{1,0:T(8,128)S(1)} %get-tuple-element.138.refs_1_.refs_4_, ...), custom_call_target="tpu_custom_call" | custom-call | flops 1 | bytes 1 | tf_op jit(solution)/shard_map/turn_c/pallas_call | solution.py:59
  108.3 4.1 %collective-permute-done.18.refs_12_ = bf16[256,768]{1,0:T(8,128)(2,1)S(1)} collective-permute-done((bf16[256,768]{1,0:T(8,128)(2,1)S(1)}, bf16[256,768]{1,0:T(8,128)(2,1)S(1)}, u32[]{:S(2)}, u32[]{:S(2)}) %collective-permute-start.18) | collective-permute-done | bytes 393248 | tf_op jit(solution)/shard_map/ppermute | solution.py:643
  112.4 8.0 %collective-permute-done.19.refs_13_ = bf16[256,768]{1,0:T(8,128)(2,1)S(1)} collective-permute-done((bf16[256,768]{1,0:T(8,128)(2,1)S(1)}, bf16[256,768]{1,0:T(8,128)(2,1)S(1)}, u32[]{:S(2)}, u32[]{:S(2)}) %collective-permute-start.19) | collective-permute-done | bytes 393248 | tf_op jit(solution)/shard_map/ppermute | solution.py:643
  120.4 6.5 %turn_a.1 = (bf16[768,768]{1,0:T(8,128)(2,1)S(1)}, f32[512,768]{1,0:T(8,128)S(1)}, bf16[512,768]{1,0:T(8,128)(2,1)S(1)}, bf16[512,1536]{1,0:T(8,128)(2,1)S(1)}, ...) custom-call(s32[5]{0:T(128)S(1)} %pad_add_fusion.refs_0_, f32[512,768]{1,0:T(8,128)S(1)} %get-tuple-element.130.refs_1_.refs_4_, ...), custom_call_target="tpu_custom_call" | custom-call | flops 1 | bytes 1 | tf_op jit(solution)/shard_map/turn_a/pallas_call | solution.py:59
  129.5 2.0 collective-permute-done.25.refs_7_.refs_8_
  131.5 3.2 %grads_d.1 = (f32[384,768]{1,0:T(8,128)S(1)}, bf16[384,768]{1,0:T(8,128)(2,1)S(1)}) custom-call(s32[5]{0:T(128)S(1)} %pad_add_fusion.refs_0_, bf16[512,1536]{1,0:T(8,128)(2,1)S(1)} %get-tuple-element.145.refs_1_, bf16[512,768]{1,0:T(8,128)(2,1)S(1)} %get-tuple-element.133.refs_1_.refs_2_, bf16[256,1536]{1,0:T(8,128)(2,1)S(1)} %get-tuple-element.146.refs_3_, ...), custom_call_target="tpu_custom_call" | custom-call | flops 1 | bytes 1 | tf_op jit(solution)/shard_map/grads_d/pallas_call | solution.py:59
  135.3 3.2 %grads_u.1 = (f32[384,768]{1,0:T(8,128)S(1)}, bf16[384,768]{1,0:T(8,128)(2,1)S(1)}) custom-call(s32[5]{0:T(128)S(1)} %pad_add_fusion.refs_0_, bf16[512,1536]{1,0:T(8,128)(2,1)S(1)} %get-tuple-element.131.refs_6_.refs_2_.refs_1_, bf16[512,768]{1,0:T(8,128)(2,1)S(1)} %get-tuple-element.143.refs_2_, ...), custom_call_target="tpu_custom_call" | custom-call | flops 1 | bytes 1 | tf_op jit(solution)/shard_map/grads_u/pallas_call | solution.py:59
  138.4 1.5 collective-permute-start.26
  140.0 7.9 %collective-permute-done.29.refs_3_ = bf16[512,768]{1,0:T(8,128)(2,1)S(1)} collective-permute-done((bf16[512,768]{1,0:T(8,128)(2,1)S(1)}, bf16[512,768]{1,0:T(8,128)(2,1)S(1)}, u32[]{:S(2)}, u32[]{:S(2)}) %collective-permute-start.29) | collective-permute-done | bytes 786464 | tf_op jit(solution)/shard_map/ppermute | solution.py:643
  147.9 11.5 %back_a.1 = (f32[512,768]{1,0:T(8,128)S(1)}, bf16[512,768]{1,0:T(8,128)(2,1)S(1)}, bf16[512,576]{1,0:T(8,128)(2,1)S(1)}, bf16[512,640]{1,0:T(8,128)(2,1)S(1)}, f...) custom-call(s32[5]{0:T(128)S(1)} %pad_add_fusion.refs_0_, f32[512,768]{1,0:T(8,128)S(1)} %get-tuple-element.159.refs_1_, ...), custom_call_target="tpu_custom_call" | custom-call | flops 1 | bytes 1 | tf_op jit(solution)/shard_map/back_a/pallas_call | solution.py:59
  159.5 5.0 %back_c.1 = (f32[256,768]{1,0:T(8,128)S(1)}, bf16[256,768]{1,0:T(8,128)(2,1)S(1)}, f32[8,768]{1,0:T(8,128)S(1)}, bf16[2,256,192]{2,1,0:T(8,128)(2,1)S(1)}, f32[2...) custom-call(s32[5]{0:T(128)S(1)} %pad_add_fusion.refs_0_, f32[256,768]{1,0:T(8,128)S(1)} %copy-done.5, ...), custom_call_target="tpu_custom_call" | custom-call | flops 1 | bytes 1 | tf_op jit(solution)/shard_map/back_c/pallas_call | solution.py:59
  165.9 2.0 lay_out.1.refs_9_
  167.9 1.7 copy-done.3
  169.6 2.3 %grads_out.1 = (f32[768,320]{1,0:T(8,128)S(1)}, bf16[768,320]{1,0:T(8,128)(2,1)S(1)}) custom-call(s32[5]{0:T(128)S(1)} %pad_add_fusion.refs_0_, bf16[512,768]{1,0:T(8,128)(2,1)S(1)} %get-tuple-element.173.refs_1_, bf16[256,768]{1,0:T(8,128)(2,1)S(1)} %get-tuple-element.174.refs_2_, bf16[512,384]{1,0:T(8,128)(2,1)S(1)} %get-tuple-element.125.refs_3_.refs_2_, ...), custom_call_target="tpu_custom_call" | custom-call | flops 1 | bytes 1 | tf_op jit(solution)/shard_map/grads_out/pallas_call | solution.py:59
  175.1 1.6 collective-permute-done.33.refs_4_
  176.8 3.4 %grads_attn.1 = (f32[384,384]{1,0:T(8,128)S(1)}, bf16[384,384]{1,0:T(8,128)(2,1)S(1)}, f32[384,512]{1,0:T(8,128)S(1)}, bf16[384,512]{1,0:T(8,128)(2,1)S(1)}) custom-call(s32[5]{0:T(128)S(1)} %pad_add_fusion.refs_0_, bf16[1536,768]{1,0:T(8,128)(2,1)S(1)} %copy-done.1, bf16[512,576]{1,0:T(8,128)(2,1)S(1)} %get-tuple-element.181.refs_2_, ...), custom_call_target="tpu_custom_call" | custom-call | flops 1 | bytes 1 | tf_op jit(solution)/shard_map/grads_attn/pallas_call | solution.py:59
  182.7 2.2 collective-permute-done.36.refs_2_
  186.1 4.4 %collective-permute-done.39.refs_2_ = bf16[192,768]{1,0:T(8,128)(2,1)S(1)} collective-permute-done((bf16[192,768]{1,0:T(8,128)(2,1)S(1)}, bf16[192,768]{1,0:T(8,128)(2,1)S(1)}, u32[]{:S(2)}, u32[]{:S(2)}) %collective-permute-start.39) | collective-permute-done | bytes 294944 | tf_op jit(solution)/shard_map/ppermute | solution.py:643
  190.5 1.7 collective-permute-start.37
  194.7 4.8 %collective-permute-done.37.refs_2_ = bf16[96,768]{1,0:T(8,128)(2,1)S(1)} collective-permute-done((bf16[96,768]{1,0:T(8,128)(2,1)S(1)}, bf16[96,768]{1,0:T(8,128)(2,1)S(1)}, u32[]{:S(2)}, u32[]{:S(2)}) %collective-permute-start.37) | collective-permute-done | bytes 147488 | tf_op jit(solution)/shard_map/ppermute | solution.py:643
  199.6 1.7 update_d.1
  202.8 2.0 collective-permute-start.40
  204.8 2.5 %collective-permute-done.42.refs_2_ = bf16[96,768]{1,0:T(8,128)(2,1)S(1)} collective-permute-done((bf16[96,768]{1,0:T(8,128)(2,1)S(1)}, bf16[96,768]{1,0:T(8,128)(2,1)S(1)}, u32[]{:S(2)}, u32[]{:S(2)}) %collective-permute-start.42) | collective-permute-done | bytes 147488 | tf_op jit(solution)/shard_map/ppermute | solution.py:643
  207.4 1.7 update_u.1
  212.9 2.3 %collective-permute-start.44 = (bf16[96,384]{1,0:T(8,128)(2,1)S(1)}, bf16[96,384]{1,0:T(8,128)(2,1)S(1)}, u32[]{:S(2)}, u32[]{:S(2)}) collective-permute-start(bf16[96,384]{1,0:T(8,128)(2,1)S(1)} %get-tuple-element.203.refs_7_), channel_id=1, source_target_pairs={{0,16},{4,20},{8,24},{12,28},{16,0},{20,4},{24,8},{28,12},{1,17},{... | collective-permute-start | bytes 221192 | tf_op jit(solution)/shard_map/ppermute | solution.py:643
  215.3 7.4 %collective-permute-done.44.refs_2_ = bf16[96,384]{1,0:T(8,128)(2,1)S(1)} collective-permute-done((bf16[96,384]{1,0:T(8,128)(2,1)S(1)}, bf16[96,384]{1,0:T(8,128)(2,1)S(1)}, u32[]{:S(2)}, u32[]{:S(2)}) %collective-permute-start.44) | collective-permute-done | bytes 73760 | tf_op jit(solution)/shard_map/ppermute | solution.py:643
  222.7 2.0 update_a.1
  225.4 2.8 %lay_grad.1 = f32[1536,768]{1,0:T(8,128)} custom-call(s32[5]{0:T(128)S(1)} %pad_add_fusion.refs_0_, f32[768,768]{1,0:T(8,128)S(1)} %add_in.1.refs_14_.refs_1_, f32[768,768]{1,0:T(8,128)S(1)} %collective-permute-done.43.refs_2_, bf16[4,96]{1,0:T(4,128)(2,1)S(1)} %copy-done.42), custom_call_target="tpu_custom_call" | custom-call | flops 1 | bytes 1 | tf_op jit(solution)/shard_map/lay_grad/pallas_call | solution.py:59
  (171 shorter events, 46.7 us)
Async XLA Ops:
  4.1 15.4 %collective-permute-start.3 = (bf16[96,768]{1,0:T(8,128)(2,1)S(1)}, bf16[96,768]{1,0:T(8,128)(2,1)S(1)}, u32[]{:S(2)}, u32[]{:S(2)}) collective-permute-start(bf16[96,768]{1,0:T(8,128)(2,1)S(1)} %get-tuple-element.123.refs_1_), channel_id=1, source_target_pairs={{0,4},{4,0},{8,12},{12,8},{16,20},{20,16},{24,28},{28,24},{1,5},{5... | collective-permute-start | bytes 442376 | tf_op jit(solution)/shard_map/ppermute | solution.py:643
  7.1 12.4 %collective-permute-start = (bf16[96,768]{1,0:T(8,128)(2,1)S(1)}, bf16[96,768]{1,0:T(8,128)(2,1)S(1)}, u32[]{:S(2)}, u32[]{:S(2)}) collective-permute-start(bf16[96,768]{1,0:T(8,128)(2,1)S(1)} %get-tuple-element.123.refs_1_), channel_id=1, source_target_pairs={{0,8},{4,12},{8,0},{12,4},{16,24},{20,28},{24,16},{28,20},{1,9},{5... | collective-permute-start | bytes 442376 | tf_op jit(solution)/shard_map/ppermute | solution.py:643
  8.7 13.9 %collective-permute-start.1 = (bf16[96,768]{1,0:T(8,128)(2,1)S(1)}, bf16[96,768]{1,0:T(8,128)(2,1)S(1)}, u32[]{:S(2)}, u32[]{:S(2)}) collective-permute-start(bf16[96,768]{1,0:T(8,128)(2,1)S(1)} %get-tuple-element.123.refs_1_), channel_id=1, source_target_pairs={{0,16},{4,20},{8,24},{12,28},{16,0},{20,4},{24,8},{28,12},{1,17},{... | collective-permute-start | bytes 442376 | tf_op jit(solution)/shard_map/ppermute | solution.py:643
  11.3 11.3 %collective-permute-start.2 = (bf16[96,768]{1,0:T(8,128)(2,1)S(1)}, bf16[96,768]{1,0:T(8,128)(2,1)S(1)}, u32[]{:S(2)}, u32[]{:S(2)}) collective-permute-start(bf16[96,768]{1,0:T(8,128)(2,1)S(1)} %get-tuple-element.123.refs_1_), channel_id=1, source_target_pairs={{0,24},{4,28},{8,16},{12,20},{16,8},{20,12},{24,0},{28,4},{1,25},{... | collective-permute-start | bytes 442376 | tf_op jit(solution)/shard_map/ppermute | solution.py:643
  11.5 4.1 %collective-permute-start.4 = (bf16[96,192]{1,0:T(8,128)(2,1)S(1)}, bf16[96,192]{1,0:T(8,128)(2,1)S(1)}, u32[]{:S(2)}, u32[]{:S(2)}) collective-permute-start(bf16[96,192]{1,0:T(8,128)(2,1)S(1)} %get-tuple-element.124.refs_5_), channel_id=1, source_target_pairs={{0,2},{1,3},{2,0},{3,1},{4,6},{5,7},{6,4},{7,5},{8,10},{9,11},{10,... | collective-permute-start | bytes 110600 | tf_op jit(solution)/shard_map/ppermute | solution.py:643
  23.1 19.3 %collective-permute-start.5 = (bf16[288,768]{1,0:T(8,128)(2,1)S(1)}, bf16[288,768]{1,0:T(8,128)(2,1)S(1)}, u32[]{:S(2)}, u32[]{:S(2)}) collective-permute-start(bf16[288,768]{1,0:T(8,128)(2,1)S(1)} %stack_q.1.refs_5_.refs_2_), channel_id=1, source_target_pairs={{0,4},{4,0},{8,12},{12,8},{16,20},{20,16},{24,28},{28,24},{1,5},{5... | collective-permute-start | bytes 1327112 | tf_op jit(solution)/shard_map/ppermute | solution.py:643
  23.7 7.7 %collective-permute-start.6 = (bf16[96,1024]{1,0:T(8,128)(2,1)S(1)}, bf16[96,1024]{1,0:T(8,128)(2,1)S(1)}, u32[]{:S(2)}, u32[]{:S(2)}) collective-permute-start(bf16[96,1024]{1,0:T(8,128)(2,1)S(1)} %pack_more.1.refs_5_.refs_1_), channel_id=1, source_target_pairs={{0,8},{4,12},{8,0},{12,4},{16,24},{20,28},{24,16},{28,20},{1,9},{5... | collective-permute-start | bytes 589832 | tf_op jit(solution)/shard_map/ppermute | solution.py:643
  25.9 15.9 %collective-permute-start.7 = (bf16[96,1024]{1,0:T(8,128)(2,1)S(1)}, bf16[96,1024]{1,0:T(8,128)(2,1)S(1)}, u32[]{:S(2)}, u32[]{:S(2)}) collective-permute-start(bf16[96,1024]{1,0:T(8,128)(2,1)S(1)} %pack_more.1.refs_5_.refs_1_), channel_id=1, source_target_pairs={{0,16},{4,20},{8,24},{12,28},{16,0},{20,4},{24,8},{28,12},{1,17},{... | collective-permute-start | bytes 589832 | tf_op jit(solution)/shard_map/ppermute | solution.py:643
  26.9 14.9 %collective-permute-start.8 = (bf16[96,1024]{1,0:T(8,128)(2,1)S(1)}, bf16[96,1024]{1,0:T(8,128)(2,1)S(1)}, u32[]{:S(2)}, u32[]{:S(2)}) collective-permute-start(bf16[96,1024]{1,0:T(8,128)(2,1)S(1)} %pack_more.1.refs_5_.refs_1_), channel_id=1, source_target_pairs={{0,24},{4,28},{8,16},{12,20},{16,8},{20,12},{24,0},{28,4},{1,25},{... | collective-permute-start | bytes 589832 | tf_op jit(solution)/shard_map/ppermute | solution.py:643
  43.0 5.8 %collective-permute-start.9 = (bf16[768,768]{1,0:T(8,128)(2,1)S(1)}, bf16[768,768]{1,0:T(8,128)(2,1)S(1)}, u32[]{:S(2)}, u32[]{:S(2)}) collective-permute-start(bf16[768,768]{1,0:T(8,128)(2,1)S(1)} %place_q.1.refs_2_.refs_4_.refs_3_.refs_12_), channel_id=1, source_target_pairs={{0,1},{1,0},{2,3},{3,2},{4,5},{5,4},{6,7},{7,6},{8,9},{9,8},{10,11... | collective-permute-start | bytes 3538952 | tf_op jit(solution)/shard_map/ppermute | solution.py:643
  43.1 26.7 %collective-permute-start.11 = (bf16[384,1024]{1,0:T(8,128)(2,1)S(1)}, bf16[384,1024]{1,0:T(8,128)(2,1)S(1)}, u32[]{:S(2)}, u32[]{:S(2)}) collective-permute-start(bf16[384,1024]{1,0:T(8,128)(2,1)S(1)} %stack_u.1.refs_5_.refs_1_), channel_id=1, source_target_pairs={{0,4},{4,0},{8,12},{12,8},{16,20},{20,16},{24,28},{28,24},{1,5},{5... | collective-permute-start | bytes 2359304 | tf_op jit(solution)/shard_map/ppermute | solution.py:643
  44.7 15.4 %collective-permute-start.12 = (bf16[96,768]{1,0:T(8,128)(2,1)S(1)}, bf16[96,768]{1,0:T(8,128)(2,1)S(1)}, u32[]{:S(2)}, u32[]{:S(2)}) collective-permute-start(bf16[96,768]{1,0:T(8,128)(2,1)S(1)} %bitcast.10), channel_id=1, source_target_pairs={{0,16},{4,20},{8,24},{12,28},{16,0},{20,4},{24,8},{28,12},{1,17},{... | collective-permute-start | bytes 442376 | tf_op jit(solution)/shard_map/ppermute | solution.py:643
  58.6 11.3 %collective-permute-start.10 = (bf16[512,384]{1,0:T(8,128)(2,1)S(1)}, bf16[512,384]{1,0:T(8,128)(2,1)S(1)}, u32[]{:S(2)}, u32[]{:S(2)}) collective-permute-start(bf16[512,384]{1,0:T(8,128)(2,1)S(1)} %get-tuple-element.125.refs_3_.refs_2_), channel_id=1, source_target_pairs={{0,2},{1,3},{2,0},{3,1},{4,6},{5,7},{6,4},{7,5},{8,10},{9,11},{10,... | collective-permute-start | bytes 1179656 | tf_op jit(solution)/shard_map/ppermute | solution.py:643
  60.7 8.6 %collective-permute-start.13 = (bf16[192,768]{1,0:T(8,128)(2,1)S(1)}, bf16[192,768]{1,0:T(8,128)(2,1)S(1)}, u32[]{:S(2)}, u32[]{:S(2)}) collective-permute-start(bf16[192,768]{1,0:T(8,128)(2,1)S(1)} %stack_d.1.refs_4_.refs_1_), channel_id=1, source_target_pairs={{0,8},{4,12},{8,0},{12,4},{16,24},{20,28},{24,16},{28,20},{1,9},{5... | collective-permute-start | bytes 884744 | tf_op jit(solution)/shard_map/ppermute | solution.py:643
  70.5 3.5 %collective-permute-start.14 = (bf16[768,1024]{1,0:T(8,128)(2,1)S(1)}, bf16[768,1024]{1,0:T(8,128)(2,1)S(1)}, u32[]{:S(2)}, u32[]{:S(2)}) collective-permute-start(bf16[768,1024]{1,0:T(8,128)(2,1)S(1)} %place_u.1.refs_1_.refs_5_.refs_6_), channel_id=1, source_target_pairs={{0,1},{1,0},{2,3},{3,2},{4,5},{5,4},{6,7},{7,6},{8,9},{9,8},{10,11... | collective-permute-start | bytes 4718600 | tf_op jit(solution)/shard_map/ppermute | solution.py:643
  70.6 15.7 %collective-permute-start.15 = (bf16[384,768]{1,0:T(8,128)(2,1)S(1)}, bf16[384,768]{1,0:T(8,128)(2,1)S(1)}, u32[]{:S(2)}, u32[]{:S(2)}) collective-permute-start(bf16[384,768]{1,0:T(8,128)(2,1)S(1)} %stack_d4.1.refs_4_.refs_1_), channel_id=1, source_target_pairs={{0,4},{4,0},{8,12},{12,8},{16,20},{20,16},{24,28},{28,24},{1,5},{5... | collective-permute-start | bytes 1769480 | tf_op jit(solution)/shard_map/ppermute | solution.py:643
  71.2 9.6 %collective-permute-start.16 = (bf16[256,384]{1,0:T(8,128)(2,1)S(1)}, bf16[256,384]{1,0:T(8,128)(2,1)S(1)}, u32[]{:S(2)}, u32[]{:S(2)}) collective-permute-start(bf16[256,384]{1,0:T(8,128)(2,1)S(1)} %get-tuple-element.126.refs_3_.refs_2_.refs_4_), channel_id=1, source_target_pairs={{0,2},{1,3},{2,0},{3,1},{4,6},{5,7},{6,4},{7,5},{8,10},{9,11},{10,... | collective-permute-start | bytes 589832 | tf_op jit(solution)/shard_map/ppermute | solution.py:643
  87.0 3.6 %collective-permute-start.17 = (bf16[768,768]{1,0:T(8,128)(2,1)S(1)}, bf16[768,768]{1,0:T(8,128)(2,1)S(1)}, u32[]{:S(2)}, u32[]{:S(2)}) collective-permute-start(bf16[768,768]{1,0:T(8,128)(2,1)S(1)} %place_d.1.refs_9_.refs_3_.refs_7_), channel_id=1, source_target_pairs={{0,1},{1,0},{2,3},{3,2},{4,5},{5,4},{6,7},{7,6},{8,9},{9,8},{10,11... | collective-permute-start | bytes 3538952 | tf_op jit(solution)/shard_map/ppermute | solution.py:643
  87.1 10.2 %collective-permute-start.21 = (bf16[512,1536]{1,0:T(8,128)(2,1)S(1)}, bf16[512,1536]{1,0:T(8,128)(2,1)S(1)}, u32[]{:S(2)}, u32[]{:S(2)}) collective-permute-start(bf16[512,1536]{1,0:T(8,128)(2,1)S(1)} %get-tuple-element.131.refs_6_.refs_2_.refs_1_), channel_id=1, source_target_pairs={{0,1},{1,0},{2,3},{3,2},{4,5},{5,4},{6,7},{7,6},{8,9},{9,8},{10,11... | collective-permute-start | bytes 4718600 | tf_op jit(solution)/shard_map/ppermute | solution.py:643
  90.5 6.8 %collective-permute-start.22 = (bf16[256,1536]{1,0:T(8,128)(2,1)S(1)}, bf16[256,1536]{1,0:T(8,128)(2,1)S(1)}, u32[]{:S(2)}, u32[]{:S(2)}) collective-permute-start(bf16[256,1536]{1,0:T(8,128)(2,1)S(1)} %get-tuple-element.135.refs_2_.refs_5_.refs_3_), channel_id=1, source_target_pairs={{0,1},{1,0},{2,3},{3,2},{4,5},{5,4},{6,7},{7,6},{8,9},{9,8},{10,11... | collective-permute-start | bytes 2359304 | tf_op jit(solution)/shard_map/ppermute | solution.py:643
  92.0 12.0 %collective-permute-start.20 = (bf16[256,768]{1,0:T(8,128)(2,1)S(1)}, bf16[256,768]{1,0:T(8,128)(2,1)S(1)}, u32[]{:S(2)}, u32[]{:S(2)}) collective-permute-start(bf16[256,768]{1,0:T(8,128)(2,1)S(1)} %drop_c.1.refs_5_.refs_10_), channel_id=1, source_target_pairs={{0,2},{1,3},{2,0},{3,1},{4,6},{5,7},{6,4},{7,5},{8,10},{9,11},{10,... | collective-permute-start | bytes 1179656 | tf_op jit(solution)/shard_map/ppermute | solution.py:643
  95.2 17.2 %collective-permute-start.18 = (bf16[256,768]{1,0:T(8,128)(2,1)S(1)}, bf16[256,768]{1,0:T(8,128)(2,1)S(1)}, u32[]{:S(2)}, u32[]{:S(2)}) collective-permute-start(bf16[256,768]{1,0:T(8,128)(2,1)S(1)} %get-tuple-element.136.refs_10_), channel_id=1, source_target_pairs={{0,2},{1,3},{2,0},{3,1},{4,6},{5,7},{6,4},{7,5},{8,10},{9,11},{10,... | collective-permute-start | bytes 1179656 | tf_op jit(solution)/shard_map/ppermute | solution.py:643
  96.1 24.3 %collective-permute-start.19 = (bf16[256,768]{1,0:T(8,128)(2,1)S(1)}, bf16[256,768]{1,0:T(8,128)(2,1)S(1)}, u32[]{:S(2)}, u32[]{:S(2)}) collective-permute-start(bf16[256,768]{1,0:T(8,128)(2,1)S(1)} %get-tuple-element.137.refs_14_.refs_11_), channel_id=1, source_target_pairs={{0,2},{1,3},{2,0},{3,1},{4,6},{5,7},{6,4},{7,5},{8,10},{9,11},{10,... | collective-permute-start | bytes 1179656 | tf_op jit(solution)/shard_map/ppermute | solution.py:643
  126.9 4.6 %collective-permute-start.24 = (bf16[512,1536]{1,0:T(8,128)(2,1)S(1)}, bf16[512,1536]{1,0:T(8,128)(2,1)S(1)}, u32[]{:S(2)}, u32[]{:S(2)}) collective-permute-start(bf16[512,1536]{1,0:T(8,128)(2,1)S(1)} %get-tuple-element.145.refs_1_), channel_id=1, source_target_pairs={{0,1},{1,0},{2,3},{3,2},{4,5},{5,4},{6,7},{7,6},{8,9},{9,8},{10,11... | collective-permute-start | bytes 4718600 | tf_op jit(solution)/shard_map/ppermute | solution.py:643
  126.9 4.5 %collective-permute-start.25 = (bf16[256,1536]{1,0:T(8,128)(2,1)S(1)}, bf16[256,1536]{1,0:T(8,128)(2,1)S(1)}, u32[]{:S(2)}, u32[]{:S(2)}) collective-permute-start(bf16[256,1536]{1,0:T(8,128)(2,1)S(1)} %get-tuple-element.146.refs_3_), channel_id=1, source_target_pairs={{0,1},{1,0},{2,3},{3,2},{4,5},{5,4},{6,7},{7,6},{8,9},{9,8},{10,11... | collective-permute-start | bytes 2359304 | tf_op jit(solution)/shard_map/ppermute | solution.py:643
  127.4 20.4 %collective-permute-start.29 = (bf16[512,768]{1,0:T(8,128)(2,1)S(1)}, bf16[512,768]{1,0:T(8,128)(2,1)S(1)}, u32[]{:S(2)}, u32[]{:S(2)}) collective-permute-start(bf16[512,768]{1,0:T(8,128)(2,1)S(1)} %get-tuple-element.147.refs_9_.refs_2_), channel_id=1, source_target_pairs={{0,2},{1,3},{2,0},{3,1},{4,6},{5,7},{6,4},{7,5},{8,10},{9,11},{10,... | collective-permute-start | bytes 2359304 | tf_op jit(solution)/shard_map/ppermute | solution.py:643
  128.6 37.3 %collective-permute-start.23 = (bf16[768,768]{1,0:T(8,128)(2,1)S(1)}, bf16[768,768]{1,0:T(8,128)(2,1)S(1)}, u32[]{:S(2)}, u32[]{:S(2)}) collective-permute-start(bf16[768,768]{1,0:T(8,128)(2,1)S(1)} %get-tuple-element.142.refs_1_), channel_id=1, source_target_pairs={{0,1},{1,0},{2,3},{3,2},{4,5},{5,4},{6,7},{7,6},{8,9},{9,8},{10,11... | collective-permute-start | bytes 3538952 | tf_op jit(solution)/shard_map/ppermute | solution.py:643
  128.6 30.8 %collective-permute-start.28 = (bf16[256,768]{1,0:T(8,128)(2,1)S(1)}, bf16[256,768]{1,0:T(8,128)(2,1)S(1)}, u32[]{:S(2)}, u32[]{:S(2)}) collective-permute-start(bf16[256,768]{1,0:T(8,128)(2,1)S(1)} %get-tuple-element.141.refs_15_.refs_2_), channel_id=1, source_target_pairs={{0,2},{1,3},{2,0},{3,1},{4,6},{5,7},{6,4},{7,5},{8,10},{9,11},{10,... | collective-permute-start | bytes 1179656 | tf_op jit(solution)/shard_map/ppermute | solution.py:643
  134.7 29.9 %collective-permute-start.27 = (bf16[384,768]{1,0:T(8,128)(2,1)S(1)}, bf16[384,768]{1,0:T(8,128)(2,1)S(1)}, u32[]{:S(2)}, u32[]{:S(2)}) collective-permute-start(bf16[384,768]{1,0:T(8,128)(2,1)S(1)} %get-tuple-element.148.refs_9_), channel_id=1, source_target_pairs={{0,4},{4,0},{8,12},{12,8},{16,20},{20,16},{24,28},{28,24},{1,5},{5... | collective-permute-start | bytes 1769480 | tf_op jit(solution)/shard_map/ppermute | solution.py:643
  138.4 26.7 %collective-permute-start.26 = (bf16[384,768]{1,0:T(8,128)(2,1)S(1)}, bf16[384,768]{1,0:T(8,128)(2,1)S(1)}, u32[]{:S(2)}, u32[]{:S(2)}) collective-permute-start(bf16[384,768]{1,0:T(8,128)(2,1)S(1)} %get-tuple-element.150.refs_14_), channel_id=1, source_target_pairs={{0,4},{4,0},{8,12},{12,8},{16,20},{20,16},{24,28},{28,24},{1,5},{5... | collective-permute-start | bytes 1769480 | tf_op jit(solution)/shard_map/ppermute | solution.py:643
  164.4 7.4 %collective-permute-start.31 = (bf16[2,256,384]{2,1,0:T(8,128)(2,1)S(1)}, bf16[2,256,384]{2,1,0:T(8,128)(2,1)S(1)}, u32[]{:S(2)}, u32[]{:S(2)}) collective-permute-start(bf16[2,256,384]{2,1,0:T(8,128)(2,1)S(1)} %get-tuple-element.166.refs_3_), channel_id=1, source_target_pairs={{0,1},{1,0},{2,3},{3,2},{4,5},{5,4},{6,7},{7,6},{8,9},{9,8},{10,11... | collective-permute-start | bytes 1179656 | tf_op jit(solution)/shard_map/ppermute | solution.py:643
  173.4 3.4 %collective-permute-start.34 = (bf16[768,512]{1,0:T(8,128)(2,1)S(1)}, bf16[768,512]{1,0:T(8,128)(2,1)S(1)}, u32[]{:S(2)}, u32[]{:S(2)}) collective-permute-start(bf16[768,512]{1,0:T(8,128)(2,1)S(1)} %get-tuple-element.184), channel_id=1, source_target_pairs={{0,1},{1,0},{2,3},{3,2},{4,5},{5,4},{6,7},{7,6},{8,9},{9,8},{10,11... | collective-permute-start | bytes 2359304 | tf_op jit(solution)/shard_map/ppermute | solution.py:643
  173.9 2.8 %collective-permute-start.33 = (bf16[512,640]{1,0:T(8,128)(2,1)S(1)}, bf16[512,640]{1,0:T(8,128)(2,1)S(1)}, u32[]{:S(2)}, u32[]{:S(2)}) collective-permute-start(bf16[512,640]{1,0:T(8,128)(2,1)S(1)} %get-tuple-element.183), channel_id=1, source_target_pairs={{0,1},{1,0},{2,3},{3,2},{4,5},{5,4},{6,7},{7,6},{8,9},{9,8},{10,11... | collective-permute-start | bytes 1966088 | tf_op jit(solution)/shard_map/ppermute | solution.py:643
  174.0 37.2 %collective-permute-start.30 = (bf16[512,768]{1,0:T(8,128)(2,1)S(1)}, bf16[512,768]{1,0:T(8,128)(2,1)S(1)}, u32[]{:S(2)}, u32[]{:S(2)}) collective-permute-start(bf16[512,768]{1,0:T(8,128)(2,1)S(1)} %get-tuple-element.165.refs_12_.refs_2_), channel_id=1, source_target_pairs={{0,2},{1,3},{2,0},{3,1},{4,6},{5,7},{6,4},{7,5},{8,10},{9,11},{10,... | collective-permute-start | bytes 2359304 | tf_op jit(solution)/shard_map/ppermute | solution.py:643
  175.1 9.8 %collective-permute-start.36 = (bf16[192,768]{1,0:T(8,128)(2,1)S(1)}, bf16[192,768]{1,0:T(8,128)(2,1)S(1)}, u32[]{:S(2)}, u32[]{:S(2)}) collective-permute-start(bf16[192,768]{1,0:T(8,128)(2,1)S(1)} %get-tuple-element.167.refs_3_), channel_id=1, source_target_pairs={{0,8},{4,12},{8,0},{12,4},{16,24},{20,28},{24,16},{28,20},{1,9},{5... | collective-permute-start | bytes 884744 | tf_op jit(solution)/shard_map/ppermute | solution.py:643
  180.2 13.4 %collective-permute-start.38 = (bf16[384,512]{1,0:T(8,128)(2,1)S(1)}, bf16[384,512]{1,0:T(8,128)(2,1)S(1)}, u32[]{:S(2)}, u32[]{:S(2)}) collective-permute-start(bf16[384,512]{1,0:T(8,128)(2,1)S(1)} %get-tuple-element.189.refs_3_), channel_id=1, source_target_pairs={{0,4},{4,0},{8,12},{12,8},{16,20},{20,16},{24,28},{28,24},{1,5},{5... | collective-permute-start | bytes 1179656 | tf_op jit(solution)/shard_map/ppermute | solution.py:643
  180.8 9.8 %collective-permute-start.39 = (bf16[192,768]{1,0:T(8,128)(2,1)S(1)}, bf16[192,768]{1,0:T(8,128)(2,1)S(1)}, u32[]{:S(2)}, u32[]{:S(2)}) collective-permute-start(bf16[192,768]{1,0:T(8,128)(2,1)S(1)} %get-tuple-element.168.refs_3_), channel_id=1, source_target_pairs={{0,8},{4,12},{8,0},{12,4},{16,24},{20,28},{24,16},{28,20},{1,9},{5... | collective-permute-start | bytes 884744 | tf_op jit(solution)/shard_map/ppermute | solution.py:643
  181.7 19.6 %collective-permute-start.35 = (bf16[384,384]{1,0:T(8,128)(2,1)S(1)}, bf16[384,384]{1,0:T(8,128)(2,1)S(1)}, u32[]{:S(2)}, u32[]{:S(2)}) collective-permute-start(bf16[384,384]{1,0:T(8,128)(2,1)S(1)} %get-tuple-element.187), channel_id=1, source_target_pairs={{0,4},{4,0},{8,12},{12,8},{16,20},{20,16},{24,28},{28,24},{1,5},{5... | collective-permute-start | bytes 884744 | tf_op jit(solution)/shard_map/ppermute | solution.py:643
  184.9 26.3 %collective-permute-start.32 = (bf16[256,768]{1,0:T(8,128)(2,1)S(1)}, bf16[256,768]{1,0:T(8,128)(2,1)S(1)}, u32[]{:S(2)}, u32[]{:S(2)}) collective-permute-start(bf16[256,768]{1,0:T(8,128)(2,1)S(1)} %get-tuple-element.180.refs_7_.refs_5_), channel_id=1, source_target_pairs={{0,2},{1,3},{2,0},{3,1},{4,6},{5,7},{6,4},{7,5},{8,10},{9,11},{10,... | collective-permute-start | bytes 1179656 | tf_op jit(solution)/shard_map/ppermute | solution.py:643
  185.5 14.1 %copy-start.23 = (f32[768,96]{0,1:T(8,128)S(1)}, f32[768,96]{0,1:T(8,128)}, u32[]{:S(2)}) copy-start(f32[768,96]{0,1:T(8,128)} %param.33) | copy-start | bytes 884740
  185.5 14.1 %copy-start.24 = (f32[768,96]{0,1:T(8,128)S(1)}, f32[768,96]{0,1:T(8,128)}, u32[]{:S(2)}) copy-start(f32[768,96]{0,1:T(8,128)} %param.38) | copy-start | bytes 884740
  190.5 9.0 %collective-permute-start.37 = (bf16[96,768]{1,0:T(8,128)(2,1)S(1)}, bf16[96,768]{1,0:T(8,128)(2,1)S(1)}, u32[]{:S(2)}, u32[]{:S(2)}) collective-permute-start(bf16[96,768]{1,0:T(8,128)(2,1)S(1)} %get-tuple-element.191.refs_3_), channel_id=1, source_target_pairs={{0,16},{4,20},{8,24},{12,28},{16,0},{20,4},{24,8},{28,12},{1,17},{... | collective-permute-start | bytes 442376 | tf_op jit(solution)/shard_map/ppermute | solution.py:643
  194.3 14.8 %collective-permute-start.41 = (bf16[192,512]{1,0:T(8,128)(2,1)S(1)}, bf16[192,512]{1,0:T(8,128)(2,1)S(1)}, u32[]{:S(2)}, u32[]{:S(2)}) collective-permute-start(bf16[192,512]{1,0:T(8,128)(2,1)S(1)} %get-tuple-element.195.refs_6_), channel_id=1, source_target_pairs={{0,8},{4,12},{8,0},{12,4},{16,24},{20,28},{24,16},{28,20},{1,9},{5... | collective-permute-start | bytes 589832 | tf_op jit(solution)/shard_map/ppermute | solution.py:643
  199.5 7.8 %collective-permute-start.42 = (bf16[96,768]{1,0:T(8,128)(2,1)S(1)}, bf16[96,768]{1,0:T(8,128)(2,1)S(1)}, u32[]{:S(2)}, u32[]{:S(2)}) collective-permute-start(bf16[96,768]{1,0:T(8,128)(2,1)S(1)} %get-tuple-element.194.refs_3_), channel_id=1, source_target_pairs={{0,16},{4,20},{8,24},{12,28},{16,0},{20,4},{24,8},{28,12},{1,17},{... | collective-permute-start | bytes 442376 | tf_op jit(solution)/shard_map/ppermute | solution.py:643
  202.8 7.7 %collective-permute-start.40 = (bf16[192,384]{1,0:T(8,128)(2,1)S(1)}, bf16[192,384]{1,0:T(8,128)(2,1)S(1)}, u32[]{:S(2)}, u32[]{:S(2)}) collective-permute-start(bf16[192,384]{1,0:T(8,128)(2,1)S(1)} %get-tuple-element.198.refs_6_), channel_id=1, source_target_pairs={{0,8},{4,12},{8,0},{12,4},{16,24},{20,28},{24,16},{28,20},{1,9},{5... | collective-permute-start | bytes 442376 | tf_op jit(solution)/shard_map/ppermute | solution.py:643
  212.2 12.5 %collective-permute-start.43 = (f32[768,768]{1,0:T(8,128)S(1)}, f32[768,768]{1,0:T(8,128)S(1)}, u32[]{:S(2)}, u32[]{:S(2)}) collective-permute-start(f32[768,768]{1,0:T(8,128)S(1)} %add_in.1.refs_14_.refs_1_), channel_id=1, source_target_pairs={{0,1},{1,0},{2,3},{3,2},{4,5},{5,4},{6,7},{7,6},{8,9},{9,8},{10,11... | collective-permute-start | bytes 7077896 | tf_op jit(solution)/shard_map/ppermute | solution.py:643
  212.3 10.4 %collective-permute-start.45 = (bf16[96,512]{1,0:T(8,128)(2,1)S(1)}, bf16[96,512]{1,0:T(8,128)(2,1)S(1)}, u32[]{:S(2)}, u32[]{:S(2)}) collective-permute-start(bf16[96,512]{1,0:T(8,128)(2,1)S(1)} %get-tuple-element.202.refs_3_), channel_id=1, source_target_pairs={{0,16},{4,20},{8,24},{12,28},{16,0},{20,4},{24,8},{28,12},{1,17},{... | collective-permute-start | bytes 294920 | tf_op jit(solution)/shard_map/ppermute | solution.py:643
  212.9 9.7 %collective-permute-start.44 = (bf16[96,384]{1,0:T(8,128)(2,1)S(1)}, bf16[96,384]{1,0:T(8,128)(2,1)S(1)}, u32[]{:S(2)}, u32[]{:S(2)}) collective-permute-start(bf16[96,384]{1,0:T(8,128)(2,1)S(1)} %get-tuple-element.203.refs_7_), channel_id=1, source_target_pairs={{0,16},{4,20},{8,24},{12,28},{16,0},{20,4},{24,8},{28,12},{1,17},{... | collective-permute-start | bytes 221192 | tf_op jit(solution)/shard_map/ppermute | solution.py:643
  (41 other events, 312.2 us)

commit v3 on v2

--- a/solution.py
+++ b/solution.py
@@ -41,7 +41,7 @@
     def __init__(self):
         self.last = None
 
-    def call(self, body, outs, ins, info, name, scratch=(), limit=20, raw_in=False, raw_out=False, deps=(), warm=(), free=False):
+    def call(self, body, outs, ins, info, name, scratch=(), limit=12, raw_in=False, raw_out=False, deps=(), warm=(), free=False):
         ins = list(ins)
         n = len(ins) + 1
         specs = [pl.BlockSpec(memory_space=pltpu.SMEM)]
@@ -50,25 +50,28 @@
         specs += [pl.BlockSpec(memory_space=VM)] * len(warm)
         specs += [pl.BlockSpec(memory_space=pl.ANY)] * (len(extra) - len(warm))
 
+        single = not isinstance(outs, (list, tuple))
+        shapes = ([outs] if single else list(outs)) + [sds((8, 128), F32)]
+        specs_out = [pl.BlockSpec(memory_space=pltpu.HBM if raw_out else VM)] * (len(shapes) - 1) + [pl.BlockSpec(memory_space=VM)]
+        token = n + len(extra) + len(shapes) - 1
+
         def run(*refs):
-            body(*refs[:n], *refs[n + len(extra) :])
-
-        single = not isinstance(outs, (list, tuple))
-        shapes = outs if single else list(outs)
-        spec = pl.BlockSpec(memory_space=pltpu.HBM if raw_out else VM)
+            body(*refs[:n], *refs[n + len(extra) : token], *refs[token + 1 :])
+            refs[token][...] = jnp.zeros((8, 128), F32)
+
         res = pl.pallas_call(
             run,
             out_shape=shapes,
             in_specs=specs,
-            out_specs=spec if single else [spec] * len(shapes),
+            out_specs=specs_out,
             scratch_shapes=list(scratch),
             compiler_params=pltpu.CompilerParams(vmem_limit_bytes=limit * 1024 * 1024),
             cost_estimate=pl.CostEstimate(flops=1, bytes_accessed=1, transcendentals=0),
             name=name,
         )(info, *ins, *extra)
         if not free:
-            self.last = res if single else res[-1]
-        return res
+            self.last = res[-1]
+        return res[0] if single else list(res[:-1])
 
 
 def low_of(info):
@@ -304,58 +307,46 @@
     return jnp.concatenate(cols, axis=0)
 
 
-def turn(order, info, kind, normed, part, there, go, weights, norms, u0, u1, d0, d1, slope, name, below=None, **kw):
-    rows, width = normed.shape
-    n = len(part)
-    skip = 0 if below is None else below.shape[0]
+def turn(order, info, kind, row, normed, part, there, go, weights, norms, u0, u1, d0, d1, slope, name, around=(), before=None, **kw):
+    width = normed.shape[1]
     units = d0.shape[1]
-    both = 2 * units
-
-    def body(sc, nm, g, sw, nr, u0, u1, d0, d1, sl, *refs):
-        parts, refs = refs[: 2 * n], refs[2 * n :]
-        if n > 1:
-            p0, p1 = refs[-2:]
-            refs = refs[:-2]
-            for k in range(n):
-                p0[k * CHUNK : (k + 1) * CHUNK, :] = parts[k][...]
-                p1[k * CHUNK : (k + 1) * CHUNK, :] = parts[n + k][...]
+    skip = around[0].shape[0] if around else 0
+    total = skip + CHUNK + (around[1].shape[0] if around else 0)
+
+    def body(sc, nm, g, sw, nr, u0, u1, d0, d1, sl, p0, p1, *refs):
+        out_ref, two_ref, own_ref, send_ref, sums_ref, part_ref = refs[-6:]
+        if around:
+            out_ref[:skip, :] = refs[0][...]
+            out_ref[skip + CHUNK :, :] = refs[1][...]
+        at = slice(row, row + CHUNK)
+        ffn = p0[...].astype(F32) + p1[...].astype(F32)
+        n2, inv2 = norm_stats((nm[at, :] * nr[0:1, :] + nr[1:2, :]) + ffn)
+        out_ref[skip : skip + CHUNK, :] = (n2 * nr[2:3, :] + nr[3:4, :]).astype(BF)
+        up = g[pl.ds(pl.multiple_of(first_row(sc, kind) + row, CHUNK), CHUNK), :].astype(F32) * row_scale(sc, sw, kind, row)
+        two = norm_pull(up, n2, inv2, nr[2:3, :])
+        sums_ref[0:1, :] = jnp.sum(up * n2, axis=0, keepdims=True)
+        sums_ref[1:2, :] = jnp.sum(up, axis=0, keepdims=True)
+        two_ref[...] = two
+        send_ref[:, :width] = two.astype(BF)
+        acc = None
+        for t, (u, d) in enumerate(((u0, d0), (u1, d1))):
+            to, base = ((own_ref, 0), (send_ref, width))[t]
+            for c in range(0, units, 256):
+                lanes = slice(base + c, base + c + 256)
+                steep = sl[at, t * units + c : t * units + c + 256]
+                to[:, lanes] = (dot_nn(send_ref[:, :width], d[:, c : c + 256]) * steep).astype(BF)
+                piece = dot_nt(to[:, lanes], u[:, c : c + 256])
+                acc = piece if acc is None else acc + piece
+        if before is None:
+            part_ref[...] = acc.astype(BF)
         else:
-            p0, p1 = parts
-        out_ref, two_ref, own_ref, send_ref, sums_ref, part_ref = refs[-6:]
-        if skip:
-            out_ref[rows:, :] = refs[0][...]
-        sums_ref[...] = jnp.zeros((8, width), F32)
-        top = first_row(sc, kind)
-
-        def step(r):
-            at = pl.ds(r, CHUNK)
-            ffn = p0[at, :].astype(F32) + p1[at, :].astype(F32)
-            n2, inv2 = norm_stats((nm[at, :] * nr[0:1, :] + nr[1:2, :]) + ffn)
-            out_ref[at, :] = (n2 * nr[2:3, :] + nr[3:4, :]).astype(BF)
-            up = g[pl.ds(pl.multiple_of(top + r, CHUNK), CHUNK), :].astype(F32) * row_scale(sc, sw, kind, r)
-            two = norm_pull(up, n2, inv2, nr[2:3, :])
-            sums_ref[0:1, :] += jnp.sum(up * n2, axis=0, keepdims=True)
-            sums_ref[1:2, :] += jnp.sum(up, axis=0, keepdims=True)
-            two_ref[at, :] = two
-            send_ref[at, :width] = two.astype(BF)
-            acc = None
-            for t, (u, d) in enumerate(((u0, d0), (u1, d1))):
-                to = (own_ref, send_ref)[t]
-                for c in range(0, units, 256):
-                    lanes = slice(t * width + c, t * width + c + 256)
-                    slope = sl[at, t * units + c : t * units + c + 256]
-                    to[at, lanes] = (dot_nn(send_ref[at, :width], d[:, c : c + 256]) * slope).astype(BF)
-                    piece = dot_nt(to[at, lanes], u[:, c : c + 256])
-                    acc = piece if acc is None else acc + piece
-            part_ref[at, :] = acc.astype(BF)
-
-        by_chunk(rows, step)
-
-    outs = [sds((rows + skip, width)), sds((rows, width), F32), sds((rows, units)), sds((rows, width + units))]
-    outs += [sds((8, width), F32), sds((rows, width))]
-    ins = [normed, go, weights, norms, u0, u1, d0, d1, slope, *part, *there] + ([] if below is None else [below])
-    scratch = [VM((rows, width), BF)] * (2 if n > 1 else 0)
-    return order.call(body, outs, ins, info, name, scratch=scratch, **kw)
+            part_ref[:CHUNK, :] = refs[-7][...]
+            part_ref[CHUNK:, :] = acc.astype(BF)
+
+    outs = [sds((total, width)), sds((CHUNK, width), F32), sds((CHUNK, units)), sds((CHUNK, width + units))]
+    outs += [sds((8, width), F32), sds((CHUNK if before is None else 2 * CHUNK, width))]
+    ins = [normed, go, weights, norms, u0, u1, d0, d1, slope, part, there, *around] + ([] if before is None else [before])
+    return order.call(body, outs, ins, info, name, **kw)
 
 
 def split_sides(info, whole, away, here):
@@ -368,7 +359,13 @@
 
 
 def grads(order, info, pairs, width, units, name, split=True, **kw):
-    flat = [x for p in pairs for x in (p[0], p[2])]
+    flat = []
+    for p in pairs:
+        flat += [x for x in (p[0], p[3]) if not any(x is y for y in flat)]
+
+    def place_of(x):
+        return next(k for k, y in enumerate(flat) if x is y)
+
 
     def body(sc, *refs):
         ins, outs = refs[: len(flat)], refs[len(flat) :]
@@ -377,9 +374,9 @@
         @pl.loop(0, width // 256)
         def _(i):
             acc = None
-            for k, (_, first, _, column) in enumerate(pairs):
-                left = ins[2 * k][:, pl.ds(pl.multiple_of(first + i * 256, 256), 256)]
-                piece = dot_tn(left, ins[2 * k + 1][:, column : column + units])
+            for x, top, first, y, row, column in pairs:
+                left = ins[place_of(x)][top : top + CHUNK, pl.ds(pl.multiple_of(first + i * 256, 256), 256)]
+                piece = dot_tn(left, ins[place_of(y)][row : row + CHUNK, column : column + units])
                 acc = piece if acc is None else acc + piece
             whole[pl.ds(pl.multiple_of(i * 256, 256), 256), :] = acc
 
@@ -399,11 +396,15 @@
     width = norms.shape[1]
     whole = kind == "a"
 
-    def body(sc, two_ref, p0, p1, nm, inv, nr, o_ref, q_ref, k_ref, v_ref, lse_ref, *refs):
+    n = rows // CHUNK
+
+    def body(sc, *refs):
+        twos, p0, p1, refs = refs[:n], refs[n], refs[n + 1], refs[n + 2 :]
+        nm, inv, nr, o_ref, q_ref, k_ref, v_ref, lse_ref, *refs = refs
         if whole:
             w0, w1, one_ref, low_ref, pg0, pg1, sums_ref, part_ref, cg_ref, kv_ref, lt_ref, dq_ref = refs
         else:
-            one_ref, low_ref, sums_ref, dq_ref, mine_ref, there_ref, cg_ref, kv_ref, lt_ref = refs
+            one_ref, low_ref, sums_ref, dq_ref, mine_ref, send_ref, cg_ref, kv_ref, lt_ref = refs
         low = low_of(sc)
         sums_ref[...] = jnp.zeros((8, width), F32)
         keys = lax.broadcasted_iota(jnp.int32, (kv_rows, 1), 0)
@@ -412,24 +413,30 @@
             kv_ref[...] = jnp.zeros((2, kv_rows, 2 * local), F32)
 
         def step(r):
-            at = pl.ds(r, CHUNK)
+            at, i = slice(r, r + CHUNK), r // CHUNK
             nrm = nm[at, :]
-            grad = two_ref[at, :] + (p0[at, :].astype(F32) + p1[at, :].astype(F32))
+            grad = twos[i][...] + (p0[at, :].astype(F32) + p1[at, :].astype(F32))
             sums_ref[0:1, :] += jnp.sum(grad * nrm, axis=0, keepdims=True)
             sums_ref[1:2, :] += jnp.sum(grad, axis=0, keepdims=True)
             one = norm_pull(grad, nrm, inv[at, :1], nr[0:1, :])
             one_ref[at, :] = one
             low_ref[at, :] = one.astype(BF)
             for t in range(2):
-                cg_ref[t] = dot_nn(low_ref[at, :], o_ref[:, t * local : (t + 1) * local]).astype(BF)
-                lt_ref[t] = jnp.transpose(lse_ref[t, at, :])[:8, :]
+                cg_ref[t, at, :] = dot_nn(low_ref[at, :], o_ref[:, t * local : (t + 1) * local]).astype(BF)
+                lt_ref[t, i] = jnp.transpose(lse_ref[t, at, :])[:8, :]
+
+        for r in range(0, rows, CHUNK):
+            step(r)
+
+        def heads_of(r):
+            at, i = pl.ds(r, CHUNK), lax.div(r, CHUNK)
 
             @pl.loop(0, 2)
             def _(t):
                 for h in range(heads):
                     lanes = slice(h * HD, (h + 1) * HD)
-                    qh, kh, cg = q_ref[t, at, lanes], k_ref[t, :, lanes], cg_ref[t, :, lanes]
-                    p = jnp.exp(dot_nt(kh, qh) + bias - lt_ref[t, h : h + 1, :])
+                    qh, kh, cg = q_ref[t, at, lanes], k_ref[t, :, lanes], cg_ref[t, at, lanes]
+                    p = jnp.exp(dot_nt(kh, qh) + bias - lt_ref[t, i, h : h + 1, :])
                     dp = dot_nt(v_ref[t, :, lanes], cg)
                     ds = (p * (dp - jnp.sum(dp * p, axis=0, keepdims=True))).astype(BF)
                     dv = dot_nn(p.astype(BF), cg)
@@ -443,7 +450,7 @@
                         kv_ref[t, :, lanes] = dk
                         kv_ref[t, :, late] = dv
 
-        by_chunk(rows, step)
+        by_chunk(rows, heads_of)
         if whole:
             for t, pg in enumerate((pg0, pg1)):
                 pg[:, :local] = dq_ref[t]
@@ -457,39 +464,40 @@
 
             by_chunk(rows, last)
         else:
+            own = pl.ds(pl.multiple_of(low * CHUNK, CHUNK), CHUNK)
+            other = pl.ds(pl.multiple_of((1 - low) * CHUNK, CHUNK), CHUNK)
             for t in range(2):
-                mine_ref[t] = kv_ref[t, pl.ds(pl.multiple_of(low * CHUNK, CHUNK), CHUNK), :]
-                there_ref[t] = kv_ref[t, pl.ds(pl.multiple_of((1 - low) * CHUNK, CHUNK), CHUNK), :].astype(BF)
+                mine_ref[t] = kv_ref[t, own, :]
+            for k, (t, at) in enumerate(((1, own), (1, other), (0, other))):
+                send_ref[k * CHUNK : (k + 1) * CHUNK, :] = kv_ref[t, at, :].astype(BF)
+            for k in range(2):
+                send_ref[3 * CHUNK :, k * local : (k + 1) * local] = dq_ref[1, k * 128 : (k + 1) * 128, :]
 
     outs = [sds((rows, width), F32), sds((rows, width))]
-    scratch = [VM((2, CHUNK, local), BF), VM((2, kv_rows, 2 * local), F32), VM((2, 8, CHUNK), F32)]
+    scratch = [VM((2, rows, local), BF), VM((2, kv_rows, 2 * local), F32), VM((2, n, 8, CHUNK), F32)]
     if whole:
         outs += [sds((rows, 3 * local)), sds((rows, 3 * local + -(3 * local) % 128)), sds((8, width), F32), sds((rows, width))]
         scratch += [VM((2, rows, local), BF)]
     else:
-        outs += [sds((8, width), F32), sds((2, rows, local)), sds((2, CHUNK, 2 * local), F32), sds((2, CHUNK, 2 * local))]
-    ins = [two, part, there, normed, inverse, norms, o_here, q, k, v, lse] + (list(weights) if whole else [])
+        outs += [sds((8, width), F32), sds((2, rows, local)), sds((2, CHUNK, 2 * local), F32), sds((3 * CHUNK + 128, 2 * local))]
+    ins = [*two, part, there, normed, inverse, norms, o_here, q, k, v, lse] + (list(weights) if whole else [])
     return order.call(body, outs, ins, info, name, scratch=scratch, **kw)
 
 
-def project_back(order, info, dq, mine, there, w_own, w_oth, out_oth, local, name, **kw):
+def project_back(order, info, dq, mine, got, w_own, w_oth, local, name, **kw):
     rows, width = dq.shape[1], w_own.shape[0]
 
-    def body(sc, dq_ref, a, b, w0, w1, o, pg0, send_ref, part_ref, pg1):
+    def body(sc, dq_ref, a, g, w0, w1, part_ref, pg):
         acc = None
-        send_ref[:, local:] = o[...]
-        for t, (w, pg) in enumerate(((w0, pg0), (w1, pg1))):
+        for t, w in enumerate((w0, w1)):
             pg[:, :local] = dq_ref[t]
-            pg[:, local:] = (a[t] + b[1 - t].astype(F32)).astype(BF)
+            pg[:, local:] = (a[t] + g[(t + 1) * CHUNK : (t + 2) * CHUNK, :].astype(F32)).astype(BF)
             piece = dot_nt(pg[...], w[:, : 3 * local])
             acc = piece if acc is None else acc + piece
         part_ref[...] = acc.astype(BF)
-        for c in range(3):
-            send_ref[c * rows : (c + 1) * rows, :local] = pg1[:, c * local : (c + 1) * local]
-
-    outs = [sds((rows, 3 * local)), sds((3 * rows, local + out_oth.shape[1])), sds((rows, width))]
+
     scratch = [VM((rows, 3 * local), BF)]
-    return order.call(body, outs, [dq, mine, there, w_own, w_oth, out_oth], info, name, scratch=scratch, **kw)
+    return order.call(body, sds((rows, width)), [dq, mine, got, w_own, w_oth], info, name, scratch=scratch, **kw)
 
 
 def grads_out(order, info, lows, ctxs, sums, local, **kw):
@@ -514,44 +522,52 @@
                     piece = dot_tn(x[:, rr], y[:, t * local : (t + 1) * local])
                     acc = piece if acc is None else acc + piece
                 o[rr, :local] = acc.astype(o.dtype)
-                o[rr, local:] = cols_ref[rr, :].astype(o.dtype)
+                o[rr, local : local + 128] = cols_ref[rr, :].astype(o.dtype)
+                o[rr, local + 128 :] = jnp.zeros((256, 64), o.dtype)
 
     ins = list(lows) + list(ctxs) + list(sums[0]) + list(sums[1])
-    outs = [sds((width, local + 128), d) for d in (F32, BF)]
+    outs = [sds((width, local + 192), d) for d in (F32, BF)]
     return order.call(body, outs, ins, info, "grads_out", scratch=[VM((width, 128), BF)], **kw)
 
 
-def grads_attn(order, info, tokens, mine, there, out_mine, split=True, **kw):
-    width, local = tokens.shape[1], mine[0].shape[1] // 3
-    full, cut = 4 * local + 128, 2 * local
-
-    def body(sc, tok, ma, mc, ta, tc, om, *outs):
-        whole = outs[-1]
+def grads_attn(order, info, tokens, pg_a, got_a, dq, mine, sent, got, split=True, **kw):
+    width, local = tokens.shape[1], pg_a.shape[1] // 3
+    full = 3 * local + -(3 * local) % 128
+
+    def body(sc, tok, ma, ta, q, m, s, g, *outs):
+        *outs, whole, here, there = outs
+        here[:, :local] = q[0]
+        here[:, local:] = (m[0] + g[CHUNK : 2 * CHUNK, :].astype(F32)).astype(BF)
+        for k in range(2):
+            there[k * 128 : (k + 1) * 128, :local] = g[3 * CHUNK :, k * local : (k + 1) * local]
+        there[:, local:] = (s[2 * CHUNK : 3 * CHUNK, :].astype(F32) + g[:CHUNK, :].astype(F32)).astype(BF)
         at = {k: pl.ds(first_row(sc, *k), rows_of(k[0])) for k in (("a", False), ("c", False), ("a", True), ("c", True))}
-        pairs = [(at["a", False], ma), (at["c", False], mc), (at["a", True], ta)]
+        pairs = [(at["a", False], ma), (at["c", False], here), (at["a", True], ta), (at["c", True], there)]
 
         @pl.loop(0, width // 256)
         def _(i):
             rr = pl.ds(pl.multiple_of(i * 256, 256), 256)
-            acc = sum(dot_tn(tok[rows, rr], ref[:, : 3 * local]) for rows, ref in pairs)
-            last = tok[at["c", True], rr]
-            for c in range(3):
-                lanes = slice(c * local, (c + 1) * local)
-                whole[rr, lanes] = acc[:, lanes] + dot_tn(last, tc[c * CHUNK : (c + 1) * CHUNK, :local])
-            whole[rr, 3 * local :] = om[rr, :] + tc[rr, local:].astype(F32)
+            whole[rr, : 3 * local] = sum(dot_tn(tok[rows, rr], ref[:, : 3 * local]) for rows, ref in pairs)
+            whole[rr, 3 * local :] = jnp.zeros((256, full - 3 * local), F32)
 
         if split:
-            here_1, away_1, here_2, away_2 = outs[:-1]
-            split_sides(sc, whole.at[:, :cut], away_1, here_1)
-            split_sides(sc, whole.at[:, cut:], away_2, here_2)
-
-    ins = [tokens, *mine, *there, out_mine]
-    if split:
-        outs = [sds((width // 2, w), d) for w in (cut, full - cut) for d in (F32, BF)]
-        scratch = [VM((width, full), F32)]
-    else:
-        outs, scratch = sds((width, full), F32), []
-    return order.call(body, outs, ins, info, "grads_attn", scratch=scratch, **kw)
+            split_sides(sc, whole, outs[1], outs[0])
+        else:
+            outs[0][...] = whole[...]
+
+    outs = [sds((width // 2, full), d) for d in (F32, BF)] if split else sds((width, full), F32)
+    scratch = [VM((width, full), F32), VM((CHUNK, 3 * local), BF), VM((CHUNK, 3 * local), BF)]
+    return order.call(body, outs, [tokens, pg_a, got_a, dq, mine, sent, got], info, "grads_attn", scratch=scratch, **kw)
+
+
+def fold_both(order, info, mine, there, name, **kw):
+    def body(sc, a, b, here, away, whole):
+        whole[...] = a[...] + b[...].astype(F32)
+        split_sides(sc, whole, away, here)
+
+    rows, width = mine.shape
+    outs = [sds((rows // 2, width), d) for d in (F32, BF)]
+    return order.call(body, outs, [mine, there], info, name, scratch=[VM((rows, width), F32)], **kw)
 
 
 def fold_pair(order, info, mine, there, name, **kw):
@@ -722,16 +738,21 @@
         got_hi_a, got_hi_c = core_swap(sent_a), core_swap(sent_c)
         args = (grad_out, weights, norms, u_own, u_oth, d_own, d_oth)
         res_c, two_c, up_c, fu_c, sums_c2, back_c = turn(
-            order, info, "c", normed_c, part_c, part_c_there, *args, slope_c, "turn_c", deps=[got_hi_a, got_hi_c])
-        result, two_a, up_a, fu_a, sums_a2, back_a = turn(
-            order, info, "a", normed_a, part_a, part_a_there, *args, slope_a, "turn_a", below=res_c)
-        back_a_there = far_swap(back_a)
-        back_c_there = far_swap(back_c)
-        got_fu_a, got_fu_c = core_swap(fu_a), core_swap(fu_c)
+            order, info, "c", 0, normed_c, part_c[0], part_c_there[0], *args, slope_c, "turn_c", deps=[got_hi_a, got_hi_c])
+        res_0, two_0, up_0, fu_0, sums_02, back_0 = turn(
+            order, info, "a", 0, normed_a, part_a[0], part_a_there[0], *args, slope_a, "turn_0")
+        result, two_1, up_1, fu_1, sums_12, back_a = turn(
+            order, info, "a", CHUNK, normed_a, part_a[1], part_a_there[1], *args, slope_a, "turn_1", around=(res_0, res_c), before=back_0)
+        back_a_there, back_c_there = far_swap(back_a), far_swap(back_c)
+        fus = (fu_0, fu_1, fu_c)
+        got_fus = [core_swap(x) for x in fus]
         width = tokens.shape[1]
-        pairs = [(fu_a, 0, inner_a, 0), (fu_c, 0, inner_c, 0), (got_fu_a, 0, got_hi_a, width), (got_fu_c, 0, got_hi_c, width)]
+        inners, sents = ((inner_a, 0), (inner_a, CHUNK), (inner_c, 0)), ((sent_a, 0), (sent_a, CHUNK), (sent_c, 0))
+        gots = ((got_hi_a, 0), (got_hi_a, CHUNK), (got_hi_c, 0))
+        pairs = [(f, 0, 0, x, r, 0) for f, (x, r) in zip(fus, inners)] + [(f, 0, 0, x, r, width) for f, (x, r) in zip(got_fus, gots)]
         grad_d = grads(order, info, pairs, width, units, "grads_d", split=direct)
-        pairs = [(sent_a, 0, up_a, 0), (sent_c, 0, up_c, 0), (got_hi_a, 0, got_fu_a, width), (got_hi_c, 0, got_fu_c, width)]
+        ups = (up_0, up_1, up_c)
+        pairs = [(x, r, 0, u, 0, 0) for (x, r), u in zip(sents, ups)] + [(x, r, 0, f, 0, width) for (x, r), f in zip(gots, got_fus)]
         grad_u = grads(order, info, pairs, width, units, "grads_u", split=direct)
         res_there = core_swap(result)
 
@@ -745,58 +766,64 @@
 
         if direct:
             fold_d, fold_u = (grad_d[0], dp_swap(grad_d[1], 1)), (grad_u[0], dp_swap(grad_u[1], 1))
+        if direct:
+            fold_d = second_fold(fold_d, "d", deps=[back_a_there])
         one_a, low_a, pg_a, pg_a_oth, sums_a1, in_a = attend_back(
-            order, info, "a", two_a, back_a, back_a_there, normed_a, inv_a, norms, o_here, q_a, k_a, v_a, lse_a, (q_own, q_oth), local, "back_a")
+            order, info, "a", (two_0, two_1), back_a, back_a_there, normed_a, inv_a, norms, o_here, q_a, k_a, v_a, lse_a, (q_own, q_oth), local, "back_a")
         in_a_there = far_swap(in_a)
         got_a = core_swap(pg_a_oth)
-        one_c, low_c, sums_c1, dq_c, kv_mine, kv_there = attend_back(
-            order, info, "c", two_c, back_c, back_c_there, normed_c, inv_c, norms, o_here, q_c, k_c, v_c, lse_c, None, local, "back_c")
-        kv_got = core_swap(kv_there)
-        if direct:
-            fold_d = second_fold(fold_d, "d")
+        if direct:
+            fold_d = third_fold(fold_d, "d")
+        one_c, low_c, sums_c1, dq_c, kv_mine, sent = attend_back(
+            order, info, "c", (two_c,), back_c, back_c_there, normed_c, inv_c, norms, o_here, q_c, k_c, v_c, lse_c, None, local, "back_c")
+        got_c = core_swap(sent)
+        if direct:
             fold_u = second_fold(fold_u, "u")
-        res_full = lay_rows(order, info, [result], [res_there], "lay_out")
         out_mine, out_oth = grads_out(
-            order, info, (low_a, low_c), (ctx_a, ctx_c), ((sums_a1, sums_c1), (sums_a2, sums_c2)), local)
-        pg_c, sent, in_c = project_back(order, info, dq_c, kv_mine, kv_got, q_own, q_oth, out_oth, local, "project_c")
+            order, info, (low_a, low_c), (ctx_a, ctx_c), ((sums_a1, sums_c1), (sums_02, sums_12, sums_c2)), local)
+        out_got = core_swap(out_oth)
+        grad_a = grads_attn(order, info, tokens, pg_a, got_a, dq_c, kv_mine, sent, got_c, split=direct)
+        everything = slice(None)
+        if direct:
+            fold_1 = grad_a[0], dp_swap(grad_a[1], 1)
+            keep, send = fold_both(order, info, out_mine, out_got, "side_o")
+            fold_2 = keep, dp_swap(send, 1)
+        in_c = project_back(order, info, dq_c, kv_mine, got_c, q_own, q_oth, local, "project_c")
         in_c_there = far_swap(in_c)
-        got_c = core_swap(sent)
-        grad_a = grads_attn(order, info, tokens, (pg_a, pg_c), (got_a, got_c), out_mine, split=direct)
-        everything = slice(None)
-        if direct:
-            keep_1, send_1, keep_2, send_2 = grad_a
-            fold_1, fold_2 = (keep_1, dp_swap(send_1, 1)), (keep_2, dp_swap(send_2, 1))
-            fold_d = third_fold(fold_d, "d")
+        if direct:
             fold_u = third_fold(fold_u, "u")
-            fold_2 = second_fold(fold_2, "vo")
+            fold_1 = second_fold(fold_1, "qkv", deps=[fold_d[1]])
+            fold_2 = second_fold(fold_2, "o", deps=[fold_u[1]])
             n_down = update(order, rates, [fold_d], [
                 (down_t, first_down.T, second_down.T, DECAY_RATE, [(everything, 0, 0, units, False)])], "update_d")
-            fold_1 = second_fold(fold_1, "qk")
+            fold_1 = third_fold(fold_1, "qkv")
             n_up = update(order, rates, [fold_u], [
                 (up_weight, first_up, second_up, DECAY_RATE, [(everything, 0, 0, units, False)])], "update_u")
-            fold_2 = third_fold(fold_2, "vo")
-            fold_1 = third_fold(fold_1, "qk")
+            fold_2 = third_fold(fold_2, "o")
         gi = add_rows(order, info, [(one_a, in_a, in_a_there), (one_c, in_c, in_c_there)], "add_in")
         gi_there = core_swap(gi)
+        res_full = lay_rows(order, info, [result], [res_there], "lay_out")
+        input_grad = lay_rows(order, info, [gi], [gi_there], "lay_grad")
         if direct:
             res = update(order, rates, [fold_1, fold_2], [
                 (qkv_weight, first_qkv, second_qkv, DECAY_RATE,
-                 [(0, 0, 0, local, False), (1, 0, local, local, False), (2, 1, 0, local, False)]),
-                (out_weight, first_out, second_out, DECAY_RATE, [(everything, 1, local, local, True)]),
-                (norm_params, first_norm, second_norm, 0.0, [(everything, 1, 2 * local, 128, True)]),
+                 [(c, 0, c * local, local, False) for c in range(3)]),
+                (out_weight, first_out, second_out, DECAY_RATE, [(everything, 1, 0, local, True)]),
+                (norm_params, first_norm, second_norm, 0.0, [(everything, 1, local, 128, True)]),
             ], "update_a")
             n_down = [x.T for x in n_down]
             n_qkv, n_out, n_norm = res[:4], res[4:8], res[8:]
-        input_grad = lay_rows(order, info, [gi], [gi_there], "lay_grad")
         if not direct:
-            su, sd, sa = (lax.psum_scatter(x, "dp", scatter_dimension=0, tiled=True) for x in (grad_u, grad_d, grad_a))
+            grad_o = out_mine + out_got.astype(F32)
+            su, sd, sa, so = (
+                lax.psum_scatter(x, "dp", scatter_dimension=0, tiled=True) for x in (grad_u, grad_d, grad_a, grad_o))
             rest = (rate, fix_one, fix_two)
             n_up = adamw_update(su, up_weight, first_up, second_up, *rest, DECAY_RATE)
             n_down = adamw_update(sd.T, down_weight, first_down, second_down, *rest, DECAY_RATE)
             sq = jnp.stack([sa[:, c * local : (c + 1) * local] for c in range(3)])
             n_qkv = adamw_update(sq, qkv_weight, first_qkv, second_qkv, *rest, DECAY_RATE)
-            n_out = adamw_update(sa[:, 3 * local : 4 * local].T, out_weight, first_out, second_out, *rest, DECAY_RATE)
-            n_norm = adamw_update(sa[:, 4 * local : 4 * local + 4].T, norm_params, first_norm, second_norm, *rest, 0.0)
+            n_out = adamw_update(so[:, :local].T, out_weight, first_out, second_out, *rest, DECAY_RATE)
+            n_norm = adamw_update(so[:, local : local + 4].T, norm_params, first_norm, second_norm, *rest, 0.0)
         return (res_full, input_grad, *n_qkv, *n_out, *n_up, *n_down, *n_norm)
 
     rows = P("dp", None)

time: 229 us -> 219 us (0.956)
  waiting for transfers between devices: 81.4 us -> 73.4 us
  local copies, waits for them, and re-layouts: 11.8 us -> 5.07 us
  starting transfers between devices: 44.3 us -> 47.9 us
    ppermute x46 -> x47, waiting for transfers between devices: 81.4 us -> 73.4 us  [swap(): return lax.ppermute(x, axis, [(i, i ^ bit) for i in range(size)])]
    unnamed x86 -> x46, local copies, waits for them, and re-layouts: 11.8 us -> 5.07 us
    ppermute x46 -> x47, starting transfers between devices: 44.3 us -> 47.9 us  [swap(): return lax.ppermute(x, axis, [(i, i ^ bit) for i in range(size)])]
    pallas_call x39 -> x41, Pallas kernels: 87.6 us -> 89.1 us  [call(): pl.pallas_call(run, out_shape=shapes, in_specs=specs, out_specs=specs_out...]
  transfers between devices with their start and end apart: 46 -> 47, of which waited for: 18 -> 20; matrix products, arithmetic and copies ran while one was open for 0% -> 0% of each run, Pallas kernels for 32% -> 36%
where the time goes in v3:
time: 219 us; the launch traced here: 218 us
  Pallas kernels  89.1 us (41%)
  waiting for transfers between devices  73.4 us (34%)
  starting transfers between devices  47.9 us (22%)
  local copies, waits for them, and re-layouts  5.07 us (2%)
  between operations  2.24 us (1%)
    pallas_call x41, Pallas kernels, call(): pl.pallas_call(run, out_shape=shapes, in_specs=specs, out_specs=specs_out...  89.1 us
    ppermute x47, waiting for transfers between devices, swap(): return lax.ppermute(x, axis, [(i, i ^ bit) for i in range(size)])  73.4 us
    ppermute x47, starting transfers between devices, swap(): return lax.ppermute(x, axis, [(i, i ^ bit) for i in range(size)])  47.9 us
    unnamed x46, local copies, waits for them, and re-layouts  5.07 us
  transfers between devices with their start and end apart: 47, of which 20 were waited for; matrix products, arithmetic and copies ran while one was open for 0% of the time, Pallas kernels for 36%

profile of v3, /device:TPU:0, one launch (start us, length us, event | category | flops | bytes accessed | tf_op | source)
XLA Modules:
  0.0 218.5 jit_solution(4713447263933977597)
XLA Ops:
  4.1 3.0 %collective-permute-start.3 = (bf16[96,768]{1,0:T(8,128)(2,1)S(1)}, bf16[96,768]{1,0:T(8,128)(2,1)S(1)}, u32[]{:S(2)}, u32[]{:S(2)}) collective-permute-start(bf16[96,768]{1,0:T(8,128)(2,1)S(1)} %get-tuple-element.179.refs_1_), channel_id=1, source_target_pairs={{0,4},{4,0},{8,12},{12,8},{16,20},{20,16},{24,28},{28,24},{1,5},{5... | collective-permute-start | bytes 442376 | tf_op jit(solution)/shard_map/ppermute | solution.py:659
  7.1 1.6 collective-permute-start
  8.7 2.6 %collective-permute-start.1 = (bf16[96,768]{1,0:T(8,128)(2,1)S(1)}, bf16[96,768]{1,0:T(8,128)(2,1)S(1)}, u32[]{:S(2)}, u32[]{:S(2)}) collective-permute-start(bf16[96,768]{1,0:T(8,128)(2,1)S(1)} %get-tuple-element.179.refs_1_), channel_id=1, source_target_pairs={{0,16},{4,20},{8,24},{12,28},{16,0},{20,4},{24,8},{28,12},{1,17},{... | collective-permute-start | bytes 442376 | tf_op jit(solution)/shard_map/ppermute | solution.py:659
  11.5 1.5 collective-permute-start.4
  13.0 2.6 %collective-permute-done.4.refs_2_ = bf16[96,192]{1,0:T(8,128)(2,1)S(1)} collective-permute-done((bf16[96,192]{1,0:T(8,128)(2,1)S(1)}, bf16[96,192]{1,0:T(8,128)(2,1)S(1)}, u32[]{:S(2)}, u32[]{:S(2)}) %collective-permute-start.4) | collective-permute-done | bytes 36896 | tf_op jit(solution)/shard_map/ppermute | solution.py:659
  15.6 1.7 copy-done
  19.6 3.0 %collective-permute-done.1.refs_2_ = bf16[96,768]{1,0:T(8,128)(2,1)S(1)} collective-permute-done((bf16[96,768]{1,0:T(8,128)(2,1)S(1)}, bf16[96,768]{1,0:T(8,128)(2,1)S(1)}, u32[]{:S(2)}, u32[]{:S(2)}) %collective-permute-start.1) | collective-permute-done | bytes 147488 | tf_op jit(solution)/shard_map/ppermute | solution.py:659
  23.7 2.1 collective-permute-start.6
  28.3 3.1 %collective-permute-done.6.refs_2_ = bf16[96,1024]{1,0:T(8,128)(2,1)S(1)} collective-permute-done((bf16[96,1024]{1,0:T(8,128)(2,1)S(1)}, bf16[96,1024]{1,0:T(8,128)(2,1)S(1)}, u32[]{:S(2)}, u32[]{:S(2)}) %collective-permute-start.6) | collective-permute-done | bytes 196640 | tf_op jit(solution)/shard_map/ppermute | solution.py:659
  31.4 10.3 %collective-permute-done.7.refs_3_ = bf16[96,1024]{1,0:T(8,128)(2,1)S(1)} collective-permute-done((bf16[96,1024]{1,0:T(8,128)(2,1)S(1)}, bf16[96,1024]{1,0:T(8,128)(2,1)S(1)}, u32[]{:S(2)}, u32[]{:S(2)}) %collective-permute-start.7) | collective-permute-done | bytes 196640 | tf_op jit(solution)/shard_map/ppermute | solution.py:659
  43.1 1.6 collective-permute-start.11
  44.6 4.2 %collective-permute-start.12 = (bf16[96,768]{1,0:T(8,128)(2,1)S(1)}, bf16[96,768]{1,0:T(8,128)(2,1)S(1)}, u32[]{:S(2)}, u32[]{:S(2)}) collective-permute-start(bf16[96,768]{1,0:T(8,128)(2,1)S(1)} %bitcast.10), channel_id=1, source_target_pairs={{0,16},{4,20},{8,24},{12,28},{16,0},{20,4},{24,8},{28,12},{1,17},{... | collective-permute-start | bytes 442376 | tf_op jit(solution)/shard_map/ppermute | solution.py:659
  48.9 8.1 %attend_a.1 = (bf16[2,512,192]{2,1,0:T(8,128)(2,1)S(1)}, bf16[2,512,192]{2,1,0:T(8,128)(2,1)S(1)}, bf16[2,512,192]{2,1,0:T(8,128)(2,1)S(1)}, f32[2,512,128]{2,1,...) custom-call(s32[5]{0:T(128)S(1)} %pad_add_fusion.refs_0_, bf16[1536,768]{1,0:T(8,128)(2,1)S(1)} %copy-done.1, ...), custom_call_target="tpu_custom_call" | custom-call | flops 1 | bytes 1 | tf_op jit(solution)/shard_map/attend_a/pallas_call | solution.py:62
  57.0 1.6 collective-permute-start.10
  59.2 5.0 %attend_c.1 = (bf16[2,256,192]{2,1,0:T(8,128)(2,1)S(1)}, bf16[2,512,192]{2,1,0:T(8,128)(2,1)S(1)}, bf16[2,512,192]{2,1,0:T(8,128)(2,1)S(1)}, f32[2,256,128]{2,1,...) custom-call(s32[5]{0:T(128)S(1)} %pad_add_fusion.refs_0_, bf16[1536,768]{1,0:T(8,128)(2,1)S(1)} %copy-done.1, ...), custom_call_target="tpu_custom_call" | custom-call | flops 1 | bytes 1 | tf_op jit(solution)/shard_map/attend_c/pallas_call | solution.py:62
  64.1 3.6 %collective-permute-done.13.refs_2_ = bf16[192,768]{1,0:T(8,128)(2,1)S(1)} collective-permute-done((bf16[192,768]{1,0:T(8,128)(2,1)S(1)}, bf16[192,768]{1,0:T(8,128)(2,1)S(1)}, u32[]{:S(2)}, u32[]{:S(2)}) %collective-permute-start.13) | collective-permute-done | bytes 294944 | tf_op jit(solution)/shard_map/ppermute | solution.py:659
  70.8 1.7 collective-permute-done.14.refs_2_.refs_7_.refs_6_
  73.8 5.4 %lift_a.1 = (f32[512,768]{1,0:T(8,128)S(1)}, f32[512,128]{1,0:T(8,128)S(1)}, f32[512,1536]{1,0:T(8,128)S(1)}, bf16[512,768]{1,0:T(8,128)(2,1)S(1)}, bf16[512,1536]{1,0:T(8,128)(2,1)S(1)}, /*index=5*/f32[8,128]{1,0:T(8,128)S(1)}) custom-call(s32[5]{0:T(128)S(1)} %pad_add_fusion.refs_0_, bf16[1536,768]{1,0:T(8,128)(2,1)S(1)} %copy-done.1, ...), custom_call_target="tpu_custom_call" | custom-call | flops 1 | bytes 1 | tf_op jit(solution)/shard_map/lift_a/pallas_call | solution.py:62
  79.2 5.6 %collective-permute-done.15.refs_2_ = bf16[384,768]{1,0:T(8,128)(2,1)S(1)} collective-permute-done((bf16[384,768]{1,0:T(8,128)(2,1)S(1)}, bf16[384,768]{1,0:T(8,128)(2,1)S(1)}, u32[]{:S(2)}, u32[]{:S(2)}) %collective-permute-start.15) | collective-permute-done | bytes 589856 | tf_op jit(solution)/shard_map/ppermute | solution.py:659
  86.0 2.9 %lift_c.1 = (f32[256,768]{1,0:T(8,128)S(1)}, f32[256,128]{1,0:T(8,128)S(1)}, f32[256,1536]{1,0:T(8,128)S(1)}, bf16[256,768]{1,0:T(8,128)(2,1)S(1)}, bf16[256,1536]{1,0:T(8,128)(2,1)S(1)}, /*index=5*/f32[8,128]{1,0:T(8,128)S(1)}) custom-call(s32[5]{0:T(128)S(1)} %pad_add_fusion.refs_0_, bf16[1536,768]{1,0:T(8,128)(2,1)S(1)} %copy-done.1, ...), custom_call_target="tpu_custom_call" | custom-call | flops 1 | bytes 1 | tf_op jit(solution)/shard_map/lift_c/pallas_call | solution.py:62
  91.6 2.0 drop_a.1
  95.7 6.7 %collective-permute-done.20.refs_11_ = bf16[256,768]{1,0:T(8,128)(2,1)S(1)} collective-permute-done((bf16[256,768]{1,0:T(8,128)(2,1)S(1)}, bf16[256,768]{1,0:T(8,128)(2,1)S(1)}, u32[]{:S(2)}, u32[]{:S(2)}) %collective-permute-start.20) | collective-permute-done | bytes 393248 | tf_op jit(solution)/shard_map/ppermute | solution.py:659
  102.4 3.4 %turn_c.1 = (bf16[256,768]{1,0:T(8,128)(2,1)S(1)}, f32[256,768]{1,0:T(8,128)S(1)}, bf16[256,768]{1,0:T(8,128)(2,1)S(1)}, bf16[256,1536]{1,0:T(8,128)(2,1)S(1)}, ...) custom-call(s32[5]{0:T(128)S(1)} %pad_add_fusion.refs_0_, ...), custom_call_target="tpu_custom_call" | custom-call | flops 1 | bytes 1 | tf_op jit(solution)/shard_map/turn_c/pallas_call | solution.py:62
  105.8 5.0 %collective-permute-done.19.refs_11_ = bf16[256,768]{1,0:T(8,128)(2,1)S(1)} collective-permute-done((bf16[256,768]{1,0:T(8,128)(2,1)S(1)}, bf16[256,768]{1,0:T(8,128)(2,1)S(1)}, u32[]{:S(2)}, u32[]{:S(2)}) %collective-permute-start.19) | collective-permute-done | bytes 393248 | tf_op jit(solution)/shard_map/ppermute | solution.py:659
  110.8 3.4 %turn_0.1 = (bf16[256,768]{1,0:T(8,128)(2,1)S(1)}, f32[256,768]{1,0:T(8,128)S(1)}, bf16[256,768]{1,0:T(8,128)(2,1)S(1)}, bf16[256,1536]{1,0:T(8,128)(2,1)S(1)}, ...) custom-call(s32[5]{0:T(128)S(1)} %pad_add_fusion.refs_0_, ...), custom_call_target="tpu_custom_call" | custom-call | flops 1 | bytes 1 | tf_op jit(solution)/shard_map/turn_0/pallas_call | solution.py:62
  114.2 4.5 %collective-permute-done.18.refs_11_ = bf16[256,768]{1,0:T(8,128)(2,1)S(1)} collective-permute-done((bf16[256,768]{1,0:T(8,128)(2,1)S(1)}, bf16[256,768]{1,0:T(8,128)(2,1)S(1)}, u32[]{:S(2)}, u32[]{:S(2)}) %collective-permute-start.18) | collective-permute-done | bytes 393248 | tf_op jit(solution)/shard_map/ppermute | solution.py:659
  118.8 3.5 %turn_1.1 = (bf16[768,768]{1,0:T(8,128)(2,1)S(1)}, f32[256,768]{1,0:T(8,128)S(1)}, bf16[256,768]{1,0:T(8,128)(2,1)S(1)}, bf16[256,1536]{1,0:T(8,128)(2,1)S(1)}, ...) custom-call(s32[5]{0:T(128)S(1)} %pad_add_fusion.refs_0_, ...), custom_call_target="tpu_custom_call" | custom-call | flops 1 | bytes 1 | tf_op jit(solution)/shard_map/turn_1/pallas_call | solution.py:62
  126.9 3.1 %grads_d.1 = (f32[384,768]{1,0:T(8,128)S(1)}, bf16[384,768]{1,0:T(8,128)(2,1)S(1)}, f32[8,128]{1,0:T(8,128)S(1)}) custom-call(s32[5]{0:T(128)S(1)} %pad_add_fusion.refs_0_, bf16[256,1536]{1,0:T(8,128)(2,1)S(1)} %get-tuple-element.236.refs_1_, bf16[512,768]{1,0:T(8,128)(2,1)S(1)} %get-tuple-element.208.refs_1_.refs_2_, ...), custom_call_target="tpu_custom_call" | custom-call | flops 1 | bytes 1 | tf_op jit(solution)/shard_map/grads_d/pallas_call | solution.py:62
  131.8 3.4 %grads_u.1 = (f32[384,768]{1,0:T(8,128)S(1)}, bf16[384,768]{1,0:T(8,128)(2,1)S(1)}, f32[8,128]{1,0:T(8,128)S(1)}) custom-call(s32[5]{0:T(128)S(1)} %pad_add_fusion.refs_0_, bf16[512,1536]{1,0:T(8,128)(2,1)S(1)} %get-tuple-element.209.refs_2_.refs_1_, bf16[256,768]{1,0:T(8,128)(2,1)S(1)} %get-tuple-element.242.refs_2_, ...), custom_call_target="tpu_custom_call" | custom-call | flops 1 | bytes 1 | tf_op jit(solution)/shard_map/grads_u/pallas_call | solution.py:62
  135.1 8.2 %collective-permute-done.24.refs_3_.refs_4_ = bf16[512,768]{1,0:T(8,128)(2,1)S(1)} collective-permute-done((bf16[512,768]{1,0:T(8,128)(2,1)S(1)}, bf16[512,768]{1,0:T(8,128)(2,1)S(1)}, u32[]{:S(2)}, u32[]{:S(2)}) %collective-permute-start.24) | collective-permute-done | bytes 786464 | tf_op jit(solution)/shard_map/ppermute | solution.py:659
  143.3 2.2 collective-permute-done.28.refs_2_
  147.7 11.1 %back_a.1 = (f32[512,768]{1,0:T(8,128)S(1)}, bf16[512,768]{1,0:T(8,128)(2,1)S(1)}, bf16[512,576]{1,0:T(8,128)(2,1)S(1)}, bf16[512,640]{1,0:T(8,128)(2,1)S(1)}, f...) custom-call(s32[5]{0:T(128)S(1)} %pad_add_fusion.refs_0_, ...), custom_call_target="tpu_custom_call" | custom-call | flops 1 | bytes 1 | tf_op jit(solution)/shard_map/back_a/pallas_call | solution.py:62
  159.4 5.0 %back_c.1 = (f32[256,768]{1,0:T(8,128)S(1)}, bf16[256,768]{1,0:T(8,128)(2,1)S(1)}, f32[8,768]{1,0:T(8,128)S(1)}, bf16[2,256,192]{2,1,0:T(8,128)(2,1)S(1)}, f32[2...) custom-call(s32[5]{0:T(128)S(1)} %pad_add_fusion.refs_0_, ...), custom_call_target="tpu_custom_call" | custom-call | flops 1 | bytes 1 | tf_op jit(solution)/shard_map/back_c/pallas_call | solution.py:62
  165.7 2.4 %grads_out.1 = (f32[768,384]{1,0:T(8,128)S(1)}, bf16[768,384]{1,0:T(8,128)(2,1)S(1)}, f32[8,128]{1,0:T(8,128)S(1)}) custom-call(s32[5]{0:T(128)S(1)} %pad_add_fusion.refs_0_, bf16[512,768]{1,0:T(8,128)(2,1)S(1)} %get-tuple-element.265.refs_1_, bf16[256,768]{1,0:T(8,128)(2,1)S(1)} %get-tuple-element.266.refs_2_, ...), custom_call_target="tpu_custom_call" | custom-call | flops 1 | bytes 1 | tf_op jit(solution)/shard_map/grads_out/pallas_call | solution.py:62
  169.4 3.6 %grads_attn.1 = (f32[384,640]{1,0:T(8,128)S(1)}, bf16[384,640]{1,0:T(8,128)(2,1)S(1)}, f32[8,128]{1,0:T(8,128)S(1)}) custom-call(s32[5]{0:T(128)S(1)} %pad_add_fusion.refs_0_, bf16[1536,768]{1,0:T(8,128)(2,1)S(1)} %copy-done.1, bf16[512,576]{1,0:T(8,128)(2,1)S(1)} %get-tuple-element.278.refs_2_, bf16[512,640]{1,0:T(8,128)(2,1)S(1)} %collective-permute-done.35.refs_3_, ...), custom_call_target="tpu_custom_call" | custom-call | flops 1 | bytes 1 | tf_op jit(solution)/shard_map/grads_attn/pallas_call | solution.py:62
  173.7 1.9 collective-permute-start.38
  175.6 1.5 collective-permute-start.41
  178.0 1.6 collective-permute-start.37
  181.0 4.8 %collective-permute-done.38.refs_2_ = bf16[192,768]{1,0:T(8,128)(2,1)S(1)} collective-permute-done((bf16[192,768]{1,0:T(8,128)(2,1)S(1)}, bf16[192,768]{1,0:T(8,128)(2,1)S(1)}, u32[]{:S(2)}, u32[]{:S(2)}) %collective-permute-start.38) | collective-permute-done | bytes 294944 | tf_op jit(solution)/shard_map/ppermute | solution.py:659
  189.2 2.3 %collective-permute-start.43 = (bf16[192,640]{1,0:T(8,128)(2,1)S(1)}, bf16[192,640]{1,0:T(8,128)(2,1)S(1)}, u32[]{:S(2)}, u32[]{:S(2)}) collective-permute-start(bf16[192,640]{1,0:T(8,128)(2,1)S(1)} %get-tuple-element.299), channel_id=1, source_target_pairs={{0,8},{4,12},{8,0},{12,4},{16,24},{20,28},{24,16},{28,20},{1,9},{5... | collective-permute-start | bytes 737288 | tf_op jit(solution)/shard_map/ppermute | solution.py:659
  191.5 4.6 %collective-permute-done.39.refs_3_.refs_2_ = bf16[96,768]{1,0:T(8,128)(2,1)S(1)} collective-permute-done((bf16[96,768]{1,0:T(8,128)(2,1)S(1)}, bf16[96,768]{1,0:T(8,128)(2,1)S(1)}, u32[]{:S(2)}, u32[]{:S(2)}) %collective-permute-start.39) | collective-permute-done | bytes 147488 | tf_op jit(solution)/shard_map/ppermute | solution.py:659
  197.6 1.7 update_d.1
  199.9 1.7 update_u.1
  204.3 2.2 collective-permute-start.45
  207.2 2.8 %collective-permute-done.23.refs_2_ = bf16[768,768]{1,0:T(8,128)(2,1)S(1)} collective-permute-done((bf16[768,768]{1,0:T(8,128)(2,1)S(1)}, bf16[768,768]{1,0:T(8,128)(2,1)S(1)}, u32[]{:S(2)}, u32[]{:S(2)}) %collective-permute-start.23) | collective-permute-done | bytes 1179680 | tf_op jit(solution)/shard_map/ppermute | solution.py:659
  210.0 2.0 lay_out.1
  212.1 2.8 %lay_grad.1 = (f32[1536,768]{1,0:T(8,128)}, f32[8,128]{1,0:T(8,128)S(1)}) custom-call(s32[5]{0:T(128)S(1)} %pad_add_fusion.refs_0_, f32[768,768]{1,0:T(8,128)S(1)} %get-tuple-element.308.refs_1_, f32[768,768]{1,0:T(8,128)S(1)} %collective-permute-done.44.refs_2_, f32[8,128]{1,0:T(8,128)S(1)} %get-tuple-element.309.refs_3_), custom_call_target="tpu_custom_call" | custom-call | flops 1 | bytes 1 | tf_op jit(solution)/shard_map/lay_grad/pallas_call | solution.py:62
  216.4 1.9 update_a.1
  (135 shorter events, 46.0 us)
Async XLA Ops:
  4.1 15.5 %collective-permute-start.3 = (bf16[96,768]{1,0:T(8,128)(2,1)S(1)}, bf16[96,768]{1,0:T(8,128)(2,1)S(1)}, u32[]{:S(2)}, u32[]{:S(2)}) collective-permute-start(bf16[96,768]{1,0:T(8,128)(2,1)S(1)} %get-tuple-element.179.refs_1_), channel_id=1, source_target_pairs={{0,4},{4,0},{8,12},{12,8},{16,20},{20,16},{24,28},{28,24},{1,5},{5... | collective-permute-start | bytes 442376 | tf_op jit(solution)/shard_map/ppermute | solution.py:659
  7.1 12.5 %collective-permute-start = (bf16[96,768]{1,0:T(8,128)(2,1)S(1)}, bf16[96,768]{1,0:T(8,128)(2,1)S(1)}, u32[]{:S(2)}, u32[]{:S(2)}) collective-permute-start(bf16[96,768]{1,0:T(8,128)(2,1)S(1)} %get-tuple-element.179.refs_1_), channel_id=1, source_target_pairs={{0,8},{4,12},{8,0},{12,4},{16,24},{20,28},{24,16},{28,20},{1,9},{5... | collective-permute-start | bytes 442376 | tf_op jit(solution)/shard_map/ppermute | solution.py:659
  8.7 13.9 %collective-permute-start.1 = (bf16[96,768]{1,0:T(8,128)(2,1)S(1)}, bf16[96,768]{1,0:T(8,128)(2,1)S(1)}, u32[]{:S(2)}, u32[]{:S(2)}) collective-permute-start(bf16[96,768]{1,0:T(8,128)(2,1)S(1)} %get-tuple-element.179.refs_1_), channel_id=1, source_target_pairs={{0,16},{4,20},{8,24},{12,28},{16,0},{20,4},{24,8},{28,12},{1,17},{... | collective-permute-start | bytes 442376 | tf_op jit(solution)/shard_map/ppermute | solution.py:659
  11.3 11.3 %collective-permute-start.2 = (bf16[96,768]{1,0:T(8,128)(2,1)S(1)}, bf16[96,768]{1,0:T(8,128)(2,1)S(1)}, u32[]{:S(2)}, u32[]{:S(2)}) collective-permute-start(bf16[96,768]{1,0:T(8,128)(2,1)S(1)} %get-tuple-element.179.refs_1_), channel_id=1, source_target_pairs={{0,24},{4,28},{8,16},{12,20},{16,8},{20,12},{24,0},{28,4},{1,25},{... | collective-permute-start | bytes 442376 | tf_op jit(solution)/shard_map/ppermute | solution.py:659
  11.5 4.1 %collective-permute-start.4 = (bf16[96,192]{1,0:T(8,128)(2,1)S(1)}, bf16[96,192]{1,0:T(8,128)(2,1)S(1)}, u32[]{:S(2)}, u32[]{:S(2)}) collective-permute-start(bf16[96,192]{1,0:T(8,128)(2,1)S(1)} %get-tuple-element.180), channel_id=1, source_target_pairs={{0,2},{1,3},{2,0},{3,1},{4,6},{5,7},{6,4},{7,5},{8,10},{9,11},{10,... | collective-permute-start | bytes 110600 | tf_op jit(solution)/shard_map/ppermute | solution.py:659
  19.5 29.3 %copy-start.1 = (bf16[1536,768]{1,0:T(8,128)(2,1)S(1)}, bf16[1536,768]{1,0:T(8,128)(2,1)}, u32[]{:S(2)}) copy-start(bf16[1536,768]{1,0:T(8,128)(2,1)} %refs_1_.13) | copy-start | bytes 7077892
  23.1 19.2 %collective-permute-start.5 = (bf16[288,768]{1,0:T(8,128)(2,1)S(1)}, bf16[288,768]{1,0:T(8,128)(2,1)S(1)}, u32[]{:S(2)}, u32[]{:S(2)}) collective-permute-start(bf16[288,768]{1,0:T(8,128)(2,1)S(1)} %get-tuple-element.183.refs_2_), channel_id=1, source_target_pairs={{0,4},{4,0},{8,12},{12,8},{16,20},{20,16},{24,28},{28,24},{1,5},{5... | collective-permute-start | bytes 1327112 | tf_op jit(solution)/shard_map/ppermute | solution.py:659
  23.7 7.7 %collective-permute-start.6 = (bf16[96,1024]{1,0:T(8,128)(2,1)S(1)}, bf16[96,1024]{1,0:T(8,128)(2,1)S(1)}, u32[]{:S(2)}, u32[]{:S(2)}) collective-permute-start(bf16[96,1024]{1,0:T(8,128)(2,1)S(1)} %get-tuple-element.184.refs_1_), channel_id=1, source_target_pairs={{0,8},{4,12},{8,0},{12,4},{16,24},{20,28},{24,16},{28,20},{1,9},{5... | collective-permute-start | bytes 589832 | tf_op jit(solution)/shard_map/ppermute | solution.py:659
  25.9 15.9 %collective-permute-start.7 = (bf16[96,1024]{1,0:T(8,128)(2,1)S(1)}, bf16[96,1024]{1,0:T(8,128)(2,1)S(1)}, u32[]{:S(2)}, u32[]{:S(2)}) collective-permute-start(bf16[96,1024]{1,0:T(8,128)(2,1)S(1)} %get-tuple-element.184.refs_1_), channel_id=1, source_target_pairs={{0,16},{4,20},{8,24},{12,28},{16,0},{20,4},{24,8},{28,12},{1,17},{... | collective-permute-start | bytes 589832 | tf_op jit(solution)/shard_map/ppermute | solution.py:659
  26.9 14.9 %collective-permute-start.8 = (bf16[96,1024]{1,0:T(8,128)(2,1)S(1)}, bf16[96,1024]{1,0:T(8,128)(2,1)S(1)}, u32[]{:S(2)}, u32[]{:S(2)}) collective-permute-start(bf16[96,1024]{1,0:T(8,128)(2,1)S(1)} %get-tuple-element.184.refs_1_), channel_id=1, source_target_pairs={{0,24},{4,28},{8,16},{12,20},{16,8},{20,12},{24,0},{28,4},{1,25},{... | collective-permute-start | bytes 589832 | tf_op jit(solution)/shard_map/ppermute | solution.py:659
  43.0 5.8 %collective-permute-start.9 = (bf16[768,768]{1,0:T(8,128)(2,1)S(1)}, bf16[768,768]{1,0:T(8,128)(2,1)S(1)}, u32[]{:S(2)}, u32[]{:S(2)}) collective-permute-start(bf16[768,768]{1,0:T(8,128)(2,1)S(1)} %get-tuple-element.187.refs_2_.refs_3_.refs_13_.refs_4_), channel_id=1, source_target_pairs={{0,1},{1,0},{2,3},{3,2},{4,5},{5,4},{6,7},{7,6},{8,9},{9,8},{10,11... | collective-permute-start | bytes 3538952 | tf_op jit(solution)/shard_map/ppermute | solution.py:659
  43.1 25.2 %collective-permute-start.11 = (bf16[384,1024]{1,0:T(8,128)(2,1)S(1)}, bf16[384,1024]{1,0:T(8,128)(2,1)S(1)}, u32[]{:S(2)}, u32[]{:S(2)}) collective-permute-start(bf16[384,1024]{1,0:T(8,128)(2,1)S(1)} %get-tuple-element.190.refs_1_), channel_id=1, source_target_pairs={{0,4},{4,0},{8,12},{12,8},{16,20},{20,16},{24,28},{28,24},{1,5},{5... | collective-permute-start | bytes 2359304 | tf_op jit(solution)/shard_map/ppermute | solution.py:659
  44.6 13.9 %collective-permute-start.12 = (bf16[96,768]{1,0:T(8,128)(2,1)S(1)}, bf16[96,768]{1,0:T(8,128)(2,1)S(1)}, u32[]{:S(2)}, u32[]{:S(2)}) collective-permute-start(bf16[96,768]{1,0:T(8,128)(2,1)S(1)} %bitcast.10), channel_id=1, source_target_pairs={{0,16},{4,20},{8,24},{12,28},{16,0},{20,4},{24,8},{28,12},{1,17},{... | collective-permute-start | bytes 442376 | tf_op jit(solution)/shard_map/ppermute | solution.py:659
  57.0 11.3 %collective-permute-start.10 = (bf16[512,384]{1,0:T(8,128)(2,1)S(1)}, bf16[512,384]{1,0:T(8,128)(2,1)S(1)}, u32[]{:S(2)}, u32[]{:S(2)}) collective-permute-start(bf16[512,384]{1,0:T(8,128)(2,1)S(1)} %get-tuple-element.189.refs_2_.refs_3_), channel_id=1, source_target_pairs={{0,2},{1,3},{2,0},{3,1},{4,6},{5,7},{6,4},{7,5},{8,10},{9,11},{10,... | collective-permute-start | bytes 1179656 | tf_op jit(solution)/shard_map/ppermute | solution.py:659
  59.1 8.6 %collective-permute-start.13 = (bf16[192,768]{1,0:T(8,128)(2,1)S(1)}, bf16[192,768]{1,0:T(8,128)(2,1)S(1)}, u32[]{:S(2)}, u32[]{:S(2)}) collective-permute-start(bf16[192,768]{1,0:T(8,128)(2,1)S(1)} %get-tuple-element.192.refs_1_), channel_id=1, source_target_pairs={{0,8},{4,12},{8,0},{12,4},{16,24},{20,28},{24,16},{28,20},{1,9},{5... | collective-permute-start | bytes 884744 | tf_op jit(solution)/shard_map/ppermute | solution.py:659
  69.0 3.5 %collective-permute-start.14 = (bf16[768,1024]{1,0:T(8,128)(2,1)S(1)}, bf16[768,1024]{1,0:T(8,128)(2,1)S(1)}, u32[]{:S(2)}, u32[]{:S(2)}) collective-permute-start(bf16[768,1024]{1,0:T(8,128)(2,1)S(1)} %get-tuple-element.196.refs_1_.refs_6_.refs_5_), channel_id=1, source_target_pairs={{0,1},{1,0},{2,3},{3,2},{4,5},{5,4},{6,7},{7,6},{8,9},{9,8},{10,11... | collective-permute-start | bytes 4718600 | tf_op jit(solution)/shard_map/ppermute | solution.py:659
  69.0 15.7 %collective-permute-start.15 = (bf16[384,768]{1,0:T(8,128)(2,1)S(1)}, bf16[384,768]{1,0:T(8,128)(2,1)S(1)}, u32[]{:S(2)}, u32[]{:S(2)}) collective-permute-start(bf16[384,768]{1,0:T(8,128)(2,1)S(1)} %get-tuple-element.203.refs_1_), channel_id=1, source_target_pairs={{0,4},{4,0},{8,12},{12,8},{16,20},{20,16},{24,28},{28,24},{1,5},{5... | collective-permute-start | bytes 1769480 | tf_op jit(solution)/shard_map/ppermute | solution.py:659
  69.6 9.6 %collective-permute-start.16 = (bf16[256,384]{1,0:T(8,128)(2,1)S(1)}, bf16[256,384]{1,0:T(8,128)(2,1)S(1)}, u32[]{:S(2)}, u32[]{:S(2)}) collective-permute-start(bf16[256,384]{1,0:T(8,128)(2,1)S(1)} %get-tuple-element.204.refs_2_.refs_4_), channel_id=1, source_target_pairs={{0,2},{1,3},{2,0},{3,1},{4,6},{5,7},{6,4},{7,5},{8,10},{9,11},{10,... | collective-permute-start | bytes 589832 | tf_op jit(solution)/shard_map/ppermute | solution.py:659
  85.4 3.6 %collective-permute-start.17 = (bf16[768,768]{1,0:T(8,128)(2,1)S(1)}, bf16[768,768]{1,0:T(8,128)(2,1)S(1)}, u32[]{:S(2)}, u32[]{:S(2)}) collective-permute-start(bf16[768,768]{1,0:T(8,128)(2,1)S(1)} %get-tuple-element.206.refs_3_.refs_7_), channel_id=1, source_target_pairs={{0,1},{1,0},{2,3},{3,2},{4,5},{5,4},{6,7},{7,6},{8,9},{9,8},{10,11... | collective-permute-start | bytes 3538952 | tf_op jit(solution)/shard_map/ppermute | solution.py:659
  85.5 10.2 %collective-permute-start.21 = (bf16[512,1536]{1,0:T(8,128)(2,1)S(1)}, bf16[512,1536]{1,0:T(8,128)(2,1)S(1)}, u32[]{:S(2)}, u32[]{:S(2)}) collective-permute-start(bf16[512,1536]{1,0:T(8,128)(2,1)S(1)} %get-tuple-element.209.refs_2_.refs_1_), channel_id=1, source_target_pairs={{0,1},{1,0},{2,3},{3,2},{4,5},{5,4},{6,7},{7,6},{8,9},{9,8},{10,11... | collective-permute-start | bytes 4718600 | tf_op jit(solution)/shard_map/ppermute | solution.py:659
  88.9 6.8 %collective-permute-start.22 = (bf16[256,1536]{1,0:T(8,128)(2,1)S(1)}, bf16[256,1536]{1,0:T(8,128)(2,1)S(1)}, u32[]{:S(2)}, u32[]{:S(2)}) collective-permute-start(bf16[256,1536]{1,0:T(8,128)(2,1)S(1)} %get-tuple-element.212.refs_2_.refs_4_), channel_id=1, source_target_pairs={{0,1},{1,0},{2,3},{3,2},{4,5},{5,4},{6,7},{7,6},{8,9},{9,8},{10,11... | collective-permute-start | bytes 2359304 | tf_op jit(solution)/shard_map/ppermute | solution.py:659
  90.4 12.0 %collective-permute-start.20 = (bf16[256,768]{1,0:T(8,128)(2,1)S(1)}, bf16[256,768]{1,0:T(8,128)(2,1)S(1)}, u32[]{:S(2)}, u32[]{:S(2)}) collective-permute-start(bf16[256,768]{1,0:T(8,128)(2,1)S(1)} %get-tuple-element.219.refs_10_), channel_id=1, source_target_pairs={{0,2},{1,3},{2,0},{3,1},{4,6},{5,7},{6,4},{7,5},{8,10},{9,11},{10,... | collective-permute-start | bytes 1179656 | tf_op jit(solution)/shard_map/ppermute | solution.py:659
  93.6 17.2 %collective-permute-start.19 = (bf16[256,768]{1,0:T(8,128)(2,1)S(1)}, bf16[256,768]{1,0:T(8,128)(2,1)S(1)}, u32[]{:S(2)}, u32[]{:S(2)}) collective-permute-start(bf16[256,768]{1,0:T(8,128)(2,1)S(1)} %get-tuple-element.216.refs_10_), channel_id=1, source_target_pairs={{0,2},{1,3},{2,0},{3,1},{4,6},{5,7},{6,4},{7,5},{8,10},{9,11},{10,... | collective-permute-start | bytes 1179656 | tf_op jit(solution)/shard_map/ppermute | solution.py:659
  94.5 24.3 %collective-permute-start.18 = (bf16[256,768]{1,0:T(8,128)(2,1)S(1)}, bf16[256,768]{1,0:T(8,128)(2,1)S(1)}, u32[]{:S(2)}, u32[]{:S(2)}) collective-permute-start(bf16[256,768]{1,0:T(8,128)(2,1)S(1)} %get-tuple-element.215.refs_10_), channel_id=1, source_target_pairs={{0,2},{1,3},{2,0},{3,1},{4,6},{5,7},{6,4},{7,5},{8,10},{9,11},{10,... | collective-permute-start | bytes 1179656 | tf_op jit(solution)/shard_map/ppermute | solution.py:659
  122.3 2.4 %collective-permute-start.26 = (bf16[256,1536]{1,0:T(8,128)(2,1)S(1)}, bf16[256,1536]{1,0:T(8,128)(2,1)S(1)}, u32[]{:S(2)}, u32[]{:S(2)}) collective-permute-start(bf16[256,1536]{1,0:T(8,128)(2,1)S(1)} %get-tuple-element.237.refs_3_), channel_id=1, source_target_pairs={{0,1},{1,0},{2,3},{3,2},{4,5},{5,4},{6,7},{7,6},{8,9},{9,8},{10,11... | collective-permute-start | bytes 2359304 | tf_op jit(solution)/shard_map/ppermute | solution.py:659
  122.4 3.4 %collective-permute-start.25 = (bf16[256,1536]{1,0:T(8,128)(2,1)S(1)}, bf16[256,1536]{1,0:T(8,128)(2,1)S(1)}, u32[]{:S(2)}, u32[]{:S(2)}) collective-permute-start(bf16[256,1536]{1,0:T(8,128)(2,1)S(1)} %get-tuple-element.236.refs_1_), channel_id=1, source_target_pairs={{0,1},{1,0},{2,3},{3,2},{4,5},{5,4},{6,7},{7,6},{8,9},{9,8},{10,11... | collective-permute-start | bytes 2359304 | tf_op jit(solution)/shard_map/ppermute | solution.py:659
  122.8 4.0 %collective-permute-start.27 = (bf16[256,1536]{1,0:T(8,128)(2,1)S(1)}, bf16[256,1536]{1,0:T(8,128)(2,1)S(1)}, u32[]{:S(2)}, u32[]{:S(2)}) collective-permute-start(bf16[256,1536]{1,0:T(8,128)(2,1)S(1)} %get-tuple-element.238.refs_4_), channel_id=1, source_target_pairs={{0,1},{1,0},{2,3},{3,2},{4,5},{5,4},{6,7},{7,6},{8,9},{9,8},{10,11... | collective-permute-start | bytes 2359304 | tf_op jit(solution)/shard_map/ppermute | solution.py:659
  122.9 20.3 %collective-permute-start.24 = (bf16[512,768]{1,0:T(8,128)(2,1)S(1)}, bf16[512,768]{1,0:T(8,128)(2,1)S(1)}, u32[]{:S(2)}, u32[]{:S(2)}) collective-permute-start(bf16[512,768]{1,0:T(8,128)(2,1)S(1)} %get-tuple-element.229.refs_3_), channel_id=1, source_target_pairs={{0,2},{1,3},{2,0},{3,1},{4,6},{5,7},{6,4},{7,5},{8,10},{9,11},{10,... | collective-permute-start | bytes 2359304 | tf_op jit(solution)/shard_map/ppermute | solution.py:659
  130.0 15.4 %collective-permute-start.28 = (bf16[384,768]{1,0:T(8,128)(2,1)S(1)}, bf16[384,768]{1,0:T(8,128)(2,1)S(1)}, u32[]{:S(2)}, u32[]{:S(2)}) collective-permute-start(bf16[384,768]{1,0:T(8,128)(2,1)S(1)} %get-tuple-element.241), channel_id=1, source_target_pairs={{0,4},{4,0},{8,12},{12,8},{16,20},{20,16},{24,28},{28,24},{1,5},{5... | collective-permute-start | bytes 1769480 | tf_op jit(solution)/shard_map/ppermute | solution.py:659
  130.6 28.8 %collective-permute-start.30 = (bf16[256,768]{1,0:T(8,128)(2,1)S(1)}, bf16[256,768]{1,0:T(8,128)(2,1)S(1)}, u32[]{:S(2)}, u32[]{:S(2)}) collective-permute-start(bf16[256,768]{1,0:T(8,128)(2,1)S(1)} %get-tuple-element.251.refs_2_), channel_id=1, source_target_pairs={{0,2},{1,3},{2,0},{3,1},{4,6},{5,7},{6,4},{7,5},{8,10},{9,11},{10,... | collective-permute-start | bytes 1179656 | tf_op jit(solution)/shard_map/ppermute | solution.py:659
  146.1 12.7 %collective-permute-start.31 = (bf16[192,768]{1,0:T(8,128)(2,1)S(1)}, bf16[192,768]{1,0:T(8,128)(2,1)S(1)}, u32[]{:S(2)}, u32[]{:S(2)}) collective-permute-start(bf16[192,768]{1,0:T(8,128)(2,1)S(1)} %get-tuple-element.258), channel_id=1, source_target_pairs={{0,8},{4,12},{8,0},{12,4},{16,24},{20,28},{24,16},{28,20},{1,9},{5... | collective-permute-start | bytes 884744 | tf_op jit(solution)/shard_map/ppermute | solution.py:659
  146.5 18.6 %collective-permute-start.33 = (bf16[384,768]{1,0:T(8,128)(2,1)S(1)}, bf16[384,768]{1,0:T(8,128)(2,1)S(1)}, u32[]{:S(2)}, u32[]{:S(2)}) collective-permute-start(bf16[384,768]{1,0:T(8,128)(2,1)S(1)} %get-tuple-element.273), channel_id=1, source_target_pairs={{0,4},{4,0},{8,12},{12,8},{16,20},{20,16},{24,28},{28,24},{1,5},{5... | collective-permute-start | bytes 1769480 | tf_op jit(solution)/shard_map/ppermute | solution.py:659
  164.4 4.9 %collective-permute-start.32 = (bf16[896,384]{1,0:T(8,128)(2,1)S(1)}, bf16[896,384]{1,0:T(8,128)(2,1)S(1)}, u32[]{:S(2)}, u32[]{:S(2)}) collective-permute-start(bf16[896,384]{1,0:T(8,128)(2,1)S(1)} %get-tuple-element.264.refs_6_), channel_id=1, source_target_pairs={{0,1},{1,0},{2,3},{3,2},{4,5},{5,4},{6,7},{7,6},{8,9},{9,8},{10,11... | collective-permute-start | bytes 2064392 | tf_op jit(solution)/shard_map/ppermute | solution.py:659
  164.5 4.9 %collective-permute-start.35 = (bf16[512,640]{1,0:T(8,128)(2,1)S(1)}, bf16[512,640]{1,0:T(8,128)(2,1)S(1)}, u32[]{:S(2)}, u32[]{:S(2)}) collective-permute-start(bf16[512,640]{1,0:T(8,128)(2,1)S(1)} %get-tuple-element.279), channel_id=1, source_target_pairs={{0,1},{1,0},{2,3},{3,2},{4,5},{5,4},{6,7},{7,6},{8,9},{9,8},{10,11... | collective-permute-start | bytes 1966088 | tf_op jit(solution)/shard_map/ppermute | solution.py:659
  168.1 9.1 %collective-permute-start.34 = (bf16[768,384]{1,0:T(8,128)(2,1)S(1)}, bf16[768,384]{1,0:T(8,128)(2,1)S(1)}, u32[]{:S(2)}, u32[]{:S(2)}) collective-permute-start(bf16[768,384]{1,0:T(8,128)(2,1)S(1)} %get-tuple-element.277), channel_id=1, source_target_pairs={{0,1},{1,0},{2,3},{3,2},{4,5},{5,4},{6,7},{7,6},{8,9},{9,8},{10,11... | collective-permute-start | bytes 1769480 | tf_op jit(solution)/shard_map/ppermute | solution.py:659
  168.2 34.6 %collective-permute-start.29 = (bf16[512,768]{1,0:T(8,128)(2,1)S(1)}, bf16[512,768]{1,0:T(8,128)(2,1)S(1)}, u32[]{:S(2)}, u32[]{:S(2)}) collective-permute-start(bf16[512,768]{1,0:T(8,128)(2,1)S(1)} %get-tuple-element.249.refs_2_), channel_id=1, source_target_pairs={{0,2},{1,3},{2,0},{3,1},{4,6},{5,7},{6,4},{7,5},{8,10},{9,11},{10,... | collective-permute-start | bytes 2359304 | tf_op jit(solution)/shard_map/ppermute | solution.py:659
  173.0 15.5 %collective-permute-start.40 = (bf16[384,640]{1,0:T(8,128)(2,1)S(1)}, bf16[384,640]{1,0:T(8,128)(2,1)S(1)}, u32[]{:S(2)}, u32[]{:S(2)}) collective-permute-start(bf16[384,640]{1,0:T(8,128)(2,1)S(1)} %get-tuple-element.291), channel_id=1, source_target_pairs={{0,4},{4,0},{8,12},{12,8},{16,20},{20,16},{24,28},{28,24},{1,5},{5... | collective-permute-start | bytes 1474568 | tf_op jit(solution)/shard_map/ppermute | solution.py:659
  173.7 12.2 %collective-permute-start.38 = (bf16[192,768]{1,0:T(8,128)(2,1)S(1)}, bf16[192,768]{1,0:T(8,128)(2,1)S(1)}, u32[]{:S(2)}, u32[]{:S(2)}) collective-permute-start(bf16[192,768]{1,0:T(8,128)(2,1)S(1)} %get-tuple-element.287), channel_id=1, source_target_pairs={{0,8},{4,12},{8,0},{12,4},{16,24},{20,28},{24,16},{28,20},{1,9},{5... | collective-permute-start | bytes 884744 | tf_op jit(solution)/shard_map/ppermute | solution.py:659
  175.6 11.7 %collective-permute-start.41 = (bf16[96,768]{1,0:T(8,128)(2,1)S(1)}, bf16[96,768]{1,0:T(8,128)(2,1)S(1)}, u32[]{:S(2)}, u32[]{:S(2)}) collective-permute-start(bf16[96,768]{1,0:T(8,128)(2,1)S(1)} %get-tuple-element.292), channel_id=1, source_target_pairs={{0,16},{4,20},{8,24},{12,28},{16,0},{20,4},{24,8},{28,12},{1,17},{... | collective-permute-start | bytes 442376 | tf_op jit(solution)/shard_map/ppermute | solution.py:659
  178.0 18.1 %collective-permute-start.37 = (bf16[384,384]{1,0:T(8,128)(2,1)S(1)}, bf16[384,384]{1,0:T(8,128)(2,1)S(1)}, u32[]{:S(2)}, u32[]{:S(2)}) collective-permute-start(bf16[384,384]{1,0:T(8,128)(2,1)S(1)} %get-tuple-element.285), channel_id=1, source_target_pairs={{0,4},{4,0},{8,12},{12,8},{16,20},{20,16},{24,28},{28,24},{1,5},{5... | collective-permute-start | bytes 884744 | tf_op jit(solution)/shard_map/ppermute | solution.py:659
  185.9 17.0 %collective-permute-start.36 = (bf16[256,768]{1,0:T(8,128)(2,1)S(1)}, bf16[256,768]{1,0:T(8,128)(2,1)S(1)}, u32[]{:S(2)}, u32[]{:S(2)}) collective-permute-start(bf16[256,768]{1,0:T(8,128)(2,1)S(1)} %get-tuple-element.283.refs_5_), channel_id=1, source_target_pairs={{0,2},{1,3},{2,0},{3,1},{4,6},{5,7},{6,4},{7,5},{8,10},{9,11},{10,... | collective-permute-start | bytes 1179656 | tf_op jit(solution)/shard_map/ppermute | solution.py:659
  187.4 8.7 %collective-permute-start.39 = (bf16[96,768]{1,0:T(8,128)(2,1)S(1)}, bf16[96,768]{1,0:T(8,128)(2,1)S(1)}, u32[]{:S(2)}, u32[]{:S(2)}) collective-permute-start(bf16[96,768]{1,0:T(8,128)(2,1)S(1)} %get-tuple-element.289), channel_id=1, source_target_pairs={{0,16},{4,20},{8,24},{12,28},{16,0},{20,4},{24,8},{28,12},{1,17},{... | collective-permute-start | bytes 442376 | tf_op jit(solution)/shard_map/ppermute | solution.py:659
  189.2 10.1 %collective-permute-start.43 = (bf16[192,640]{1,0:T(8,128)(2,1)S(1)}, bf16[192,640]{1,0:T(8,128)(2,1)S(1)}, u32[]{:S(2)}, u32[]{:S(2)}) collective-permute-start(bf16[192,640]{1,0:T(8,128)(2,1)S(1)} %get-tuple-element.299), channel_id=1, source_target_pairs={{0,8},{4,12},{8,0},{12,4},{16,24},{20,28},{24,16},{28,20},{1,9},{5... | collective-permute-start | bytes 737288 | tf_op jit(solution)/shard_map/ppermute | solution.py:659
  196.7 5.5 %collective-permute-start.42 = (bf16[192,384]{1,0:T(8,128)(2,1)S(1)}, bf16[192,384]{1,0:T(8,128)(2,1)S(1)}, u32[]{:S(2)}, u32[]{:S(2)}) collective-permute-start(bf16[192,384]{1,0:T(8,128)(2,1)S(1)} %get-tuple-element.296), channel_id=1, source_target_pairs={{0,8},{4,12},{8,0},{12,4},{16,24},{20,28},{24,16},{28,20},{1,9},{5... | collective-permute-start | bytes 442376 | tf_op jit(solution)/shard_map/ppermute | solution.py:659
  203.7 8.3 %collective-permute-start.44 = (f32[768,768]{1,0:T(8,128)S(1)}, f32[768,768]{1,0:T(8,128)S(1)}, u32[]{:S(2)}, u32[]{:S(2)}) collective-permute-start(f32[768,768]{1,0:T(8,128)S(1)} %get-tuple-element.308.refs_1_), channel_id=1, source_target_pairs={{0,1},{1,0},{2,3},{3,2},{4,5},{5,4},{6,7},{7,6},{8,9},{9,8},{10,11... | collective-permute-start | bytes 7077896 | tf_op jit(solution)/shard_map/ppermute | solution.py:659
  203.8 6.2 %collective-permute-start.23 = (bf16[768,768]{1,0:T(8,128)(2,1)S(1)}, bf16[768,768]{1,0:T(8,128)(2,1)S(1)}, u32[]{:S(2)}, u32[]{:S(2)}) collective-permute-start(bf16[768,768]{1,0:T(8,128)(2,1)S(1)} %get-tuple-element.226.refs_1_), channel_id=1, source_target_pairs={{0,1},{1,0},{2,3},{3,2},{4,5},{5,4},{6,7},{7,6},{8,9},{9,8},{10,11... | collective-permute-start | bytes 3538952 | tf_op jit(solution)/shard_map/ppermute | solution.py:659
  204.3 12.0 %collective-permute-start.45 = (bf16[96,640]{1,0:T(8,128)(2,1)S(1)}, bf16[96,640]{1,0:T(8,128)(2,1)S(1)}, u32[]{:S(2)}, u32[]{:S(2)}) collective-permute-start(bf16[96,640]{1,0:T(8,128)(2,1)S(1)} %get-tuple-element.312), channel_id=1, source_target_pairs={{0,16},{4,20},{8,24},{12,28},{16,0},{20,4},{24,8},{28,12},{1,17},{... | collective-permute-start | bytes 368648 | tf_op jit(solution)/shard_map/ppermute | solution.py:659
  206.5 9.8 %collective-permute-start.46 = (bf16[96,384]{1,0:T(8,128)(2,1)S(1)}, bf16[96,384]{1,0:T(8,128)(2,1)S(1)}, u32[]{:S(2)}, u32[]{:S(2)}) collective-permute-start(bf16[96,384]{1,0:T(8,128)(2,1)S(1)} %get-tuple-element.314), channel_id=1, source_target_pairs={{0,16},{4,20},{8,24},{12,28},{16,0},{20,4},{24,8},{28,12},{1,17},{... | collective-permute-start | bytes 221192 | tf_op jit(solution)/shard_map/ppermute | solution.py:659
  (22 other events, 143.2 us)

commit v4 on v3

--- a/solution.py
+++ b/solution.py
@@ -793,15 +793,16 @@
         if direct:
             fold_u = third_fold(fold_u, "u")
             fold_1 = second_fold(fold_1, "qkv", deps=[fold_d[1]])
-            fold_2 = second_fold(fold_2, "o", deps=[fold_u[1]])
+            fold_2 = second_fold(fold_2, "o")
             n_down = update(order, rates, [fold_d], [
                 (down_t, first_down.T, second_down.T, DECAY_RATE, [(everything, 0, 0, units, False)])], "update_d")
-            fold_1 = third_fold(fold_1, "qkv")
-            n_up = update(order, rates, [fold_u], [
-                (up_weight, first_up, second_up, DECAY_RATE, [(everything, 0, 0, units, False)])], "update_u")
+            fold_1 = third_fold(fold_1, "qkv", deps=[fold_u[1]])
             fold_2 = third_fold(fold_2, "o")
         gi = add_rows(order, info, [(one_a, in_a, in_a_there), (one_c, in_c, in_c_there)], "add_in")
         gi_there = core_swap(gi)
+        if direct:
+            n_up = update(order, rates, [fold_u], [
+                (up_weight, first_up, second_up, DECAY_RATE, [(everything, 0, 0, units, False)])], "update_u")
         res_full = lay_rows(order, info, [result], [res_there], "lay_out")
         input_grad = lay_rows(order, info, [gi], [gi_there], "lay_grad")
         if direct:

time: 219 us -> 218 us (level)
  waiting for transfers between devices: 73.4 us -> 71.2 us
    ppermute x47, waiting for transfers between devices: 73.4 us -> 71.2 us  [swap(): return lax.ppermute(x, axis, [(i, i ^ bit) for i in range(size)])]
  transfers between devices with their start and end apart: 47 -> 47, of which waited for: 20 -> 22; matrix products, arithmetic and copies ran while one was open for 0% -> 0% of each run, Pallas kernels for 36% -> 36%
where the time goes in v4:
time: 218 us; the launch traced here: 217 us
  Pallas kernels  89.1 us (41%)
  waiting for transfers between devices  71.2 us (33%)
  starting transfers between devices  49 us (22%)
  local copies, waits for them, and re-layouts  5.07 us (2%)
  between operations  2.21 us (1%)
    pallas_call x41, Pallas kernels, call(): pl.pallas_call(run, out_shape=shapes, in_specs=specs, out_specs=specs_out...  89.1 us
    ppermute x47, waiting for transfers between devices, swap(): return lax.ppermute(x, axis, [(i, i ^ bit) for i in range(size)])  71.2 us
    ppermute x47, starting transfers between devices, swap(): return lax.ppermute(x, axis, [(i, i ^ bit) for i in range(size)])  49 us
    unnamed x46, local copies, waits for them, and re-layouts  5.07 us
  transfers between devices with their start and end apart: 47, of which 22 were waited for; matrix products, arithmetic and copies ran while one was open for 0% of the time, Pallas kernels for 36%

profile of v4, /device:TPU:0, one launch (start us, length us, event | category | flops | bytes accessed | tf_op | source)
XLA Modules:
  0.0 217.3 jit_solution(6219089592115581327)
XLA Ops:
  4.1 3.0 %collective-permute-start.3 = (bf16[96,768]{1,0:T(8,128)(2,1)S(1)}, bf16[96,768]{1,0:T(8,128)(2,1)S(1)}, u32[]{:S(2)}, u32[]{:S(2)}) collective-permute-start(bf16[96,768]{1,0:T(8,128)(2,1)S(1)} %get-tuple-element.179.refs_1_), channel_id=1, source_target_pairs={{0,4},{4,0},{8,12},{12,8},{16,20},{20,16},{24,28},{28,24},{1,5},{5... | collective-permute-start | bytes 442376 | tf_op jit(solution)/shard_map/ppermute | solution.py:659
  7.1 1.6 collective-permute-start
  8.7 2.6 %collective-permute-start.1 = (bf16[96,768]{1,0:T(8,128)(2,1)S(1)}, bf16[96,768]{1,0:T(8,128)(2,1)S(1)}, u32[]{:S(2)}, u32[]{:S(2)}) collective-permute-start(bf16[96,768]{1,0:T(8,128)(2,1)S(1)} %get-tuple-element.179.refs_1_), channel_id=1, source_target_pairs={{0,16},{4,20},{8,24},{12,28},{16,0},{20,4},{24,8},{28,12},{1,17},{... | collective-permute-start | bytes 442376 | tf_op jit(solution)/shard_map/ppermute | solution.py:659
  11.5 1.5 collective-permute-start.4
  13.0 2.6 %collective-permute-done.4.refs_2_ = bf16[96,192]{1,0:T(8,128)(2,1)S(1)} collective-permute-done((bf16[96,192]{1,0:T(8,128)(2,1)S(1)}, bf16[96,192]{1,0:T(8,128)(2,1)S(1)}, u32[]{:S(2)}, u32[]{:S(2)}) %collective-permute-start.4) | collective-permute-done | bytes 36896 | tf_op jit(solution)/shard_map/ppermute | solution.py:659
  15.6 1.7 copy-done
  19.6 3.0 %collective-permute-done.1.refs_2_ = bf16[96,768]{1,0:T(8,128)(2,1)S(1)} collective-permute-done((bf16[96,768]{1,0:T(8,128)(2,1)S(1)}, bf16[96,768]{1,0:T(8,128)(2,1)S(1)}, u32[]{:S(2)}, u32[]{:S(2)}) %collective-permute-start.1) | collective-permute-done | bytes 147488 | tf_op jit(solution)/shard_map/ppermute | solution.py:659
  23.7 2.1 collective-permute-start.6
  26.9 1.5 collective-permute-start.8
  28.3 3.1 %collective-permute-done.6.refs_2_ = bf16[96,1024]{1,0:T(8,128)(2,1)S(1)} collective-permute-done((bf16[96,1024]{1,0:T(8,128)(2,1)S(1)}, bf16[96,1024]{1,0:T(8,128)(2,1)S(1)}, u32[]{:S(2)}, u32[]{:S(2)}) %collective-permute-start.6) | collective-permute-done | bytes 196640 | tf_op jit(solution)/shard_map/ppermute | solution.py:659
  31.4 10.3 %collective-permute-done.7.refs_3_ = bf16[96,1024]{1,0:T(8,128)(2,1)S(1)} collective-permute-done((bf16[96,1024]{1,0:T(8,128)(2,1)S(1)}, bf16[96,1024]{1,0:T(8,128)(2,1)S(1)}, u32[]{:S(2)}, u32[]{:S(2)}) %collective-permute-start.7) | collective-permute-done | bytes 196640 | tf_op jit(solution)/shard_map/ppermute | solution.py:659
  43.1 1.6 collective-permute-start.11
  44.6 4.2 %collective-permute-start.12 = (bf16[96,768]{1,0:T(8,128)(2,1)S(1)}, bf16[96,768]{1,0:T(8,128)(2,1)S(1)}, u32[]{:S(2)}, u32[]{:S(2)}) collective-permute-start(bf16[96,768]{1,0:T(8,128)(2,1)S(1)} %bitcast.10), channel_id=1, source_target_pairs={{0,16},{4,20},{8,24},{12,28},{16,0},{20,4},{24,8},{28,12},{1,17},{... | collective-permute-start | bytes 442376 | tf_op jit(solution)/shard_map/ppermute | solution.py:659
  48.9 8.1 %attend_a.1 = (bf16[2,512,192]{2,1,0:T(8,128)(2,1)S(1)}, bf16[2,512,192]{2,1,0:T(8,128)(2,1)S(1)}, bf16[2,512,192]{2,1,0:T(8,128)(2,1)S(1)}, f32[2,512,128]{2,1,...) custom-call(s32[5]{0:T(128)S(1)} %pad_add_fusion.refs_0_, bf16[1536,768]{1,0:T(8,128)(2,1)S(1)} %copy-done.1, ...), custom_call_target="tpu_custom_call" | custom-call | flops 1 | bytes 1 | tf_op jit(solution)/shard_map/attend_a/pallas_call | solution.py:62
  57.0 1.6 collective-permute-start.10
  59.2 5.0 %attend_c.1 = (bf16[2,256,192]{2,1,0:T(8,128)(2,1)S(1)}, bf16[2,512,192]{2,1,0:T(8,128)(2,1)S(1)}, bf16[2,512,192]{2,1,0:T(8,128)(2,1)S(1)}, f32[2,256,128]{2,1,...) custom-call(s32[5]{0:T(128)S(1)} %pad_add_fusion.refs_0_, bf16[1536,768]{1,0:T(8,128)(2,1)S(1)} %copy-done.1, ...), custom_call_target="tpu_custom_call" | custom-call | flops 1 | bytes 1 | tf_op jit(solution)/shard_map/attend_c/pallas_call | solution.py:62
  64.1 3.6 %collective-permute-done.13.refs_2_ = bf16[192,768]{1,0:T(8,128)(2,1)S(1)} collective-permute-done((bf16[192,768]{1,0:T(8,128)(2,1)S(1)}, bf16[192,768]{1,0:T(8,128)(2,1)S(1)}, u32[]{:S(2)}, u32[]{:S(2)}) %collective-permute-start.13) | collective-permute-done | bytes 294944 | tf_op jit(solution)/shard_map/ppermute | solution.py:659
  70.8 1.7 collective-permute-done.14.refs_2_.refs_7_.refs_6_
  73.8 5.4 %lift_a.1 = (f32[512,768]{1,0:T(8,128)S(1)}, f32[512,128]{1,0:T(8,128)S(1)}, f32[512,1536]{1,0:T(8,128)S(1)}, bf16[512,768]{1,0:T(8,128)(2,1)S(1)}, bf16[512,1536]{1,0:T(8,128)(2,1)S(1)}, /*index=5*/f32[8,128]{1,0:T(8,128)S(1)}) custom-call(s32[5]{0:T(128)S(1)} %pad_add_fusion.refs_0_, bf16[1536,768]{1,0:T(8,128)(2,1)S(1)} %copy-done.1, ...), custom_call_target="tpu_custom_call" | custom-call | flops 1 | bytes 1 | tf_op jit(solution)/shard_map/lift_a/pallas_call | solution.py:62
  79.2 5.6 %collective-permute-done.15.refs_2_ = bf16[384,768]{1,0:T(8,128)(2,1)S(1)} collective-permute-done((bf16[384,768]{1,0:T(8,128)(2,1)S(1)}, bf16[384,768]{1,0:T(8,128)(2,1)S(1)}, u32[]{:S(2)}, u32[]{:S(2)}) %collective-permute-start.15) | collective-permute-done | bytes 589856 | tf_op jit(solution)/shard_map/ppermute | solution.py:659
  86.0 2.9 %lift_c.1 = (f32[256,768]{1,0:T(8,128)S(1)}, f32[256,128]{1,0:T(8,128)S(1)}, f32[256,1536]{1,0:T(8,128)S(1)}, bf16[256,768]{1,0:T(8,128)(2,1)S(1)}, bf16[256,1536]{1,0:T(8,128)(2,1)S(1)}, /*index=5*/f32[8,128]{1,0:T(8,128)S(1)}) custom-call(s32[5]{0:T(128)S(1)} %pad_add_fusion.refs_0_, bf16[1536,768]{1,0:T(8,128)(2,1)S(1)} %copy-done.1, ...), custom_call_target="tpu_custom_call" | custom-call | flops 1 | bytes 1 | tf_op jit(solution)/shard_map/lift_c/pallas_call | solution.py:62
  91.6 2.0 drop_a.1
  95.7 6.7 %collective-permute-done.20.refs_11_ = bf16[256,768]{1,0:T(8,128)(2,1)S(1)} collective-permute-done((bf16[256,768]{1,0:T(8,128)(2,1)S(1)}, bf16[256,768]{1,0:T(8,128)(2,1)S(1)}, u32[]{:S(2)}, u32[]{:S(2)}) %collective-permute-start.20) | collective-permute-done | bytes 393248 | tf_op jit(solution)/shard_map/ppermute | solution.py:659
  102.4 3.4 %turn_c.1 = (bf16[256,768]{1,0:T(8,128)(2,1)S(1)}, f32[256,768]{1,0:T(8,128)S(1)}, bf16[256,768]{1,0:T(8,128)(2,1)S(1)}, bf16[256,1536]{1,0:T(8,128)(2,1)S(1)}, ...) custom-call(s32[5]{0:T(128)S(1)} %pad_add_fusion.refs_0_, ...), custom_call_target="tpu_custom_call" | custom-call | flops 1 | bytes 1 | tf_op jit(solution)/shard_map/turn_c/pallas_call | solution.py:62
  105.8 5.0 %collective-permute-done.19.refs_11_ = bf16[256,768]{1,0:T(8,128)(2,1)S(1)} collective-permute-done((bf16[256,768]{1,0:T(8,128)(2,1)S(1)}, bf16[256,768]{1,0:T(8,128)(2,1)S(1)}, u32[]{:S(2)}, u32[]{:S(2)}) %collective-permute-start.19) | collective-permute-done | bytes 393248 | tf_op jit(solution)/shard_map/ppermute | solution.py:659
  110.8 3.4 %turn_0.1 = (bf16[256,768]{1,0:T(8,128)(2,1)S(1)}, f32[256,768]{1,0:T(8,128)S(1)}, bf16[256,768]{1,0:T(8,128)(2,1)S(1)}, bf16[256,1536]{1,0:T(8,128)(2,1)S(1)}, ...) custom-call(s32[5]{0:T(128)S(1)} %pad_add_fusion.refs_0_, ...), custom_call_target="tpu_custom_call" | custom-call | flops 1 | bytes 1 | tf_op jit(solution)/shard_map/turn_0/pallas_call | solution.py:62
  114.2 4.5 %collective-permute-done.18.refs_11_ = bf16[256,768]{1,0:T(8,128)(2,1)S(1)} collective-permute-done((bf16[256,768]{1,0:T(8,128)(2,1)S(1)}, bf16[256,768]{1,0:T(8,128)(2,1)S(1)}, u32[]{:S(2)}, u32[]{:S(2)}) %collective-permute-start.18) | collective-permute-done | bytes 393248 | tf_op jit(solution)/shard_map/ppermute | solution.py:659
  118.8 3.5 %turn_1.1 = (bf16[768,768]{1,0:T(8,128)(2,1)S(1)}, f32[256,768]{1,0:T(8,128)S(1)}, bf16[256,768]{1,0:T(8,128)(2,1)S(1)}, bf16[256,1536]{1,0:T(8,128)(2,1)S(1)}, ...) custom-call(s32[5]{0:T(128)S(1)} %pad_add_fusion.refs_0_, ...), custom_call_target="tpu_custom_call" | custom-call | flops 1 | bytes 1 | tf_op jit(solution)/shard_map/turn_1/pallas_call | solution.py:62
  126.9 3.1 %grads_d.1 = (f32[384,768]{1,0:T(8,128)S(1)}, bf16[384,768]{1,0:T(8,128)(2,1)S(1)}, f32[8,128]{1,0:T(8,128)S(1)}) custom-call(s32[5]{0:T(128)S(1)} %pad_add_fusion.refs_0_, bf16[256,1536]{1,0:T(8,128)(2,1)S(1)} %get-tuple-element.230.refs_1_, bf16[512,768]{1,0:T(8,128)(2,1)S(1)} %get-tuple-element.208.refs_1_.refs_2_, ...), custom_call_target="tpu_custom_call" | custom-call | flops 1 | bytes 1 | tf_op jit(solution)/shard_map/grads_d/pallas_call | solution.py:62
  131.8 3.4 %grads_u.1 = (f32[384,768]{1,0:T(8,128)S(1)}, bf16[384,768]{1,0:T(8,128)(2,1)S(1)}, f32[8,128]{1,0:T(8,128)S(1)}) custom-call(s32[5]{0:T(128)S(1)} %pad_add_fusion.refs_0_, bf16[512,1536]{1,0:T(8,128)(2,1)S(1)} %get-tuple-element.209.refs_2_.refs_1_, bf16[256,768]{1,0:T(8,128)(2,1)S(1)} %get-tuple-element.227.refs_2_, ...), custom_call_target="tpu_custom_call" | custom-call | flops 1 | bytes 1 | tf_op jit(solution)/shard_map/grads_u/pallas_call | solution.py:62
  135.1 8.2 %collective-permute-done.30.refs_3_.refs_4_ = bf16[512,768]{1,0:T(8,128)(2,1)S(1)} collective-permute-done((bf16[512,768]{1,0:T(8,128)(2,1)S(1)}, bf16[512,768]{1,0:T(8,128)(2,1)S(1)}, u32[]{:S(2)}, u32[]{:S(2)}) %collective-permute-start.30) | collective-permute-done | bytes 786464 | tf_op jit(solution)/shard_map/ppermute | solution.py:659
  143.3 2.2 %collective-permute-done.29.refs_2_ = bf16[384,768]{1,0:T(8,128)(2,1)S(1)} collective-permute-done((bf16[384,768]{1,0:T(8,128)(2,1)S(1)}, bf16[384,768]{1,0:T(8,128)(2,1)S(1)}, u32[]{:S(2)}, u32[]{:S(2)}) %collective-permute-start.29) | collective-permute-done | bytes 589856 | tf_op jit(solution)/shard_map/ppermute | solution.py:659
  147.7 11.1 %back_a.1 = (f32[512,768]{1,0:T(8,128)S(1)}, bf16[512,768]{1,0:T(8,128)(2,1)S(1)}, bf16[512,576]{1,0:T(8,128)(2,1)S(1)}, bf16[512,640]{1,0:T(8,128)(2,1)S(1)}, f...) custom-call(s32[5]{0:T(128)S(1)} %pad_add_fusion.refs_0_, ...), custom_call_target="tpu_custom_call" | custom-call | flops 1 | bytes 1 | tf_op jit(solution)/shard_map/back_a/pallas_call | solution.py:62
  159.4 5.0 %back_c.1 = (f32[256,768]{1,0:T(8,128)S(1)}, bf16[256,768]{1,0:T(8,128)(2,1)S(1)}, f32[8,768]{1,0:T(8,128)S(1)}, bf16[2,256,192]{2,1,0:T(8,128)(2,1)S(1)}, f32[2...) custom-call(s32[5]{0:T(128)S(1)} %pad_add_fusion.refs_0_, ...), custom_call_target="tpu_custom_call" | custom-call | flops 1 | bytes 1 | tf_op jit(solution)/shard_map/back_c/pallas_call | solution.py:62
  165.7 2.4 %grads_out.1 = (f32[768,384]{1,0:T(8,128)S(1)}, bf16[768,384]{1,0:T(8,128)(2,1)S(1)}, f32[8,128]{1,0:T(8,128)S(1)}) custom-call(s32[5]{0:T(128)S(1)} %pad_add_fusion.refs_0_, bf16[512,768]{1,0:T(8,128)(2,1)S(1)} %get-tuple-element.267.refs_1_, bf16[256,768]{1,0:T(8,128)(2,1)S(1)} %get-tuple-element.268.refs_2_, ...), custom_call_target="tpu_custom_call" | custom-call | flops 1 | bytes 1 | tf_op jit(solution)/shard_map/grads_out/pallas_call | solution.py:62
  169.4 3.6 %grads_attn.1 = (f32[384,640]{1,0:T(8,128)S(1)}, bf16[384,640]{1,0:T(8,128)(2,1)S(1)}, f32[8,128]{1,0:T(8,128)S(1)}) custom-call(s32[5]{0:T(128)S(1)} %pad_add_fusion.refs_0_, bf16[1536,768]{1,0:T(8,128)(2,1)S(1)} %copy-done.1, bf16[512,576]{1,0:T(8,128)(2,1)S(1)} %get-tuple-element.277.refs_2_, bf16[512,640]{1,0:T(8,128)(2,1)S(1)} %collective-permute-done.35.refs_3_, ...), custom_call_target="tpu_custom_call" | custom-call | flops 1 | bytes 1 | tf_op jit(solution)/shard_map/grads_attn/pallas_call | solution.py:62
  173.7 1.9 collective-permute-start.32
  177.0 2.5 %collective-permute-start.41 = (bf16[96,768]{1,0:T(8,128)(2,1)S(1)}, bf16[96,768]{1,0:T(8,128)(2,1)S(1)}, u32[]{:S(2)}, u32[]{:S(2)}) collective-permute-start(bf16[96,768]{1,0:T(8,128)(2,1)S(1)} %get-tuple-element.293), channel_id=1, source_target_pairs={{0,16},{4,20},{8,24},{12,28},{16,0},{20,4},{24,8},{28,12},{1,17},{... | collective-permute-start | bytes 442376 | tf_op jit(solution)/shard_map/ppermute | solution.py:659
  179.5 1.5 project_c.1
  181.0 4.8 %collective-permute-done.32.refs_2_ = bf16[192,768]{1,0:T(8,128)(2,1)S(1)} collective-permute-done((bf16[192,768]{1,0:T(8,128)(2,1)S(1)}, bf16[192,768]{1,0:T(8,128)(2,1)S(1)}, u32[]{:S(2)}, u32[]{:S(2)}) %collective-permute-start.32) | collective-permute-done | bytes 294944 | tf_op jit(solution)/shard_map/ppermute | solution.py:659
  188.9 2.5 %collective-permute-start.36 = (bf16[96,768]{1,0:T(8,128)(2,1)S(1)}, bf16[96,768]{1,0:T(8,128)(2,1)S(1)}, u32[]{:S(2)}, u32[]{:S(2)}) collective-permute-start(bf16[96,768]{1,0:T(8,128)(2,1)S(1)} %get-tuple-element.284), channel_id=1, source_target_pairs={{0,16},{4,20},{8,24},{12,28},{16,0},{20,4},{24,8},{28,12},{1,17},{... | collective-permute-start | bytes 442376 | tf_op jit(solution)/shard_map/ppermute | solution.py:659
  195.3 1.7 update_d.1
  197.6 1.7 collective-permute-done.43.refs_2_
  203.1 1.5 collective-permute-start.45
  206.1 1.7 update_u.1
  208.8 2.0 lay_out.1
  211.0 2.8 %lay_grad.1 = (f32[1536,768]{1,0:T(8,128)}, f32[8,128]{1,0:T(8,128)S(1)}) custom-call(s32[5]{0:T(128)S(1)} %pad_add_fusion.refs_0_, f32[768,768]{1,0:T(8,128)S(1)} %get-tuple-element.308.refs_1_, f32[768,768]{1,0:T(8,128)S(1)} %collective-permute-done.44.refs_2_, f32[8,128]{1,0:T(8,128)S(1)} %get-tuple-element.309.refs_3_), custom_call_target="tpu_custom_call" | custom-call | flops 1 | bytes 1 | tf_op jit(solution)/shard_map/lay_grad/pallas_call | solution.py:62
  215.2 1.9 update_a.1
  (135 shorter events, 48.6 us)
Async XLA Ops:
  4.1 15.5 %collective-permute-start.3 = (bf16[96,768]{1,0:T(8,128)(2,1)S(1)}, bf16[96,768]{1,0:T(8,128)(2,1)S(1)}, u32[]{:S(2)}, u32[]{:S(2)}) collective-permute-start(bf16[96,768]{1,0:T(8,128)(2,1)S(1)} %get-tuple-element.179.refs_1_), channel_id=1, source_target_pairs={{0,4},{4,0},{8,12},{12,8},{16,20},{20,16},{24,28},{28,24},{1,5},{5... | collective-permute-start | bytes 442376 | tf_op jit(solution)/shard_map/ppermute | solution.py:659
  7.1 12.5 %collective-permute-start = (bf16[96,768]{1,0:T(8,128)(2,1)S(1)}, bf16[96,768]{1,0:T(8,128)(2,1)S(1)}, u32[]{:S(2)}, u32[]{:S(2)}) collective-permute-start(bf16[96,768]{1,0:T(8,128)(2,1)S(1)} %get-tuple-element.179.refs_1_), channel_id=1, source_target_pairs={{0,8},{4,12},{8,0},{12,4},{16,24},{20,28},{24,16},{28,20},{1,9},{5... | collective-permute-start | bytes 442376 | tf_op jit(solution)/shard_map/ppermute | solution.py:659
  8.7 13.9 %collective-permute-start.1 = (bf16[96,768]{1,0:T(8,128)(2,1)S(1)}, bf16[96,768]{1,0:T(8,128)(2,1)S(1)}, u32[]{:S(2)}, u32[]{:S(2)}) collective-permute-start(bf16[96,768]{1,0:T(8,128)(2,1)S(1)} %get-tuple-element.179.refs_1_), channel_id=1, source_target_pairs={{0,16},{4,20},{8,24},{12,28},{16,0},{20,4},{24,8},{28,12},{1,17},{... | collective-permute-start | bytes 442376 | tf_op jit(solution)/shard_map/ppermute | solution.py:659
  11.3 11.3 %collective-permute-start.2 = (bf16[96,768]{1,0:T(8,128)(2,1)S(1)}, bf16[96,768]{1,0:T(8,128)(2,1)S(1)}, u32[]{:S(2)}, u32[]{:S(2)}) collective-permute-start(bf16[96,768]{1,0:T(8,128)(2,1)S(1)} %get-tuple-element.179.refs_1_), channel_id=1, source_target_pairs={{0,24},{4,28},{8,16},{12,20},{16,8},{20,12},{24,0},{28,4},{1,25},{... | collective-permute-start | bytes 442376 | tf_op jit(solution)/shard_map/ppermute | solution.py:659
  11.5 4.1 %collective-permute-start.4 = (bf16[96,192]{1,0:T(8,128)(2,1)S(1)}, bf16[96,192]{1,0:T(8,128)(2,1)S(1)}, u32[]{:S(2)}, u32[]{:S(2)}) collective-permute-start(bf16[96,192]{1,0:T(8,128)(2,1)S(1)} %get-tuple-element.180), channel_id=1, source_target_pairs={{0,2},{1,3},{2,0},{3,1},{4,6},{5,7},{6,4},{7,5},{8,10},{9,11},{10,... | collective-permute-start | bytes 110600 | tf_op jit(solution)/shard_map/ppermute | solution.py:659
  19.5 29.3 %copy-start.1 = (bf16[1536,768]{1,0:T(8,128)(2,1)S(1)}, bf16[1536,768]{1,0:T(8,128)(2,1)}, u32[]{:S(2)}) copy-start(bf16[1536,768]{1,0:T(8,128)(2,1)} %refs_1_.13) | copy-start | bytes 7077892
  23.1 19.2 %collective-permute-start.5 = (bf16[288,768]{1,0:T(8,128)(2,1)S(1)}, bf16[288,768]{1,0:T(8,128)(2,1)S(1)}, u32[]{:S(2)}, u32[]{:S(2)}) collective-permute-start(bf16[288,768]{1,0:T(8,128)(2,1)S(1)} %get-tuple-element.183.refs_2_), channel_id=1, source_target_pairs={{0,4},{4,0},{8,12},{12,8},{16,20},{20,16},{24,28},{28,24},{1,5},{5... | collective-permute-start | bytes 1327112 | tf_op jit(solution)/shard_map/ppermute | solution.py:659
  23.7 7.7 %collective-permute-start.6 = (bf16[96,1024]{1,0:T(8,128)(2,1)S(1)}, bf16[96,1024]{1,0:T(8,128)(2,1)S(1)}, u32[]{:S(2)}, u32[]{:S(2)}) collective-permute-start(bf16[96,1024]{1,0:T(8,128)(2,1)S(1)} %get-tuple-element.184.refs_1_), channel_id=1, source_target_pairs={{0,8},{4,12},{8,0},{12,4},{16,24},{20,28},{24,16},{28,20},{1,9},{5... | collective-permute-start | bytes 589832 | tf_op jit(solution)/shard_map/ppermute | solution.py:659
  25.9 15.9 %collective-permute-start.7 = (bf16[96,1024]{1,0:T(8,128)(2,1)S(1)}, bf16[96,1024]{1,0:T(8,128)(2,1)S(1)}, u32[]{:S(2)}, u32[]{:S(2)}) collective-permute-start(bf16[96,1024]{1,0:T(8,128)(2,1)S(1)} %get-tuple-element.184.refs_1_), channel_id=1, source_target_pairs={{0,16},{4,20},{8,24},{12,28},{16,0},{20,4},{24,8},{28,12},{1,17},{... | collective-permute-start | bytes 589832 | tf_op jit(solution)/shard_map/ppermute | solution.py:659
  26.9 14.9 %collective-permute-start.8 = (bf16[96,1024]{1,0:T(8,128)(2,1)S(1)}, bf16[96,1024]{1,0:T(8,128)(2,1)S(1)}, u32[]{:S(2)}, u32[]{:S(2)}) collective-permute-start(bf16[96,1024]{1,0:T(8,128)(2,1)S(1)} %get-tuple-element.184.refs_1_), channel_id=1, source_target_pairs={{0,24},{4,28},{8,16},{12,20},{16,8},{20,12},{24,0},{28,4},{1,25},{... | collective-permute-start | bytes 589832 | tf_op jit(solution)/shard_map/ppermute | solution.py:659
  43.0 5.8 %collective-permute-start.9 = (bf16[768,768]{1,0:T(8,128)(2,1)S(1)}, bf16[768,768]{1,0:T(8,128)(2,1)S(1)}, u32[]{:S(2)}, u32[]{:S(2)}) collective-permute-start(bf16[768,768]{1,0:T(8,128)(2,1)S(1)} %get-tuple-element.187.refs_2_.refs_3_.refs_13_.refs_4_), channel_id=1, source_target_pairs={{0,1},{1,0},{2,3},{3,2},{4,5},{5,4},{6,7},{7,6},{8,9},{9,8},{10,11... | collective-permute-start | bytes 3538952 | tf_op jit(solution)/shard_map/ppermute | solution.py:659
  43.1 25.2 %collective-permute-start.11 = (bf16[384,1024]{1,0:T(8,128)(2,1)S(1)}, bf16[384,1024]{1,0:T(8,128)(2,1)S(1)}, u32[]{:S(2)}, u32[]{:S(2)}) collective-permute-start(bf16[384,1024]{1,0:T(8,128)(2,1)S(1)} %get-tuple-element.190.refs_1_), channel_id=1, source_target_pairs={{0,4},{4,0},{8,12},{12,8},{16,20},{20,16},{24,28},{28,24},{1,5},{5... | collective-permute-start | bytes 2359304 | tf_op jit(solution)/shard_map/ppermute | solution.py:659
  44.6 13.9 %collective-permute-start.12 = (bf16[96,768]{1,0:T(8,128)(2,1)S(1)}, bf16[96,768]{1,0:T(8,128)(2,1)S(1)}, u32[]{:S(2)}, u32[]{:S(2)}) collective-permute-start(bf16[96,768]{1,0:T(8,128)(2,1)S(1)} %bitcast.10), channel_id=1, source_target_pairs={{0,16},{4,20},{8,24},{12,28},{16,0},{20,4},{24,8},{28,12},{1,17},{... | collective-permute-start | bytes 442376 | tf_op jit(solution)/shard_map/ppermute | solution.py:659
  57.0 11.3 %collective-permute-start.10 = (bf16[512,384]{1,0:T(8,128)(2,1)S(1)}, bf16[512,384]{1,0:T(8,128)(2,1)S(1)}, u32[]{:S(2)}, u32[]{:S(2)}) collective-permute-start(bf16[512,384]{1,0:T(8,128)(2,1)S(1)} %get-tuple-element.189.refs_2_.refs_3_), channel_id=1, source_target_pairs={{0,2},{1,3},{2,0},{3,1},{4,6},{5,7},{6,4},{7,5},{8,10},{9,11},{10,... | collective-permute-start | bytes 1179656 | tf_op jit(solution)/shard_map/ppermute | solution.py:659
  59.1 8.6 %collective-permute-start.13 = (bf16[192,768]{1,0:T(8,128)(2,1)S(1)}, bf16[192,768]{1,0:T(8,128)(2,1)S(1)}, u32[]{:S(2)}, u32[]{:S(2)}) collective-permute-start(bf16[192,768]{1,0:T(8,128)(2,1)S(1)} %get-tuple-element.192.refs_1_), channel_id=1, source_target_pairs={{0,8},{4,12},{8,0},{12,4},{16,24},{20,28},{24,16},{28,20},{1,9},{5... | collective-permute-start | bytes 884744 | tf_op jit(solution)/shard_map/ppermute | solution.py:659
  69.0 3.5 %collective-permute-start.14 = (bf16[768,1024]{1,0:T(8,128)(2,1)S(1)}, bf16[768,1024]{1,0:T(8,128)(2,1)S(1)}, u32[]{:S(2)}, u32[]{:S(2)}) collective-permute-start(bf16[768,1024]{1,0:T(8,128)(2,1)S(1)} %get-tuple-element.196.refs_1_.refs_6_.refs_5_), channel_id=1, source_target_pairs={{0,1},{1,0},{2,3},{3,2},{4,5},{5,4},{6,7},{7,6},{8,9},{9,8},{10,11... | collective-permute-start | bytes 4718600 | tf_op jit(solution)/shard_map/ppermute | solution.py:659
  69.0 15.7 %collective-permute-start.15 = (bf16[384,768]{1,0:T(8,128)(2,1)S(1)}, bf16[384,768]{1,0:T(8,128)(2,1)S(1)}, u32[]{:S(2)}, u32[]{:S(2)}) collective-permute-start(bf16[384,768]{1,0:T(8,128)(2,1)S(1)} %get-tuple-element.203.refs_1_), channel_id=1, source_target_pairs={{0,4},{4,0},{8,12},{12,8},{16,20},{20,16},{24,28},{28,24},{1,5},{5... | collective-permute-start | bytes 1769480 | tf_op jit(solution)/shard_map/ppermute | solution.py:659
  69.6 9.6 %collective-permute-start.16 = (bf16[256,384]{1,0:T(8,128)(2,1)S(1)}, bf16[256,384]{1,0:T(8,128)(2,1)S(1)}, u32[]{:S(2)}, u32[]{:S(2)}) collective-permute-start(bf16[256,384]{1,0:T(8,128)(2,1)S(1)} %get-tuple-element.204.refs_2_.refs_4_), channel_id=1, source_target_pairs={{0,2},{1,3},{2,0},{3,1},{4,6},{5,7},{6,4},{7,5},{8,10},{9,11},{10,... | collective-permute-start | bytes 589832 | tf_op jit(solution)/shard_map/ppermute | solution.py:659
  85.4 3.6 %collective-permute-start.17 = (bf16[768,768]{1,0:T(8,128)(2,1)S(1)}, bf16[768,768]{1,0:T(8,128)(2,1)S(1)}, u32[]{:S(2)}, u32[]{:S(2)}) collective-permute-start(bf16[768,768]{1,0:T(8,128)(2,1)S(1)} %get-tuple-element.206.refs_3_.refs_7_), channel_id=1, source_target_pairs={{0,1},{1,0},{2,3},{3,2},{4,5},{5,4},{6,7},{7,6},{8,9},{9,8},{10,11... | collective-permute-start | bytes 3538952 | tf_op jit(solution)/shard_map/ppermute | solution.py:659
  85.5 10.2 %collective-permute-start.21 = (bf16[512,1536]{1,0:T(8,128)(2,1)S(1)}, bf16[512,1536]{1,0:T(8,128)(2,1)S(1)}, u32[]{:S(2)}, u32[]{:S(2)}) collective-permute-start(bf16[512,1536]{1,0:T(8,128)(2,1)S(1)} %get-tuple-element.209.refs_2_.refs_1_), channel_id=1, source_target_pairs={{0,1},{1,0},{2,3},{3,2},{4,5},{5,4},{6,7},{7,6},{8,9},{9,8},{10,11... | collective-permute-start | bytes 4718600 | tf_op jit(solution)/shard_map/ppermute | solution.py:659
  88.9 6.8 %collective-permute-start.22 = (bf16[256,1536]{1,0:T(8,128)(2,1)S(1)}, bf16[256,1536]{1,0:T(8,128)(2,1)S(1)}, u32[]{:S(2)}, u32[]{:S(2)}) collective-permute-start(bf16[256,1536]{1,0:T(8,128)(2,1)S(1)} %get-tuple-element.212.refs_2_.refs_4_), channel_id=1, source_target_pairs={{0,1},{1,0},{2,3},{3,2},{4,5},{5,4},{6,7},{7,6},{8,9},{9,8},{10,11... | collective-permute-start | bytes 2359304 | tf_op jit(solution)/shard_map/ppermute | solution.py:659
  90.4 12.0 %collective-permute-start.20 = (bf16[256,768]{1,0:T(8,128)(2,1)S(1)}, bf16[256,768]{1,0:T(8,128)(2,1)S(1)}, u32[]{:S(2)}, u32[]{:S(2)}) collective-permute-start(bf16[256,768]{1,0:T(8,128)(2,1)S(1)} %get-tuple-element.219.refs_10_), channel_id=1, source_target_pairs={{0,2},{1,3},{2,0},{3,1},{4,6},{5,7},{6,4},{7,5},{8,10},{9,11},{10,... | collective-permute-start | bytes 1179656 | tf_op jit(solution)/shard_map/ppermute | solution.py:659
  93.6 17.2 %collective-permute-start.19 = (bf16[256,768]{1,0:T(8,128)(2,1)S(1)}, bf16[256,768]{1,0:T(8,128)(2,1)S(1)}, u32[]{:S(2)}, u32[]{:S(2)}) collective-permute-start(bf16[256,768]{1,0:T(8,128)(2,1)S(1)} %get-tuple-element.216.refs_10_), channel_id=1, source_target_pairs={{0,2},{1,3},{2,0},{3,1},{4,6},{5,7},{6,4},{7,5},{8,10},{9,11},{10,... | collective-permute-start | bytes 1179656 | tf_op jit(solution)/shard_map/ppermute | solution.py:659
  94.5 24.3 %collective-permute-start.18 = (bf16[256,768]{1,0:T(8,128)(2,1)S(1)}, bf16[256,768]{1,0:T(8,128)(2,1)S(1)}, u32[]{:S(2)}, u32[]{:S(2)}) collective-permute-start(bf16[256,768]{1,0:T(8,128)(2,1)S(1)} %get-tuple-element.215.refs_10_), channel_id=1, source_target_pairs={{0,2},{1,3},{2,0},{3,1},{4,6},{5,7},{6,4},{7,5},{8,10},{9,11},{10,... | collective-permute-start | bytes 1179656 | tf_op jit(solution)/shard_map/ppermute | solution.py:659
  122.3 2.4 %collective-permute-start.25 = (bf16[256,1536]{1,0:T(8,128)(2,1)S(1)}, bf16[256,1536]{1,0:T(8,128)(2,1)S(1)}, u32[]{:S(2)}, u32[]{:S(2)}) collective-permute-start(bf16[256,1536]{1,0:T(8,128)(2,1)S(1)} %get-tuple-element.231.refs_3_), channel_id=1, source_target_pairs={{0,1},{1,0},{2,3},{3,2},{4,5},{5,4},{6,7},{7,6},{8,9},{9,8},{10,11... | collective-permute-start | bytes 2359304 | tf_op jit(solution)/shard_map/ppermute | solution.py:659
  122.4 3.4 %collective-permute-start.24 = (bf16[256,1536]{1,0:T(8,128)(2,1)S(1)}, bf16[256,1536]{1,0:T(8,128)(2,1)S(1)}, u32[]{:S(2)}, u32[]{:S(2)}) collective-permute-start(bf16[256,1536]{1,0:T(8,128)(2,1)S(1)} %get-tuple-element.230.refs_1_), channel_id=1, source_target_pairs={{0,1},{1,0},{2,3},{3,2},{4,5},{5,4},{6,7},{7,6},{8,9},{9,8},{10,11... | collective-permute-start | bytes 2359304 | tf_op jit(solution)/shard_map/ppermute | solution.py:659
  122.8 4.0 %collective-permute-start.26 = (bf16[256,1536]{1,0:T(8,128)(2,1)S(1)}, bf16[256,1536]{1,0:T(8,128)(2,1)S(1)}, u32[]{:S(2)}, u32[]{:S(2)}) collective-permute-start(bf16[256,1536]{1,0:T(8,128)(2,1)S(1)} %get-tuple-element.232.refs_4_), channel_id=1, source_target_pairs={{0,1},{1,0},{2,3},{3,2},{4,5},{5,4},{6,7},{7,6},{8,9},{9,8},{10,11... | collective-permute-start | bytes 2359304 | tf_op jit(solution)/shard_map/ppermute | solution.py:659
  122.9 20.3 %collective-permute-start.30 = (bf16[512,768]{1,0:T(8,128)(2,1)S(1)}, bf16[512,768]{1,0:T(8,128)(2,1)S(1)}, u32[]{:S(2)}, u32[]{:S(2)}) collective-permute-start(bf16[512,768]{1,0:T(8,128)(2,1)S(1)} %get-tuple-element.247.refs_3_), channel_id=1, source_target_pairs={{0,2},{1,3},{2,0},{3,1},{4,6},{5,7},{6,4},{7,5},{8,10},{9,11},{10,... | collective-permute-start | bytes 2359304 | tf_op jit(solution)/shard_map/ppermute | solution.py:659
  130.0 15.4 %collective-permute-start.29 = (bf16[384,768]{1,0:T(8,128)(2,1)S(1)}, bf16[384,768]{1,0:T(8,128)(2,1)S(1)}, u32[]{:S(2)}, u32[]{:S(2)}) collective-permute-start(bf16[384,768]{1,0:T(8,128)(2,1)S(1)} %get-tuple-element.246), channel_id=1, source_target_pairs={{0,4},{4,0},{8,12},{12,8},{16,20},{20,16},{24,28},{28,24},{1,5},{5... | collective-permute-start | bytes 1769480 | tf_op jit(solution)/shard_map/ppermute | solution.py:659
  130.6 28.8 %collective-permute-start.28 = (bf16[256,768]{1,0:T(8,128)(2,1)S(1)}, bf16[256,768]{1,0:T(8,128)(2,1)S(1)}, u32[]{:S(2)}, u32[]{:S(2)}) collective-permute-start(bf16[256,768]{1,0:T(8,128)(2,1)S(1)} %get-tuple-element.238.refs_2_), channel_id=1, source_target_pairs={{0,2},{1,3},{2,0},{3,1},{4,6},{5,7},{6,4},{7,5},{8,10},{9,11},{10,... | collective-permute-start | bytes 1179656 | tf_op jit(solution)/shard_map/ppermute | solution.py:659
  146.1 12.7 %collective-permute-start.31 = (bf16[192,768]{1,0:T(8,128)(2,1)S(1)}, bf16[192,768]{1,0:T(8,128)(2,1)S(1)}, u32[]{:S(2)}, u32[]{:S(2)}) collective-permute-start(bf16[192,768]{1,0:T(8,128)(2,1)S(1)} %get-tuple-element.250), channel_id=1, source_target_pairs={{0,8},{4,12},{8,0},{12,4},{16,24},{20,28},{24,16},{28,20},{1,9},{5... | collective-permute-start | bytes 884744 | tf_op jit(solution)/shard_map/ppermute | solution.py:659
  146.5 18.6 %collective-permute-start.27 = (bf16[384,768]{1,0:T(8,128)(2,1)S(1)}, bf16[384,768]{1,0:T(8,128)(2,1)S(1)}, u32[]{:S(2)}, u32[]{:S(2)}) collective-permute-start(bf16[384,768]{1,0:T(8,128)(2,1)S(1)} %get-tuple-element.236), channel_id=1, source_target_pairs={{0,4},{4,0},{8,12},{12,8},{16,20},{20,16},{24,28},{28,24},{1,5},{5... | collective-permute-start | bytes 1769480 | tf_op jit(solution)/shard_map/ppermute | solution.py:659
  164.4 4.9 %collective-permute-start.33 = (bf16[896,384]{1,0:T(8,128)(2,1)S(1)}, bf16[896,384]{1,0:T(8,128)(2,1)S(1)}, u32[]{:S(2)}, u32[]{:S(2)}) collective-permute-start(bf16[896,384]{1,0:T(8,128)(2,1)S(1)} %get-tuple-element.266.refs_6_), channel_id=1, source_target_pairs={{0,1},{1,0},{2,3},{3,2},{4,5},{5,4},{6,7},{7,6},{8,9},{9,8},{10,11... | collective-permute-start | bytes 2064392 | tf_op jit(solution)/shard_map/ppermute | solution.py:659
  164.5 4.9 %collective-permute-start.35 = (bf16[512,640]{1,0:T(8,128)(2,1)S(1)}, bf16[512,640]{1,0:T(8,128)(2,1)S(1)}, u32[]{:S(2)}, u32[]{:S(2)}) collective-permute-start(bf16[512,640]{1,0:T(8,128)(2,1)S(1)} %get-tuple-element.278), channel_id=1, source_target_pairs={{0,1},{1,0},{2,3},{3,2},{4,5},{5,4},{6,7},{7,6},{8,9},{9,8},{10,11... | collective-permute-start | bytes 1966088 | tf_op jit(solution)/shard_map/ppermute | solution.py:659
  168.1 7.6 %collective-permute-start.34 = (bf16[768,384]{1,0:T(8,128)(2,1)S(1)}, bf16[768,384]{1,0:T(8,128)(2,1)S(1)}, u32[]{:S(2)}, u32[]{:S(2)}) collective-permute-start(bf16[768,384]{1,0:T(8,128)(2,1)S(1)} %get-tuple-element.276), channel_id=1, source_target_pairs={{0,1},{1,0},{2,3},{3,2},{4,5},{5,4},{6,7},{7,6},{8,9},{9,8},{10,11... | collective-permute-start | bytes 1769480 | tf_op jit(solution)/shard_map/ppermute | solution.py:659
  168.2 33.4 %collective-permute-start.37 = (bf16[512,768]{1,0:T(8,128)(2,1)S(1)}, bf16[512,768]{1,0:T(8,128)(2,1)S(1)}, u32[]{:S(2)}, u32[]{:S(2)}) collective-permute-start(bf16[512,768]{1,0:T(8,128)(2,1)S(1)} %get-tuple-element.286.refs_2_), channel_id=1, source_target_pairs={{0,2},{1,3},{2,0},{3,1},{4,6},{5,7},{6,4},{7,5},{8,10},{9,11},{10,... | collective-permute-start | bytes 2359304 | tf_op jit(solution)/shard_map/ppermute | solution.py:659
  173.0 14.4 %collective-permute-start.40 = (bf16[384,640]{1,0:T(8,128)(2,1)S(1)}, bf16[384,640]{1,0:T(8,128)(2,1)S(1)}, u32[]{:S(2)}, u32[]{:S(2)}) collective-permute-start(bf16[384,640]{1,0:T(8,128)(2,1)S(1)} %get-tuple-element.292), channel_id=1, source_target_pairs={{0,4},{4,0},{8,12},{12,8},{16,20},{20,16},{24,28},{28,24},{1,5},{5... | collective-permute-start | bytes 1474568 | tf_op jit(solution)/shard_map/ppermute | solution.py:659
  173.7 12.2 %collective-permute-start.32 = (bf16[192,768]{1,0:T(8,128)(2,1)S(1)}, bf16[192,768]{1,0:T(8,128)(2,1)S(1)}, u32[]{:S(2)}, u32[]{:S(2)}) collective-permute-start(bf16[192,768]{1,0:T(8,128)(2,1)S(1)} %get-tuple-element.263), channel_id=1, source_target_pairs={{0,8},{4,12},{8,0},{12,4},{16,24},{20,28},{24,16},{28,20},{1,9},{5... | collective-permute-start | bytes 884744 | tf_op jit(solution)/shard_map/ppermute | solution.py:659
  176.5 16.2 %collective-permute-start.39 = (bf16[384,384]{1,0:T(8,128)(2,1)S(1)}, bf16[384,384]{1,0:T(8,128)(2,1)S(1)}, u32[]{:S(2)}, u32[]{:S(2)}) collective-permute-start(bf16[384,384]{1,0:T(8,128)(2,1)S(1)} %get-tuple-element.290), channel_id=1, source_target_pairs={{0,4},{4,0},{8,12},{12,8},{16,20},{20,16},{24,28},{28,24},{1,5},{5... | collective-permute-start | bytes 884744 | tf_op jit(solution)/shard_map/ppermute | solution.py:659
  177.0 10.3 %collective-permute-start.41 = (bf16[96,768]{1,0:T(8,128)(2,1)S(1)}, bf16[96,768]{1,0:T(8,128)(2,1)S(1)}, u32[]{:S(2)}, u32[]{:S(2)}) collective-permute-start(bf16[96,768]{1,0:T(8,128)(2,1)S(1)} %get-tuple-element.293), channel_id=1, source_target_pairs={{0,16},{4,20},{8,24},{12,28},{16,0},{20,4},{24,8},{28,12},{1,17},{... | collective-permute-start | bytes 442376 | tf_op jit(solution)/shard_map/ppermute | solution.py:659
  185.9 15.8 %collective-permute-start.38 = (bf16[256,768]{1,0:T(8,128)(2,1)S(1)}, bf16[256,768]{1,0:T(8,128)(2,1)S(1)}, u32[]{:S(2)}, u32[]{:S(2)}) collective-permute-start(bf16[256,768]{1,0:T(8,128)(2,1)S(1)} %get-tuple-element.288.refs_5_), channel_id=1, source_target_pairs={{0,2},{1,3},{2,0},{3,1},{4,6},{5,7},{6,4},{7,5},{8,10},{9,11},{10,... | collective-permute-start | bytes 1179656 | tf_op jit(solution)/shard_map/ppermute | solution.py:659
  188.0 11.3 %collective-permute-start.43 = (bf16[192,640]{1,0:T(8,128)(2,1)S(1)}, bf16[192,640]{1,0:T(8,128)(2,1)S(1)}, u32[]{:S(2)}, u32[]{:S(2)}) collective-permute-start(bf16[192,640]{1,0:T(8,128)(2,1)S(1)} %get-tuple-element.299), channel_id=1, source_target_pairs={{0,8},{4,12},{8,0},{12,4},{16,24},{20,28},{24,16},{28,20},{1,9},{5... | collective-permute-start | bytes 737288 | tf_op jit(solution)/shard_map/ppermute | solution.py:659
  188.9 8.7 %collective-permute-start.36 = (bf16[96,768]{1,0:T(8,128)(2,1)S(1)}, bf16[96,768]{1,0:T(8,128)(2,1)S(1)}, u32[]{:S(2)}, u32[]{:S(2)}) collective-permute-start(bf16[96,768]{1,0:T(8,128)(2,1)S(1)} %get-tuple-element.284), channel_id=1, source_target_pairs={{0,16},{4,20},{8,24},{12,28},{16,0},{20,4},{24,8},{28,12},{1,17},{... | collective-permute-start | bytes 442376 | tf_op jit(solution)/shard_map/ppermute | solution.py:659
  193.3 7.8 %collective-permute-start.42 = (bf16[192,384]{1,0:T(8,128)(2,1)S(1)}, bf16[192,384]{1,0:T(8,128)(2,1)S(1)}, u32[]{:S(2)}, u32[]{:S(2)}) collective-permute-start(bf16[192,384]{1,0:T(8,128)(2,1)S(1)} %get-tuple-element.297), channel_id=1, source_target_pairs={{0,8},{4,12},{8,0},{12,4},{16,24},{20,28},{24,16},{28,20},{1,9},{5... | collective-permute-start | bytes 442376 | tf_op jit(solution)/shard_map/ppermute | solution.py:659
  202.6 8.3 %collective-permute-start.44 = (f32[768,768]{1,0:T(8,128)S(1)}, f32[768,768]{1,0:T(8,128)S(1)}, u32[]{:S(2)}, u32[]{:S(2)}) collective-permute-start(f32[768,768]{1,0:T(8,128)S(1)} %get-tuple-element.308.refs_1_), channel_id=1, source_target_pairs={{0,1},{1,0},{2,3},{3,2},{4,5},{5,4},{6,7},{7,6},{8,9},{9,8},{10,11... | collective-permute-start | bytes 7077896 | tf_op jit(solution)/shard_map/ppermute | solution.py:659
  202.6 6.2 %collective-permute-start.23 = (bf16[768,768]{1,0:T(8,128)(2,1)S(1)}, bf16[768,768]{1,0:T(8,128)(2,1)S(1)}, u32[]{:S(2)}, u32[]{:S(2)}) collective-permute-start(bf16[768,768]{1,0:T(8,128)(2,1)S(1)} %get-tuple-element.226.refs_1_), channel_id=1, source_target_pairs={{0,1},{1,0},{2,3},{3,2},{4,5},{5,4},{6,7},{7,6},{8,9},{9,8},{10,11... | collective-permute-start | bytes 3538952 | tf_op jit(solution)/shard_map/ppermute | solution.py:659
  203.1 12.0 %collective-permute-start.45 = (bf16[96,640]{1,0:T(8,128)(2,1)S(1)}, bf16[96,640]{1,0:T(8,128)(2,1)S(1)}, u32[]{:S(2)}, u32[]{:S(2)}) collective-permute-start(bf16[96,640]{1,0:T(8,128)(2,1)S(1)} %get-tuple-element.312), channel_id=1, source_target_pairs={{0,16},{4,20},{8,24},{12,28},{16,0},{20,4},{24,8},{28,12},{1,17},{... | collective-permute-start | bytes 368648 | tf_op jit(solution)/shard_map/ppermute | solution.py:659
  204.6 10.5 %collective-permute-start.46 = (bf16[96,384]{1,0:T(8,128)(2,1)S(1)}, bf16[96,384]{1,0:T(8,128)(2,1)S(1)}, u32[]{:S(2)}, u32[]{:S(2)}) collective-permute-start(bf16[96,384]{1,0:T(8,128)(2,1)S(1)} %get-tuple-element.314), channel_id=1, source_target_pairs={{0,16},{4,20},{8,24},{12,28},{16,0},{20,4},{24,8},{28,12},{1,17},{... | collective-permute-start | bytes 221192 | tf_op jit(solution)/shard_map/ppermute | solution.py:659
  (22 other events, 120.8 us)

commit v5 on v4

--- a/solution.py
+++ b/solution.py
@@ -41,7 +41,7 @@
     def __init__(self):
         self.last = None
 
-    def call(self, body, outs, ins, info, name, scratch=(), limit=12, raw_in=False, raw_out=False, deps=(), warm=(), free=False):
+    def call(self, body, outs, ins, info, name, scratch=(), limit=12, raw_in=False, raw_out=False, deps=(), warm=(), free=False, flops=1):
         ins = list(ins)
         n = len(ins) + 1
         specs = [pl.BlockSpec(memory_space=pltpu.SMEM)]
@@ -66,7 +66,7 @@
             out_specs=specs_out,
             scratch_shapes=list(scratch),
             compiler_params=pltpu.CompilerParams(vmem_limit_bytes=limit * 1024 * 1024),
-            cost_estimate=pl.CostEstimate(flops=1, bytes_accessed=1, transcendentals=0),
+            cost_estimate=pl.CostEstimate(flops=flops, bytes_accessed=1, transcendentals=0),
             name=name,
         )(info, *ins, *extra)
         if not free:
@@ -605,30 +605,25 @@
     return order.call(body, sds((rows, groups[0][0].shape[1]), F32), [x for g in groups for x in g], info, name, **kw)
 
 
-def lay_rows(order, info, mine, there, name, **kw):
-    pieces = []
-    for g, arrays in enumerate((mine, there)):
-        i = 0
-        for n, x in enumerate(arrays):
-            for r in range(0, x.shape[0], CHUNK):
-                pieces.append((g, g * len(mine) + n, r, i))
-                i += 1
-    count, arrays = len(pieces), list(mine) + list(there)
-    width = mine[0].shape[1]
+def lay_rows(order, info, groups, name, **kw):
+    arrays = [x for g in groups for x in g]
+    count = 6 * len(groups)
 
     def body(sc, *refs):
-        out, sems = refs[len(arrays)], refs[len(arrays) + 1]
+        outs, sems = refs[len(arrays) : -1], refs[-1]
         copies = []
-        for k, (g, n, r, i) in enumerate(pieces):
-            half = low_of(sc) if g == 0 else 1 - low_of(sc)
-            row = (2 * half + i) * CHUNK if i < 2 else (4 + half) * CHUNK
-            at = pl.ds(pl.multiple_of(row, CHUNK), CHUNK)
-            copies.append(pltpu.make_async_copy(refs[n].at[r : r + CHUNK, :], out.at[at, :], sems.at[k]))
-            copies[-1].start()
+        for n in range(len(arrays)):
+            half = 1 - low_of(sc) if n % 2 else low_of(sc)
+            for i in range(3):
+                row = (2 * half + i) * CHUNK if i < 2 else (4 + half) * CHUNK
+                at = pl.ds(pl.multiple_of(row, CHUNK), CHUNK)
+                part = refs[n].at[i * CHUNK : (i + 1) * CHUNK, :]
+                copies.append(pltpu.make_async_copy(part, outs[n // 2].at[at, :], sems.at[3 * n + i]))
+                copies[-1].start()
         for c in copies:
             c.wait()
 
-    outs = sds((count * CHUNK, width), mine[0].dtype)
+    outs = [sds((6 * CHUNK, g[0].shape[1]), g[0].dtype) for g in groups]
     return order.call(body, outs, arrays, info, name, scratch=[pltpu.SemaphoreType.DMA((count,))], raw_out=True, **kw)
 
 
@@ -803,17 +798,16 @@
         if direct:
             n_up = update(order, rates, [fold_u], [
                 (up_weight, first_up, second_up, DECAY_RATE, [(everything, 0, 0, units, False)])], "update_u")
-        res_full = lay_rows(order, info, [result], [res_there], "lay_out")
-        input_grad = lay_rows(order, info, [gi], [gi_there], "lay_grad")
         if direct:
             res = update(order, rates, [fold_1, fold_2], [
                 (qkv_weight, first_qkv, second_qkv, DECAY_RATE,
                  [(c, 0, c * local, local, False) for c in range(3)]),
                 (out_weight, first_out, second_out, DECAY_RATE, [(everything, 1, 0, local, True)]),
                 (norm_params, first_norm, second_norm, 0.0, [(everything, 1, local, 128, True)]),
-            ], "update_a")
+            ], "update_a", flops=100_000_000_000)
             n_down = [x.T for x in n_down]
             n_qkv, n_out, n_norm = res[:4], res[4:8], res[8:]
+        input_grad, res_full = lay_rows(order, info, [(gi, gi_there), (result, res_there)], "lay_out")
         if not direct:
             grad_o = out_mine + out_got.astype(F32)
             su, sd, sa, so = (

time: 218 us -> 216 us (level)
    pallas_call x41 -> x40, Pallas kernels: 89.1 us -> 88.5 us  [call(): pl.pallas_call(run, out_shape=shapes, in_specs=specs, out_specs=specs_out...]
  transfers between devices with their start and end apart: 47 -> 47, of which waited for: 22 -> 20; matrix products, arithmetic and copies ran while one was open for 0% -> 0% of each run, Pallas kernels for 36% -> 36%
where the time goes in v5:
time: 216 us
  Pallas kernels  88.5 us (41%)
  waiting for transfers between devices  70.3 us (33%)
  starting transfers between devices  49.1 us (23%)
  local copies, waits for them, and re-layouts  5.07 us (2%)
  between operations  2.21 us (1%)
    pallas_call x40, Pallas kernels, call(): pl.pallas_call(run, out_shape=shapes, in_specs=specs, out_specs=specs_out...  88.5 us
    ppermute x47, waiting for transfers between devices, swap(): return lax.ppermute(x, axis, [(i, i ^ bit) for i in range(size)])  70.3 us
    ppermute x47, starting transfers between devices, swap(): return lax.ppermute(x, axis, [(i, i ^ bit) for i in range(size)])  49.1 us
    unnamed x46, local copies, waits for them, and re-layouts  5.07 us
  transfers between devices with their start and end apart: 47, of which 20 were waited for; matrix products, arithmetic and copies ran while one was open for 0% of the time, Pallas kernels for 36%

profile of v5, /device:TPU:0, one launch (start us, length us, event | category | flops | bytes accessed | tf_op | source)
XLA Modules:
  0.0 216.0 jit_solution(13678490175567947998)
XLA Ops:
  4.1 3.0 %collective-permute-start.3 = (bf16[96,768]{1,0:T(8,128)(2,1)S(1)}, bf16[96,768]{1,0:T(8,128)(2,1)S(1)}, u32[]{:S(2)}, u32[]{:S(2)}) collective-permute-start(bf16[96,768]{1,0:T(8,128)(2,1)S(1)} %get-tuple-element.178.refs_1_), channel_id=1, source_target_pairs={{0,4},{4,0},{8,12},{12,8},{16,20},{20,16},{24,28},{28,24},{1,5},{5... | collective-permute-start | bytes 442376 | tf_op jit(solution)/shard_map/ppermute | solution.py:654
  7.1 1.6 collective-permute-start
  8.7 2.6 %collective-permute-start.1 = (bf16[96,768]{1,0:T(8,128)(2,1)S(1)}, bf16[96,768]{1,0:T(8,128)(2,1)S(1)}, u32[]{:S(2)}, u32[]{:S(2)}) collective-permute-start(bf16[96,768]{1,0:T(8,128)(2,1)S(1)} %get-tuple-element.178.refs_1_), channel_id=1, source_target_pairs={{0,16},{4,20},{8,24},{12,28},{16,0},{20,4},{24,8},{28,12},{1,17},{... | collective-permute-start | bytes 442376 | tf_op jit(solution)/shard_map/ppermute | solution.py:654
  11.5 1.5 collective-permute-start.4
  13.0 2.6 %collective-permute-done.4.refs_2_ = bf16[96,192]{1,0:T(8,128)(2,1)S(1)} collective-permute-done((bf16[96,192]{1,0:T(8,128)(2,1)S(1)}, bf16[96,192]{1,0:T(8,128)(2,1)S(1)}, u32[]{:S(2)}, u32[]{:S(2)}) %collective-permute-start.4) | collective-permute-done | bytes 36896 | tf_op jit(solution)/shard_map/ppermute | solution.py:654
  15.6 1.7 copy-done
  19.6 3.0 %collective-permute-done.1.refs_2_ = bf16[96,768]{1,0:T(8,128)(2,1)S(1)} collective-permute-done((bf16[96,768]{1,0:T(8,128)(2,1)S(1)}, bf16[96,768]{1,0:T(8,128)(2,1)S(1)}, u32[]{:S(2)}, u32[]{:S(2)}) %collective-permute-start.1) | collective-permute-done | bytes 147488 | tf_op jit(solution)/shard_map/ppermute | solution.py:654
  23.7 2.1 collective-permute-start.6
  28.3 3.1 %collective-permute-done.6.refs_2_ = bf16[96,1024]{1,0:T(8,128)(2,1)S(1)} collective-permute-done((bf16[96,1024]{1,0:T(8,128)(2,1)S(1)}, bf16[96,1024]{1,0:T(8,128)(2,1)S(1)}, u32[]{:S(2)}, u32[]{:S(2)}) %collective-permute-start.6) | collective-permute-done | bytes 196640 | tf_op jit(solution)/shard_map/ppermute | solution.py:654
  31.4 10.3 %collective-permute-done.7.refs_3_ = bf16[96,1024]{1,0:T(8,128)(2,1)S(1)} collective-permute-done((bf16[96,1024]{1,0:T(8,128)(2,1)S(1)}, bf16[96,1024]{1,0:T(8,128)(2,1)S(1)}, u32[]{:S(2)}, u32[]{:S(2)}) %collective-permute-start.7) | collective-permute-done | bytes 196640 | tf_op jit(solution)/shard_map/ppermute | solution.py:654
  43.1 1.6 collective-permute-start.11
  44.6 4.2 %collective-permute-start.12 = (bf16[96,768]{1,0:T(8,128)(2,1)S(1)}, bf16[96,768]{1,0:T(8,128)(2,1)S(1)}, u32[]{:S(2)}, u32[]{:S(2)}) collective-permute-start(bf16[96,768]{1,0:T(8,128)(2,1)S(1)} %bitcast.10), channel_id=1, source_target_pairs={{0,16},{4,20},{8,24},{12,28},{16,0},{20,4},{24,8},{28,12},{1,17},{... | collective-permute-start | bytes 442376 | tf_op jit(solution)/shard_map/ppermute | solution.py:654
  48.9 8.1 %attend_a.1 = (bf16[2,512,192]{2,1,0:T(8,128)(2,1)S(1)}, bf16[2,512,192]{2,1,0:T(8,128)(2,1)S(1)}, bf16[2,512,192]{2,1,0:T(8,128)(2,1)S(1)}, f32[2,512,128]{2,1,...) custom-call(s32[5]{0:T(128)S(1)} %pad_add_fusion.refs_0_, bf16[1536,768]{1,0:T(8,128)(2,1)S(1)} %copy-done.1, ...), custom_call_target="tpu_custom_call" | custom-call | flops 1 | bytes 1 | tf_op jit(solution)/shard_map/attend_a/pallas_call | solution.py:62
  57.0 1.6 collective-permute-start.10
  59.2 5.0 %attend_c.1 = (bf16[2,256,192]{2,1,0:T(8,128)(2,1)S(1)}, bf16[2,512,192]{2,1,0:T(8,128)(2,1)S(1)}, bf16[2,512,192]{2,1,0:T(8,128)(2,1)S(1)}, f32[2,256,128]{2,1,...) custom-call(s32[5]{0:T(128)S(1)} %pad_add_fusion.refs_0_, bf16[1536,768]{1,0:T(8,128)(2,1)S(1)} %copy-done.1, ...), custom_call_target="tpu_custom_call" | custom-call | flops 1 | bytes 1 | tf_op jit(solution)/shard_map/attend_c/pallas_call | solution.py:62
  64.1 3.6 %collective-permute-done.13.refs_2_ = bf16[192,768]{1,0:T(8,128)(2,1)S(1)} collective-permute-done((bf16[192,768]{1,0:T(8,128)(2,1)S(1)}, bf16[192,768]{1,0:T(8,128)(2,1)S(1)}, u32[]{:S(2)}, u32[]{:S(2)}) %collective-permute-start.13) | collective-permute-done | bytes 294944 | tf_op jit(solution)/shard_map/ppermute | solution.py:654
  70.8 1.7 collective-permute-done.14.refs_2_.refs_7_.refs_6_
  73.8 5.4 %lift_a.1 = (f32[512,768]{1,0:T(8,128)S(1)}, f32[512,128]{1,0:T(8,128)S(1)}, f32[512,1536]{1,0:T(8,128)S(1)}, bf16[512,768]{1,0:T(8,128)(2,1)S(1)}, bf16[512,1536]{1,0:T(8,128)(2,1)S(1)}, /*index=5*/f32[8,128]{1,0:T(8,128)S(1)}) custom-call(s32[5]{0:T(128)S(1)} %pad_add_fusion.refs_0_, bf16[1536,768]{1,0:T(8,128)(2,1)S(1)} %copy-done.1, ...), custom_call_target="tpu_custom_call" | custom-call | flops 1 | bytes 1 | tf_op jit(solution)/shard_map/lift_a/pallas_call | solution.py:62
  79.2 5.6 %collective-permute-done.15.refs_2_ = bf16[384,768]{1,0:T(8,128)(2,1)S(1)} collective-permute-done((bf16[384,768]{1,0:T(8,128)(2,1)S(1)}, bf16[384,768]{1,0:T(8,128)(2,1)S(1)}, u32[]{:S(2)}, u32[]{:S(2)}) %collective-permute-start.15) | collective-permute-done | bytes 589856 | tf_op jit(solution)/shard_map/ppermute | solution.py:654
  86.0 2.9 %lift_c.1 = (f32[256,768]{1,0:T(8,128)S(1)}, f32[256,128]{1,0:T(8,128)S(1)}, f32[256,1536]{1,0:T(8,128)S(1)}, bf16[256,768]{1,0:T(8,128)(2,1)S(1)}, bf16[256,1536]{1,0:T(8,128)(2,1)S(1)}, /*index=5*/f32[8,128]{1,0:T(8,128)S(1)}) custom-call(s32[5]{0:T(128)S(1)} %pad_add_fusion.refs_0_, bf16[1536,768]{1,0:T(8,128)(2,1)S(1)} %copy-done.1, ...), custom_call_target="tpu_custom_call" | custom-call | flops 1 | bytes 1 | tf_op jit(solution)/shard_map/lift_c/pallas_call | solution.py:62
  91.6 2.0 drop_a.1
  95.7 6.7 %collective-permute-done.19.refs_11_ = bf16[256,768]{1,0:T(8,128)(2,1)S(1)} collective-permute-done((bf16[256,768]{1,0:T(8,128)(2,1)S(1)}, bf16[256,768]{1,0:T(8,128)(2,1)S(1)}, u32[]{:S(2)}, u32[]{:S(2)}) %collective-permute-start.19) | collective-permute-done | bytes 393248 | tf_op jit(solution)/shard_map/ppermute | solution.py:654
  102.4 3.4 %turn_c.1 = (bf16[256,768]{1,0:T(8,128)(2,1)S(1)}, f32[256,768]{1,0:T(8,128)S(1)}, bf16[256,768]{1,0:T(8,128)(2,1)S(1)}, bf16[256,1536]{1,0:T(8,128)(2,1)S(1)}, ...) custom-call(s32[5]{0:T(128)S(1)} %pad_add_fusion.refs_0_, ...), custom_call_target="tpu_custom_call" | custom-call | flops 1 | bytes 1 | tf_op jit(solution)/shard_map/turn_c/pallas_call | solution.py:62
  105.8 5.0 %collective-permute-done.18.refs_11_ = bf16[256,768]{1,0:T(8,128)(2,1)S(1)} collective-permute-done((bf16[256,768]{1,0:T(8,128)(2,1)S(1)}, bf16[256,768]{1,0:T(8,128)(2,1)S(1)}, u32[]{:S(2)}, u32[]{:S(2)}) %collective-permute-start.18) | collective-permute-done | bytes 393248 | tf_op jit(solution)/shard_map/ppermute | solution.py:654
  110.8 3.4 %turn_0.1 = (bf16[256,768]{1,0:T(8,128)(2,1)S(1)}, f32[256,768]{1,0:T(8,128)S(1)}, bf16[256,768]{1,0:T(8,128)(2,1)S(1)}, bf16[256,1536]{1,0:T(8,128)(2,1)S(1)}, ...) custom-call(s32[5]{0:T(128)S(1)} %pad_add_fusion.refs_0_, ...), custom_call_target="tpu_custom_call" | custom-call | flops 1 | bytes 1 | tf_op jit(solution)/shard_map/turn_0/pallas_call | solution.py:62
  114.2 4.5 %collective-permute-done.22.refs_11_ = bf16[256,768]{1,0:T(8,128)(2,1)S(1)} collective-permute-done((bf16[256,768]{1,0:T(8,128)(2,1)S(1)}, bf16[256,768]{1,0:T(8,128)(2,1)S(1)}, u32[]{:S(2)}, u32[]{:S(2)}) %collective-permute-start.22) | collective-permute-done | bytes 393248 | tf_op jit(solution)/shard_map/ppermute | solution.py:654
  118.8 3.5 %turn_1.1 = (bf16[768,768]{1,0:T(8,128)(2,1)S(1)}, f32[256,768]{1,0:T(8,128)S(1)}, bf16[256,768]{1,0:T(8,128)(2,1)S(1)}, bf16[256,1536]{1,0:T(8,128)(2,1)S(1)}, ...) custom-call(s32[5]{0:T(128)S(1)} %pad_add_fusion.refs_0_, ...), custom_call_target="tpu_custom_call" | custom-call | flops 1 | bytes 1 | tf_op jit(solution)/shard_map/turn_1/pallas_call | solution.py:62
  126.9 3.1 %grads_d.1 = (f32[384,768]{1,0:T(8,128)S(1)}, bf16[384,768]{1,0:T(8,128)(2,1)S(1)}, f32[8,128]{1,0:T(8,128)S(1)}) custom-call(s32[5]{0:T(128)S(1)} %pad_add_fusion.refs_0_, bf16[256,1536]{1,0:T(8,128)(2,1)S(1)} %get-tuple-element.234.refs_1_, bf16[512,768]{1,0:T(8,128)(2,1)S(1)} %get-tuple-element.207.refs_1_.refs_2_, ...), custom_call_target="tpu_custom_call" | custom-call | flops 1 | bytes 1 | tf_op jit(solution)/shard_map/grads_d/pallas_call | solution.py:62
  131.8 3.4 %grads_u.1 = (f32[384,768]{1,0:T(8,128)S(1)}, bf16[384,768]{1,0:T(8,128)(2,1)S(1)}, f32[8,128]{1,0:T(8,128)S(1)}) custom-call(s32[5]{0:T(128)S(1)} %pad_add_fusion.refs_0_, bf16[512,1536]{1,0:T(8,128)(2,1)S(1)} %get-tuple-element.208.refs_2_.refs_1_, bf16[256,768]{1,0:T(8,128)(2,1)S(1)} %get-tuple-element.240.refs_2_, ...), custom_call_target="tpu_custom_call" | custom-call | flops 1 | bytes 1 | tf_op jit(solution)/shard_map/grads_u/pallas_call | solution.py:62
  135.1 8.2 %collective-permute-done.23.refs_3_.refs_4_ = bf16[512,768]{1,0:T(8,128)(2,1)S(1)} collective-permute-done((bf16[512,768]{1,0:T(8,128)(2,1)S(1)}, bf16[512,768]{1,0:T(8,128)(2,1)S(1)}, u32[]{:S(2)}, u32[]{:S(2)}) %collective-permute-start.23) | collective-permute-done | bytes 786464 | tf_op jit(solution)/shard_map/ppermute | solution.py:654
  143.3 2.2 %collective-permute-done.27.refs_2_ = bf16[384,768]{1,0:T(8,128)(2,1)S(1)} collective-permute-done((bf16[384,768]{1,0:T(8,128)(2,1)S(1)}, bf16[384,768]{1,0:T(8,128)(2,1)S(1)}, u32[]{:S(2)}, u32[]{:S(2)}) %collective-permute-start.27) | collective-permute-done | bytes 589856 | tf_op jit(solution)/shard_map/ppermute | solution.py:654
  147.7 11.2 %back_a.1 = (f32[512,768]{1,0:T(8,128)S(1)}, bf16[512,768]{1,0:T(8,128)(2,1)S(1)}, bf16[512,576]{1,0:T(8,128)(2,1)S(1)}, bf16[512,640]{1,0:T(8,128)(2,1)S(1)}, f...) custom-call(s32[5]{0:T(128)S(1)} %pad_add_fusion.refs_0_, ...), custom_call_target="tpu_custom_call" | custom-call | flops 1 | bytes 1 | tf_op jit(solution)/shard_map/back_a/pallas_call | solution.py:62
  159.4 5.0 %back_c.1 = (f32[256,768]{1,0:T(8,128)S(1)}, bf16[256,768]{1,0:T(8,128)(2,1)S(1)}, f32[8,768]{1,0:T(8,128)S(1)}, bf16[2,256,192]{2,1,0:T(8,128)(2,1)S(1)}, f32[2...) custom-call(s32[5]{0:T(128)S(1)} %pad_add_fusion.refs_0_, ...), custom_call_target="tpu_custom_call" | custom-call | flops 1 | bytes 1 | tf_op jit(solution)/shard_map/back_c/pallas_call | solution.py:62
  165.7 2.4 %grads_out.1 = (f32[768,384]{1,0:T(8,128)S(1)}, bf16[768,384]{1,0:T(8,128)(2,1)S(1)}, f32[8,128]{1,0:T(8,128)S(1)}) custom-call(s32[5]{0:T(128)S(1)} %pad_add_fusion.refs_0_, bf16[512,768]{1,0:T(8,128)(2,1)S(1)} %get-tuple-element.263.refs_1_, bf16[256,768]{1,0:T(8,128)(2,1)S(1)} %get-tuple-element.264.refs_2_, ...), custom_call_target="tpu_custom_call" | custom-call | flops 1 | bytes 1 | tf_op jit(solution)/shard_map/grads_out/pallas_call | solution.py:62
  168.2 3.6 %grads_attn.1 = (f32[384,640]{1,0:T(8,128)S(1)}, bf16[384,640]{1,0:T(8,128)(2,1)S(1)}, f32[8,128]{1,0:T(8,128)S(1)}) custom-call(s32[5]{0:T(128)S(1)} %pad_add_fusion.refs_0_, bf16[1536,768]{1,0:T(8,128)(2,1)S(1)} %copy-done.1, bf16[512,576]{1,0:T(8,128)(2,1)S(1)} %get-tuple-element.276.refs_2_, bf16[512,640]{1,0:T(8,128)(2,1)S(1)} %collective-permute-done.34.refs_3_, ...), custom_call_target="tpu_custom_call" | custom-call | flops 1 | bytes 1 | tf_op jit(solution)/shard_map/grads_attn/pallas_call | solution.py:62
  173.7 1.9 collective-permute-start.39
  177.0 2.5 %collective-permute-start.38 = (bf16[96,768]{1,0:T(8,128)(2,1)S(1)}, bf16[96,768]{1,0:T(8,128)(2,1)S(1)}, u32[]{:S(2)}, u32[]{:S(2)}) collective-permute-start(bf16[96,768]{1,0:T(8,128)(2,1)S(1)} %get-tuple-element.286), channel_id=1, source_target_pairs={{0,16},{4,20},{8,24},{12,28},{16,0},{20,4},{24,8},{28,12},{1,17},{... | collective-permute-start | bytes 442376 | tf_op jit(solution)/shard_map/ppermute | solution.py:654
  181.0 4.8 %collective-permute-done.39.refs_2_ = bf16[192,768]{1,0:T(8,128)(2,1)S(1)} collective-permute-done((bf16[192,768]{1,0:T(8,128)(2,1)S(1)}, bf16[192,768]{1,0:T(8,128)(2,1)S(1)}, u32[]{:S(2)}, u32[]{:S(2)}) %collective-permute-start.39) | collective-permute-done | bytes 294944 | tf_op jit(solution)/shard_map/ppermute | solution.py:654
  188.1 3.2 %collective-permute-start.42 = (bf16[96,768]{1,0:T(8,128)(2,1)S(1)}, bf16[96,768]{1,0:T(8,128)(2,1)S(1)}, u32[]{:S(2)}, u32[]{:S(2)}) collective-permute-start(bf16[96,768]{1,0:T(8,128)(2,1)S(1)} %get-tuple-element.296), channel_id=1, source_target_pairs={{0,16},{4,20},{8,24},{12,28},{16,0},{20,4},{24,8},{28,12},{1,17},{... | collective-permute-start | bytes 442376 | tf_op jit(solution)/shard_map/ppermute | solution.py:654
  193.6 1.7 update_d.1
  195.3 2.1 collective-permute-done.42.refs_3_.refs_2_
  197.4 1.8 collective-permute-done.41.refs_2_
  199.8 1.7 collective-permute-start.45
  202.2 1.8 collective-permute-start.46
  205.7 1.7 update_u.1
  207.4 2.2 %collective-permute-done.46.refs_4_ = bf16[96,384]{1,0:T(8,128)(2,1)S(1)} collective-permute-done((bf16[96,384]{1,0:T(8,128)(2,1)S(1)}, bf16[96,384]{1,0:T(8,128)(2,1)S(1)}, u32[]{:S(2)}, u32[]{:S(2)}) %collective-permute-start.46) | collective-permute-done | bytes 73760 | tf_op jit(solution)/shard_map/ppermute | solution.py:654
  209.7 1.9 update_a.1
  211.7 4.1 %lay_out.1 = (f32[1536,768]{1,0:T(8,128)}, bf16[1536,768]{1,0:T(8,128)(2,1)}, f32[8,128]{1,0:T(8,128)}) custom-call(s32[5]{0:T(128)S(1)} %pad_add_fusion.refs_0_, f32[768,768]{1,0:T(8,128)S(1)} %get-tuple-element.302.refs_1_, f32[768,768]{1,0:T(8,128)S(1)} %collective-permute-done.43.refs_2_, bf16[768,768]{1,0:T(8,128)(2,1)S(1)} %get-tuple-element.303.refs_3_, ...), custom_call_target="tpu_custom_call" | custom-call | flops 1 | bytes 1 | tf_op jit(solution)/shard_map/lay_out/pallas_call | solution.py:62
  (134 shorter events, 43.8 us)
Async XLA Ops:
  4.1 15.5 %collective-permute-start.3 = (bf16[96,768]{1,0:T(8,128)(2,1)S(1)}, bf16[96,768]{1,0:T(8,128)(2,1)S(1)}, u32[]{:S(2)}, u32[]{:S(2)}) collective-permute-start(bf16[96,768]{1,0:T(8,128)(2,1)S(1)} %get-tuple-element.178.refs_1_), channel_id=1, source_target_pairs={{0,4},{4,0},{8,12},{12,8},{16,20},{20,16},{24,28},{28,24},{1,5},{5... | collective-permute-start | bytes 442376 | tf_op jit(solution)/shard_map/ppermute | solution.py:654
  7.1 12.5 %collective-permute-start = (bf16[96,768]{1,0:T(8,128)(2,1)S(1)}, bf16[96,768]{1,0:T(8,128)(2,1)S(1)}, u32[]{:S(2)}, u32[]{:S(2)}) collective-permute-start(bf16[96,768]{1,0:T(8,128)(2,1)S(1)} %get-tuple-element.178.refs_1_), channel_id=1, source_target_pairs={{0,8},{4,12},{8,0},{12,4},{16,24},{20,28},{24,16},{28,20},{1,9},{5... | collective-permute-start | bytes 442376 | tf_op jit(solution)/shard_map/ppermute | solution.py:654
  8.7 13.9 %collective-permute-start.1 = (bf16[96,768]{1,0:T(8,128)(2,1)S(1)}, bf16[96,768]{1,0:T(8,128)(2,1)S(1)}, u32[]{:S(2)}, u32[]{:S(2)}) collective-permute-start(bf16[96,768]{1,0:T(8,128)(2,1)S(1)} %get-tuple-element.178.refs_1_), channel_id=1, source_target_pairs={{0,16},{4,20},{8,24},{12,28},{16,0},{20,4},{24,8},{28,12},{1,17},{... | collective-permute-start | bytes 442376 | tf_op jit(solution)/shard_map/ppermute | solution.py:654
  11.3 11.3 %collective-permute-start.2 = (bf16[96,768]{1,0:T(8,128)(2,1)S(1)}, bf16[96,768]{1,0:T(8,128)(2,1)S(1)}, u32[]{:S(2)}, u32[]{:S(2)}) collective-permute-start(bf16[96,768]{1,0:T(8,128)(2,1)S(1)} %get-tuple-element.178.refs_1_), channel_id=1, source_target_pairs={{0,24},{4,28},{8,16},{12,20},{16,8},{20,12},{24,0},{28,4},{1,25},{... | collective-permute-start | bytes 442376 | tf_op jit(solution)/shard_map/ppermute | solution.py:654
  11.5 4.1 %collective-permute-start.4 = (bf16[96,192]{1,0:T(8,128)(2,1)S(1)}, bf16[96,192]{1,0:T(8,128)(2,1)S(1)}, u32[]{:S(2)}, u32[]{:S(2)}) collective-permute-start(bf16[96,192]{1,0:T(8,128)(2,1)S(1)} %get-tuple-element.179), channel_id=1, source_target_pairs={{0,2},{1,3},{2,0},{3,1},{4,6},{5,7},{6,4},{7,5},{8,10},{9,11},{10,... | collective-permute-start | bytes 110600 | tf_op jit(solution)/shard_map/ppermute | solution.py:654
  19.5 29.3 %copy-start.1 = (bf16[1536,768]{1,0:T(8,128)(2,1)S(1)}, bf16[1536,768]{1,0:T(8,128)(2,1)}, u32[]{:S(2)}) copy-start(bf16[1536,768]{1,0:T(8,128)(2,1)} %refs_1_.13) | copy-start | bytes 7077892
  23.1 19.2 %collective-permute-start.5 = (bf16[288,768]{1,0:T(8,128)(2,1)S(1)}, bf16[288,768]{1,0:T(8,128)(2,1)S(1)}, u32[]{:S(2)}, u32[]{:S(2)}) collective-permute-start(bf16[288,768]{1,0:T(8,128)(2,1)S(1)} %get-tuple-element.182.refs_2_), channel_id=1, source_target_pairs={{0,4},{4,0},{8,12},{12,8},{16,20},{20,16},{24,28},{28,24},{1,5},{5... | collective-permute-start | bytes 1327112 | tf_op jit(solution)/shard_map/ppermute | solution.py:654
  23.7 7.7 %collective-permute-start.6 = (bf16[96,1024]{1,0:T(8,128)(2,1)S(1)}, bf16[96,1024]{1,0:T(8,128)(2,1)S(1)}, u32[]{:S(2)}, u32[]{:S(2)}) collective-permute-start(bf16[96,1024]{1,0:T(8,128)(2,1)S(1)} %get-tuple-element.183.refs_1_), channel_id=1, source_target_pairs={{0,8},{4,12},{8,0},{12,4},{16,24},{20,28},{24,16},{28,20},{1,9},{5... | collective-permute-start | bytes 589832 | tf_op jit(solution)/shard_map/ppermute | solution.py:654
  25.9 15.9 %collective-permute-start.7 = (bf16[96,1024]{1,0:T(8,128)(2,1)S(1)}, bf16[96,1024]{1,0:T(8,128)(2,1)S(1)}, u32[]{:S(2)}, u32[]{:S(2)}) collective-permute-start(bf16[96,1024]{1,0:T(8,128)(2,1)S(1)} %get-tuple-element.183.refs_1_), channel_id=1, source_target_pairs={{0,16},{4,20},{8,24},{12,28},{16,0},{20,4},{24,8},{28,12},{1,17},{... | collective-permute-start | bytes 589832 | tf_op jit(solution)/shard_map/ppermute | solution.py:654
  26.9 14.9 %collective-permute-start.8 = (bf16[96,1024]{1,0:T(8,128)(2,1)S(1)}, bf16[96,1024]{1,0:T(8,128)(2,1)S(1)}, u32[]{:S(2)}, u32[]{:S(2)}) collective-permute-start(bf16[96,1024]{1,0:T(8,128)(2,1)S(1)} %get-tuple-element.183.refs_1_), channel_id=1, source_target_pairs={{0,24},{4,28},{8,16},{12,20},{16,8},{20,12},{24,0},{28,4},{1,25},{... | collective-permute-start | bytes 589832 | tf_op jit(solution)/shard_map/ppermute | solution.py:654
  43.0 5.8 %collective-permute-start.9 = (bf16[768,768]{1,0:T(8,128)(2,1)S(1)}, bf16[768,768]{1,0:T(8,128)(2,1)S(1)}, u32[]{:S(2)}, u32[]{:S(2)}) collective-permute-start(bf16[768,768]{1,0:T(8,128)(2,1)S(1)} %get-tuple-element.186.refs_2_.refs_3_.refs_13_.refs_4_), channel_id=1, source_target_pairs={{0,1},{1,0},{2,3},{3,2},{4,5},{5,4},{6,7},{7,6},{8,9},{9,8},{10,11... | collective-permute-start | bytes 3538952 | tf_op jit(solution)/shard_map/ppermute | solution.py:654
  43.1 25.2 %collective-permute-start.11 = (bf16[384,1024]{1,0:T(8,128)(2,1)S(1)}, bf16[384,1024]{1,0:T(8,128)(2,1)S(1)}, u32[]{:S(2)}, u32[]{:S(2)}) collective-permute-start(bf16[384,1024]{1,0:T(8,128)(2,1)S(1)} %get-tuple-element.189.refs_1_), channel_id=1, source_target_pairs={{0,4},{4,0},{8,12},{12,8},{16,20},{20,16},{24,28},{28,24},{1,5},{5... | collective-permute-start | bytes 2359304 | tf_op jit(solution)/shard_map/ppermute | solution.py:654
  44.6 13.9 %collective-permute-start.12 = (bf16[96,768]{1,0:T(8,128)(2,1)S(1)}, bf16[96,768]{1,0:T(8,128)(2,1)S(1)}, u32[]{:S(2)}, u32[]{:S(2)}) collective-permute-start(bf16[96,768]{1,0:T(8,128)(2,1)S(1)} %bitcast.10), channel_id=1, source_target_pairs={{0,16},{4,20},{8,24},{12,28},{16,0},{20,4},{24,8},{28,12},{1,17},{... | collective-permute-start | bytes 442376 | tf_op jit(solution)/shard_map/ppermute | solution.py:654
  57.0 11.3 %collective-permute-start.10 = (bf16[512,384]{1,0:T(8,128)(2,1)S(1)}, bf16[512,384]{1,0:T(8,128)(2,1)S(1)}, u32[]{:S(2)}, u32[]{:S(2)}) collective-permute-start(bf16[512,384]{1,0:T(8,128)(2,1)S(1)} %get-tuple-element.188.refs_2_.refs_3_), channel_id=1, source_target_pairs={{0,2},{1,3},{2,0},{3,1},{4,6},{5,7},{6,4},{7,5},{8,10},{9,11},{10,... | collective-permute-start | bytes 1179656 | tf_op jit(solution)/shard_map/ppermute | solution.py:654
  59.1 8.6 %collective-permute-start.13 = (bf16[192,768]{1,0:T(8,128)(2,1)S(1)}, bf16[192,768]{1,0:T(8,128)(2,1)S(1)}, u32[]{:S(2)}, u32[]{:S(2)}) collective-permute-start(bf16[192,768]{1,0:T(8,128)(2,1)S(1)} %get-tuple-element.191.refs_1_), channel_id=1, source_target_pairs={{0,8},{4,12},{8,0},{12,4},{16,24},{20,28},{24,16},{28,20},{1,9},{5... | collective-permute-start | bytes 884744 | tf_op jit(solution)/shard_map/ppermute | solution.py:654
  69.0 3.5 %collective-permute-start.14 = (bf16[768,1024]{1,0:T(8,128)(2,1)S(1)}, bf16[768,1024]{1,0:T(8,128)(2,1)S(1)}, u32[]{:S(2)}, u32[]{:S(2)}) collective-permute-start(bf16[768,1024]{1,0:T(8,128)(2,1)S(1)} %get-tuple-element.195.refs_1_.refs_6_.refs_5_), channel_id=1, source_target_pairs={{0,1},{1,0},{2,3},{3,2},{4,5},{5,4},{6,7},{7,6},{8,9},{9,8},{10,11... | collective-permute-start | bytes 4718600 | tf_op jit(solution)/shard_map/ppermute | solution.py:654
  69.0 15.7 %collective-permute-start.15 = (bf16[384,768]{1,0:T(8,128)(2,1)S(1)}, bf16[384,768]{1,0:T(8,128)(2,1)S(1)}, u32[]{:S(2)}, u32[]{:S(2)}) collective-permute-start(bf16[384,768]{1,0:T(8,128)(2,1)S(1)} %get-tuple-element.202.refs_1_), channel_id=1, source_target_pairs={{0,4},{4,0},{8,12},{12,8},{16,20},{20,16},{24,28},{28,24},{1,5},{5... | collective-permute-start | bytes 1769480 | tf_op jit(solution)/shard_map/ppermute | solution.py:654
  69.6 9.6 %collective-permute-start.16 = (bf16[256,384]{1,0:T(8,128)(2,1)S(1)}, bf16[256,384]{1,0:T(8,128)(2,1)S(1)}, u32[]{:S(2)}, u32[]{:S(2)}) collective-permute-start(bf16[256,384]{1,0:T(8,128)(2,1)S(1)} %get-tuple-element.203.refs_2_.refs_4_), channel_id=1, source_target_pairs={{0,2},{1,3},{2,0},{3,1},{4,6},{5,7},{6,4},{7,5},{8,10},{9,11},{10,... | collective-permute-start | bytes 589832 | tf_op jit(solution)/shard_map/ppermute | solution.py:654
  85.4 3.6 %collective-permute-start.17 = (bf16[768,768]{1,0:T(8,128)(2,1)S(1)}, bf16[768,768]{1,0:T(8,128)(2,1)S(1)}, u32[]{:S(2)}, u32[]{:S(2)}) collective-permute-start(bf16[768,768]{1,0:T(8,128)(2,1)S(1)} %get-tuple-element.205.refs_3_.refs_7_), channel_id=1, source_target_pairs={{0,1},{1,0},{2,3},{3,2},{4,5},{5,4},{6,7},{7,6},{8,9},{9,8},{10,11... | collective-permute-start | bytes 3538952 | tf_op jit(solution)/shard_map/ppermute | solution.py:654
  85.5 10.2 %collective-permute-start.20 = (bf16[512,1536]{1,0:T(8,128)(2,1)S(1)}, bf16[512,1536]{1,0:T(8,128)(2,1)S(1)}, u32[]{:S(2)}, u32[]{:S(2)}) collective-permute-start(bf16[512,1536]{1,0:T(8,128)(2,1)S(1)} %get-tuple-element.208.refs_2_.refs_1_), channel_id=1, source_target_pairs={{0,1},{1,0},{2,3},{3,2},{4,5},{5,4},{6,7},{7,6},{8,9},{9,8},{10,11... | collective-permute-start | bytes 4718600 | tf_op jit(solution)/shard_map/ppermute | solution.py:654
  88.9 6.8 %collective-permute-start.21 = (bf16[256,1536]{1,0:T(8,128)(2,1)S(1)}, bf16[256,1536]{1,0:T(8,128)(2,1)S(1)}, u32[]{:S(2)}, u32[]{:S(2)}) collective-permute-start(bf16[256,1536]{1,0:T(8,128)(2,1)S(1)} %get-tuple-element.211.refs_2_.refs_4_), channel_id=1, source_target_pairs={{0,1},{1,0},{2,3},{3,2},{4,5},{5,4},{6,7},{7,6},{8,9},{9,8},{10,11... | collective-permute-start | bytes 2359304 | tf_op jit(solution)/shard_map/ppermute | solution.py:654
  90.4 12.0 %collective-permute-start.19 = (bf16[256,768]{1,0:T(8,128)(2,1)S(1)}, bf16[256,768]{1,0:T(8,128)(2,1)S(1)}, u32[]{:S(2)}, u32[]{:S(2)}) collective-permute-start(bf16[256,768]{1,0:T(8,128)(2,1)S(1)} %get-tuple-element.217.refs_10_), channel_id=1, source_target_pairs={{0,2},{1,3},{2,0},{3,1},{4,6},{5,7},{6,4},{7,5},{8,10},{9,11},{10,... | collective-permute-start | bytes 1179656 | tf_op jit(solution)/shard_map/ppermute | solution.py:654
  93.6 17.2 %collective-permute-start.18 = (bf16[256,768]{1,0:T(8,128)(2,1)S(1)}, bf16[256,768]{1,0:T(8,128)(2,1)S(1)}, u32[]{:S(2)}, u32[]{:S(2)}) collective-permute-start(bf16[256,768]{1,0:T(8,128)(2,1)S(1)} %get-tuple-element.214.refs_10_), channel_id=1, source_target_pairs={{0,2},{1,3},{2,0},{3,1},{4,6},{5,7},{6,4},{7,5},{8,10},{9,11},{10,... | collective-permute-start | bytes 1179656 | tf_op jit(solution)/shard_map/ppermute | solution.py:654
  94.5 24.3 %collective-permute-start.22 = (bf16[256,768]{1,0:T(8,128)(2,1)S(1)}, bf16[256,768]{1,0:T(8,128)(2,1)S(1)}, u32[]{:S(2)}, u32[]{:S(2)}) collective-permute-start(bf16[256,768]{1,0:T(8,128)(2,1)S(1)} %get-tuple-element.221.refs_10_), channel_id=1, source_target_pairs={{0,2},{1,3},{2,0},{3,1},{4,6},{5,7},{6,4},{7,5},{8,10},{9,11},{10,... | collective-permute-start | bytes 1179656 | tf_op jit(solution)/shard_map/ppermute | solution.py:654
  122.3 2.4 %collective-permute-start.25 = (bf16[256,1536]{1,0:T(8,128)(2,1)S(1)}, bf16[256,1536]{1,0:T(8,128)(2,1)S(1)}, u32[]{:S(2)}, u32[]{:S(2)}) collective-permute-start(bf16[256,1536]{1,0:T(8,128)(2,1)S(1)} %get-tuple-element.235.refs_3_), channel_id=1, source_target_pairs={{0,1},{1,0},{2,3},{3,2},{4,5},{5,4},{6,7},{7,6},{8,9},{9,8},{10,11... | collective-permute-start | bytes 2359304 | tf_op jit(solution)/shard_map/ppermute | solution.py:654
  122.4 3.4 %collective-permute-start.24 = (bf16[256,1536]{1,0:T(8,128)(2,1)S(1)}, bf16[256,1536]{1,0:T(8,128)(2,1)S(1)}, u32[]{:S(2)}, u32[]{:S(2)}) collective-permute-start(bf16[256,1536]{1,0:T(8,128)(2,1)S(1)} %get-tuple-element.234.refs_1_), channel_id=1, source_target_pairs={{0,1},{1,0},{2,3},{3,2},{4,5},{5,4},{6,7},{7,6},{8,9},{9,8},{10,11... | collective-permute-start | bytes 2359304 | tf_op jit(solution)/shard_map/ppermute | solution.py:654
  122.8 4.0 %collective-permute-start.26 = (bf16[256,1536]{1,0:T(8,128)(2,1)S(1)}, bf16[256,1536]{1,0:T(8,128)(2,1)S(1)}, u32[]{:S(2)}, u32[]{:S(2)}) collective-permute-start(bf16[256,1536]{1,0:T(8,128)(2,1)S(1)} %get-tuple-element.236.refs_4_), channel_id=1, source_target_pairs={{0,1},{1,0},{2,3},{3,2},{4,5},{5,4},{6,7},{7,6},{8,9},{9,8},{10,11... | collective-permute-start | bytes 2359304 | tf_op jit(solution)/shard_map/ppermute | solution.py:654
  122.9 20.3 %collective-permute-start.23 = (bf16[512,768]{1,0:T(8,128)(2,1)S(1)}, bf16[512,768]{1,0:T(8,128)(2,1)S(1)}, u32[]{:S(2)}, u32[]{:S(2)}) collective-permute-start(bf16[512,768]{1,0:T(8,128)(2,1)S(1)} %get-tuple-element.227.refs_3_), channel_id=1, source_target_pairs={{0,2},{1,3},{2,0},{3,1},{4,6},{5,7},{6,4},{7,5},{8,10},{9,11},{10,... | collective-permute-start | bytes 2359304 | tf_op jit(solution)/shard_map/ppermute | solution.py:654
  130.0 15.4 %collective-permute-start.27 = (bf16[384,768]{1,0:T(8,128)(2,1)S(1)}, bf16[384,768]{1,0:T(8,128)(2,1)S(1)}, u32[]{:S(2)}, u32[]{:S(2)}) collective-permute-start(bf16[384,768]{1,0:T(8,128)(2,1)S(1)} %get-tuple-element.239), channel_id=1, source_target_pairs={{0,4},{4,0},{8,12},{12,8},{16,20},{20,16},{24,28},{28,24},{1,5},{5... | collective-permute-start | bytes 1769480 | tf_op jit(solution)/shard_map/ppermute | solution.py:654
  130.6 28.8 %collective-permute-start.29 = (bf16[256,768]{1,0:T(8,128)(2,1)S(1)}, bf16[256,768]{1,0:T(8,128)(2,1)S(1)}, u32[]{:S(2)}, u32[]{:S(2)}) collective-permute-start(bf16[256,768]{1,0:T(8,128)(2,1)S(1)} %get-tuple-element.249.refs_2_), channel_id=1, source_target_pairs={{0,2},{1,3},{2,0},{3,1},{4,6},{5,7},{6,4},{7,5},{8,10},{9,11},{10,... | collective-permute-start | bytes 1179656 | tf_op jit(solution)/shard_map/ppermute | solution.py:654
  146.1 12.7 %collective-permute-start.30 = (bf16[192,768]{1,0:T(8,128)(2,1)S(1)}, bf16[192,768]{1,0:T(8,128)(2,1)S(1)}, u32[]{:S(2)}, u32[]{:S(2)}) collective-permute-start(bf16[192,768]{1,0:T(8,128)(2,1)S(1)} %get-tuple-element.256), channel_id=1, source_target_pairs={{0,8},{4,12},{8,0},{12,4},{16,24},{20,28},{24,16},{28,20},{1,9},{5... | collective-permute-start | bytes 884744 | tf_op jit(solution)/shard_map/ppermute | solution.py:654
  146.5 18.6 %collective-permute-start.32 = (bf16[384,768]{1,0:T(8,128)(2,1)S(1)}, bf16[384,768]{1,0:T(8,128)(2,1)S(1)}, u32[]{:S(2)}, u32[]{:S(2)}) collective-permute-start(bf16[384,768]{1,0:T(8,128)(2,1)S(1)} %get-tuple-element.271), channel_id=1, source_target_pairs={{0,4},{4,0},{8,12},{12,8},{16,20},{20,16},{24,28},{28,24},{1,5},{5... | collective-permute-start | bytes 1769480 | tf_op jit(solution)/shard_map/ppermute | solution.py:654
  164.5 3.8 %collective-permute-start.31 = (bf16[896,384]{1,0:T(8,128)(2,1)S(1)}, bf16[896,384]{1,0:T(8,128)(2,1)S(1)}, u32[]{:S(2)}, u32[]{:S(2)}) collective-permute-start(bf16[896,384]{1,0:T(8,128)(2,1)S(1)} %get-tuple-element.262.refs_6_), channel_id=1, source_target_pairs={{0,1},{1,0},{2,3},{3,2},{4,5},{5,4},{6,7},{7,6},{8,9},{9,8},{10,11... | collective-permute-start | bytes 2064392 | tf_op jit(solution)/shard_map/ppermute | solution.py:654
  164.5 3.7 %collective-permute-start.34 = (bf16[512,640]{1,0:T(8,128)(2,1)S(1)}, bf16[512,640]{1,0:T(8,128)(2,1)S(1)}, u32[]{:S(2)}, u32[]{:S(2)}) collective-permute-start(bf16[512,640]{1,0:T(8,128)(2,1)S(1)} %get-tuple-element.277), channel_id=1, source_target_pairs={{0,1},{1,0},{2,3},{3,2},{4,5},{5,4},{6,7},{7,6},{8,9},{9,8},{10,11... | collective-permute-start | bytes 1966088 | tf_op jit(solution)/shard_map/ppermute | solution.py:654
  168.1 7.5 %collective-permute-start.33 = (bf16[768,384]{1,0:T(8,128)(2,1)S(1)}, bf16[768,384]{1,0:T(8,128)(2,1)S(1)}, u32[]{:S(2)}, u32[]{:S(2)}) collective-permute-start(bf16[768,384]{1,0:T(8,128)(2,1)S(1)} %get-tuple-element.275), channel_id=1, source_target_pairs={{0,1},{1,0},{2,3},{3,2},{4,5},{5,4},{6,7},{7,6},{8,9},{9,8},{10,11... | collective-permute-start | bytes 1769480 | tf_op jit(solution)/shard_map/ppermute | solution.py:654
  171.8 15.5 %collective-permute-start.37 = (bf16[384,640]{1,0:T(8,128)(2,1)S(1)}, bf16[384,640]{1,0:T(8,128)(2,1)S(1)}, u32[]{:S(2)}, u32[]{:S(2)}) collective-permute-start(bf16[384,640]{1,0:T(8,128)(2,1)S(1)} %get-tuple-element.285), channel_id=1, source_target_pairs={{0,4},{4,0},{8,12},{12,8},{16,20},{20,16},{24,28},{28,24},{1,5},{5... | collective-permute-start | bytes 1474568 | tf_op jit(solution)/shard_map/ppermute | solution.py:654
  172.8 31.3 %collective-permute-start.28 = (bf16[512,768]{1,0:T(8,128)(2,1)S(1)}, bf16[512,768]{1,0:T(8,128)(2,1)S(1)}, u32[]{:S(2)}, u32[]{:S(2)}) collective-permute-start(bf16[512,768]{1,0:T(8,128)(2,1)S(1)} %get-tuple-element.247.refs_2_), channel_id=1, source_target_pairs={{0,2},{1,3},{2,0},{3,1},{4,6},{5,7},{6,4},{7,5},{8,10},{9,11},{10,... | collective-permute-start | bytes 2359304 | tf_op jit(solution)/shard_map/ppermute | solution.py:654
  173.7 12.2 %collective-permute-start.39 = (bf16[192,768]{1,0:T(8,128)(2,1)S(1)}, bf16[192,768]{1,0:T(8,128)(2,1)S(1)}, u32[]{:S(2)}, u32[]{:S(2)}) collective-permute-start(bf16[192,768]{1,0:T(8,128)(2,1)S(1)} %get-tuple-element.288), channel_id=1, source_target_pairs={{0,8},{4,12},{8,0},{12,4},{16,24},{20,28},{24,16},{28,20},{1,9},{5... | collective-permute-start | bytes 884744 | tf_op jit(solution)/shard_map/ppermute | solution.py:654
  176.4 15.6 %collective-permute-start.36 = (bf16[384,384]{1,0:T(8,128)(2,1)S(1)}, bf16[384,384]{1,0:T(8,128)(2,1)S(1)}, u32[]{:S(2)}, u32[]{:S(2)}) collective-permute-start(bf16[384,384]{1,0:T(8,128)(2,1)S(1)} %get-tuple-element.283), channel_id=1, source_target_pairs={{0,4},{4,0},{8,12},{12,8},{16,20},{20,16},{24,28},{28,24},{1,5},{5... | collective-permute-start | bytes 884744 | tf_op jit(solution)/shard_map/ppermute | solution.py:654
  177.0 10.3 %collective-permute-start.38 = (bf16[96,768]{1,0:T(8,128)(2,1)S(1)}, bf16[96,768]{1,0:T(8,128)(2,1)S(1)}, u32[]{:S(2)}, u32[]{:S(2)}) collective-permute-start(bf16[96,768]{1,0:T(8,128)(2,1)S(1)} %get-tuple-element.286), channel_id=1, source_target_pairs={{0,16},{4,20},{8,24},{12,28},{16,0},{20,4},{24,8},{28,12},{1,17},{... | collective-permute-start | bytes 442376 | tf_op jit(solution)/shard_map/ppermute | solution.py:654
  185.8 18.2 %collective-permute-start.35 = (bf16[256,768]{1,0:T(8,128)(2,1)S(1)}, bf16[256,768]{1,0:T(8,128)(2,1)S(1)}, u32[]{:S(2)}, u32[]{:S(2)}) collective-permute-start(bf16[256,768]{1,0:T(8,128)(2,1)S(1)} %get-tuple-element.281.refs_5_), channel_id=1, source_target_pairs={{0,2},{1,3},{2,0},{3,1},{4,6},{5,7},{6,4},{7,5},{8,10},{9,11},{10,... | collective-permute-start | bytes 1179656 | tf_op jit(solution)/shard_map/ppermute | solution.py:654
  188.0 11.2 %collective-permute-start.41 = (bf16[192,640]{1,0:T(8,128)(2,1)S(1)}, bf16[192,640]{1,0:T(8,128)(2,1)S(1)}, u32[]{:S(2)}, u32[]{:S(2)}) collective-permute-start(bf16[192,640]{1,0:T(8,128)(2,1)S(1)} %get-tuple-element.295), channel_id=1, source_target_pairs={{0,8},{4,12},{8,0},{12,4},{16,24},{20,28},{24,16},{28,20},{1,9},{5... | collective-permute-start | bytes 737288 | tf_op jit(solution)/shard_map/ppermute | solution.py:654
  188.1 9.3 %collective-permute-start.42 = (bf16[96,768]{1,0:T(8,128)(2,1)S(1)}, bf16[96,768]{1,0:T(8,128)(2,1)S(1)}, u32[]{:S(2)}, u32[]{:S(2)}) collective-permute-start(bf16[96,768]{1,0:T(8,128)(2,1)S(1)} %get-tuple-element.296), channel_id=1, source_target_pairs={{0,16},{4,20},{8,24},{12,28},{16,0},{20,4},{24,8},{28,12},{1,17},{... | collective-permute-start | bytes 442376 | tf_op jit(solution)/shard_map/ppermute | solution.py:654
  192.7 8.9 %collective-permute-start.40 = (bf16[192,384]{1,0:T(8,128)(2,1)S(1)}, bf16[192,384]{1,0:T(8,128)(2,1)S(1)}, u32[]{:S(2)}, u32[]{:S(2)}) collective-permute-start(bf16[192,384]{1,0:T(8,128)(2,1)S(1)} %get-tuple-element.293), channel_id=1, source_target_pairs={{0,8},{4,12},{8,0},{12,4},{16,24},{20,28},{24,16},{28,20},{1,9},{5... | collective-permute-start | bytes 442376 | tf_op jit(solution)/shard_map/ppermute | solution.py:654
  199.8 9.8 %collective-permute-start.45 = (bf16[96,640]{1,0:T(8,128)(2,1)S(1)}, bf16[96,640]{1,0:T(8,128)(2,1)S(1)}, u32[]{:S(2)}, u32[]{:S(2)}) collective-permute-start(bf16[96,640]{1,0:T(8,128)(2,1)S(1)} %get-tuple-element.305), channel_id=1, source_target_pairs={{0,16},{4,20},{8,24},{12,28},{16,0},{20,4},{24,8},{28,12},{1,17},{... | collective-permute-start | bytes 368648 | tf_op jit(solution)/shard_map/ppermute | solution.py:654
  202.2 7.4 %collective-permute-start.46 = (bf16[96,384]{1,0:T(8,128)(2,1)S(1)}, bf16[96,384]{1,0:T(8,128)(2,1)S(1)}, u32[]{:S(2)}, u32[]{:S(2)}) collective-permute-start(bf16[96,384]{1,0:T(8,128)(2,1)S(1)} %get-tuple-element.307), channel_id=1, source_target_pairs={{0,16},{4,20},{8,24},{12,28},{16,0},{20,4},{24,8},{28,12},{1,17},{... | collective-permute-start | bytes 221192 | tf_op jit(solution)/shard_map/ppermute | solution.py:654
  204.0 7.7 %collective-permute-start.44 = (bf16[768,768]{1,0:T(8,128)(2,1)S(1)}, bf16[768,768]{1,0:T(8,128)(2,1)S(1)}, u32[]{:S(2)}, u32[]{:S(2)}) collective-permute-start(bf16[768,768]{1,0:T(8,128)(2,1)S(1)} %get-tuple-element.303.refs_3_), channel_id=1, source_target_pairs={{0,1},{1,0},{2,3},{3,2},{4,5},{5,4},{6,7},{7,6},{8,9},{9,8},{10,11... | collective-permute-start | bytes 3538952 | tf_op jit(solution)/shard_map/ppermute | solution.py:654
  205.1 6.6 %collective-permute-start.43 = (f32[768,768]{1,0:T(8,128)S(1)}, f32[768,768]{1,0:T(8,128)S(1)}, u32[]{:S(2)}, u32[]{:S(2)}) collective-permute-start(f32[768,768]{1,0:T(8,128)S(1)} %get-tuple-element.302.refs_1_), channel_id=1, source_target_pairs={{0,1},{1,0},{2,3},{3,2},{4,5},{5,4},{6,7},{7,6},{8,9},{9,8},{10,11... | collective-permute-start | bytes 7077896 | tf_op jit(solution)/shard_map/ppermute | solution.py:654
  (22 other events, 121.1 us)
